TPU v7x, 32 devices: a whole 2x2x4 slice. The times are simulated.
32 devices in a mesh: row: 16 (over z, x, core), col: 2 (over y).
Axes of the slice: x: 2, y: 2, z: 4, core: 2. Of those that a mesh axis runs over, the one named last changes fastest.
Arguments:
- pair_rep: bfloat16 [256, 256, 128], P('row', 'col'), may hold values from -6 to 6
- chain_len: int32 [4], replicated, may hold values from 1 to 64, as said below
- tri_gain: float32 [128], replicated, may hold values from 0.5 to 2
- tri_in: bfloat16 [128, 640], replicated, may hold values from -0.5 to 0.5
- sum_gain: float32 [128], replicated, may hold values from 0.5 to 2
- tri_out: bfloat16 [128, 128], replicated, may hold values from -0.5 to 0.5
- att_gain: float32 [128], replicated, may hold values from 0.5 to 8
- att_in: bfloat16 [128, 512], replicated, may hold values from -0.5 to 0.5
- att_bias: bfloat16 [128, 4], replicated, may hold values from -2 to 2
- att_out: bfloat16 [128, 128], replicated, may hold values from -4 to 4
Outputs:
- new_pair: bfloat16 [256, 256, 128], P('row', 'col')
Inputs may be any that keep to these rules, and one draw needn't show every extreme that they name: `chain_len`: one chain in every draw has all 64 slots live.
All inputs are finite; a program needn't handle non-finite values.
Results may differ from a plain program's by a relative error of at most 0.039.
The roundings to bfloat16 on the way count: a program that leaves them out, or rounds other values in their place, can miss the bound.
Values may be sent and summed in bfloat16 or wider, within the bound.
No kernel may reach another device: no remote copies, remote signals or barrier semaphores. Data moves between devices by JAX's collectives and lax.ppermute only.
A program may use at most 128 MiB of HBM per device.

v0:
```python
import functools
import math

import jax
import jax.numpy as jnp
from jax import lax
from jax.experimental import pallas as pl
from jax.experimental.pallas import tpu as pltpu
from jax.sharding import PartitionSpec as P


CH = 128
H = 4
DH = 32
KCD = 16
SLOT = 64

EPSILON = 1e-05
NEG_SCORE = -1e30
VMEM_LIMIT = 60 * 1024 * 1024

F32 = jnp.float32
BF16 = jnp.bfloat16


def layer_norm(values, norm_gain):
    centre = values - jnp.mean(values, axis=-1, keepdims=True)
    spread = jnp.mean(centre * centre, axis=-1, keepdims=True)
    return centre * lax.rsqrt(spread + EPSILON) * norm_gain


def sigmoid(values):
    return jax.nn.sigmoid(values)


def dot(a, b):
    return jnp.dot(a, b, preferred_element_type=F32)


def dot_nt(a, b):
    return lax.dot_general(a, b, (((1,), (1,)), ((), ())), preferred_element_type=F32)


def call(kernel, out_shape, n_smem, n_in, scratch=()):
    smem = pl.BlockSpec(memory_space=pltpu.SMEM)
    vmem = pl.BlockSpec(memory_space=pltpu.VMEM)
    outs = jax.tree.map(lambda _: vmem, out_shape)
    return pl.pallas_call(
        kernel,
        out_shape=out_shape,
        in_specs=[smem] * n_smem + [vmem] * n_in,
        out_specs=outs,
        scratch_shapes=list(scratch),
        compiler_params=pltpu.CompilerParams(vmem_limit_bytes=VMEM_LIMIT),
    )


def edge_kernel(len_ref, pair_ref, gain_ref, w_ref, left_ref, right_ref, scratch_ref, *, cols):
    rows, kcd, width = pair_ref.shape
    row_start = lax.axis_index("row") * rows
    col_start = lax.axis_index("col") * cols
    cells = rows * kcd
    normed = layer_norm(pair_ref[...].reshape(cells, width).astype(F32), gain_ref[...])
    proj = dot(normed.astype(BF16), w_ref[...])
    row_len = len_ref[row_start // SLOT]
    row_base = row_start % SLOT
    col_len = len_ref[col_start // SLOT]
    cell = lax.broadcasted_iota(jnp.int32, (cells, width), 0)
    row_live = (cell // kcd + row_base) < row_len
    live = jnp.where(row_live & (cell % kcd < col_len), 1.0, 0.0).astype(F32)
    right = sigmoid(proj[:, 2 * CH : 3 * CH]) * proj[:, 3 * CH : 4 * CH] * live
    scratch_ref[...] = right
    for k in range(kcd):
        right_ref[k] = scratch_ref[pl.ds(k, rows, stride=kcd), :].astype(BF16)
    left = sigmoid(proj[:, :CH]) * proj[:, CH : 2 * CH] * live
    left_ref[...] = left.astype(BF16).reshape(rows, kcd, width)


def gate_kernel(pair_ref, gain_ref, w_ref, out_ref):
    rows, cols, width = pair_ref.shape
    step = 2

    def body(t, carry):
        at = pl.ds(t * step, step)
        x = pair_ref[at].reshape(step * cols, width).astype(F32)
        normed = layer_norm(x, gain_ref[...]).astype(BF16)
        out_ref[at] = sigmoid(dot(normed, w_ref[:, 4 * CH :])).reshape(step, cols, width)
        return carry

    lax.fori_loop(0, rows // step, body, 0, unroll=2)


def make_tri_kernel(n_col, n_blk, place):
    def kernel(*refs):
        lefts = refs[:n_col]
        rights = refs[n_col : n_col + n_blk]
        (pair_ref, gate_ref, sum_gain_ref, w_ref, att_gain_ref, bias_w_ref) = refs[
            n_col + n_blk : n_col + n_blk + 6
        ]
        mid_ref, norm_ref, bias_ref, left_ref, sum_ref, bias_scr = refs[n_col + n_blk + 6 :]
        rows, cols, width = pair_ref.shape
        kcd = lefts[0].shape[1]
        blk = rights[0].shape[2]
        for d in range(n_col):
            left_ref[d] = lefts[d][...].reshape(rows * kcd, width).astype(F32)
        group = 8
        for s in range(n_blk):
            first = pl.multiple_of(place(s) * blk, blk)

            def sums(g, carry, s=s, first=first):
                acc = [jnp.zeros((blk, width), F32) for _ in range(group)]
                for d in range(n_col):
                    for k in range(kcd):
                        right = rights[s][d, k].astype(F32)
                        for u in range(group):
                            left = left_ref[d, pl.ds((g * group + u) * kcd + k, 1), :]
                            acc[u] = acc[u] + left * right
                for u in range(group):
                    sum_ref[g * group + u, pl.ds(first, blk), :] = acc[u]
                return carry

            lax.fori_loop(0, rows // group, sums, 0)
        step = 2

        def finish(t, carry):
            at = pl.ds(t * step, step)
            total = sum_ref[at].reshape(step * cols, width)
            normed = layer_norm(total, sum_gain_ref[...]).astype(BF16)
            update = dot(normed, w_ref[...])
            pair = pair_ref[at].reshape(step * cols, width).astype(F32)
            gate = gate_ref[at].reshape(step * cols, width)
            mid = (pair + gate * update).astype(BF16)
            mid_ref[at] = mid.reshape(step, cols, width)
            att = layer_norm(mid.astype(F32), att_gain_ref[...]).astype(BF16)
            norm_ref[at] = att.reshape(step, cols, width)
            bias = lax.dot_general(
                bias_w_ref[...], att, (((0,), (1,)), ((), ())), preferred_element_type=F32
            )
            for u in range(step):
                bias_scr[t * step + u] = bias[:, u * cols : (u + 1) * cols]
            return carry

        lax.fori_loop(0, rows // step, finish, 0, unroll=2)
        for h in range(H):
            bias_ref[h] = bias_scr[:, h, :].astype(BF16)

    return kernel


def project_kernel(norm_ref, w_ref, q_ref, k_ref, v_ref, gate_ref):
    rows, cols, width = norm_ref.shape
    step = 2

    def body(t, carry):
        at = pl.ds(t * step, step)
        out = dot(norm_ref[at].reshape(step * cols, width), w_ref[...])
        shape = (step, cols, width)
        q_ref[at] = out[:, :width].astype(BF16).reshape(shape)
        k_ref[at] = out[:, width : 2 * width].astype(BF16).reshape(shape)
        v_ref[at] = out[:, 2 * width : 3 * width].astype(BF16).reshape(shape)
        gate_ref[at] = sigmoid(out[:, 3 * width :]).reshape(shape)
        return carry

    lax.fori_loop(0, rows // step, body, 0)


def make_attend_kernel(n_col, n_blk, place, col_of):
    def kernel(*refs):
        len_ref = refs[0]
        biases = refs[1 : 1 + n_blk]
        others = refs[1 + n_blk : n_blk + n_col]
        q_ref, k_ref, v_ref, gate_ref, mid_ref, gain_ref, kv_w_ref, out_w_ref = refs[
            n_blk + n_col : n_blk + n_col + 8
        ]
        out_ref, bias_ref, keys_ref, values_ref = refs[n_blk + n_col + 8 :]
        rows, cols, width = q_ref.shape
        blk = biases[0].shape[2]
        chains = cols // SLOT
        lane = lax.broadcasted_iota(jnp.int32, (blk, cols), 1)
        for d in range(n_col):
            first_chain = col_of(d) * chains
            limit = jnp.zeros((blk, cols), jnp.int32)
            for q in range(chains):
                inside = lane // SLOT == q
                limit = jnp.where(inside, q * SLOT + len_ref[first_chain + q], limit)
            live = lane < limit
            for s in range(n_blk):
                first = place(s) * blk
                for h in range(H):
                    at = pl.multiple_of(h * cols + first, blk)
                    value = biases[s][d, h].astype(F32)
                    bias_ref[pl.ds(at, blk), d * cols : (d + 1) * cols] = jnp.where(
                        live, value, NEG_SCORE
                    )
        head = lax.broadcasted_iota(jnp.int32, (cols, width), 1) // DH
        khead = lax.broadcasted_iota(jnp.int32, (n_col * cols, width), 1) // DH
        scale = 1.0 / math.sqrt(DH)
        ones = jnp.ones((n_col * cols, width), BF16)

        step = 2

        def spread(t, carry):
            at = pl.ds(t * step, step)
            keys_ref[at, 0:cols] = k_ref[at]
            values_ref[at, 0:cols] = v_ref[at]
            for d in range(n_col - 1):
                there = others[d][at].reshape(step * cols, width).astype(F32)
                normed = layer_norm(there, gain_ref[...]).astype(BF16)
                kv = dot(normed, kv_w_ref[:, width : 3 * width]).astype(BF16)
                low = (d + 1) * cols
                keys_ref[at, low : low + cols] = kv[:, :width].reshape(step, cols, width)
                values_ref[at, low : low + cols] = kv[:, width:].reshape(step, cols, width)
            return carry

        lax.fori_loop(0, rows // step, spread, 0, unroll=2)

        def attend(i, carry):
            key = keys_ref[i]
            value = jnp.concatenate([values_ref[i], ones], axis=1)
            query = q_ref[i]
            stack = jnp.concatenate(
                [jnp.where(head == h, query, jnp.zeros_like(query)) for h in range(H)], axis=0
            )
            scores = dot_nt(stack, key) * scale + bias_ref[...]
            top = jnp.max(scores, axis=-1, keepdims=True)
            weights = jnp.exp(scores - top).astype(BF16)
            both = dot(weights, value)
            summed = both[:cols, :width]
            totals = both[:cols, width:]
            for h in range(1, H):
                mine = head == h
                part = both[h * cols : (h + 1) * cols]
                summed = jnp.where(mine, part[:, :width], summed)
                totals = jnp.where(mine, part[:, width:], totals)
            attended = (summed / totals * gate_ref[i]).astype(BF16)
            new = mid_ref[i].astype(F32) + dot(attended, out_w_ref[...])
            out_ref[i] = new.astype(BF16)
            return carry

        lax.fori_loop(0, rows, attend, 0, unroll=4)

    return kernel


class Grid:
    def __init__(self, n_row, n_col):
        self.n_row = n_row
        self.n_col = n_col
        self.n_blk = n_row // n_col
        self.fast = n_col == 2 and n_row & (n_row - 1) == 0
        self.offsets = [0]
        if self.fast:
            bit = self.n_blk // 2
            while bit:
                self.offsets = self.offsets + [o ^ bit for o in self.offsets]
                bit //= 2

    def place(self, s):
        if self.fast:
            return (lax.axis_index("row") & (self.n_blk - 1)) ^ self.offsets[s]
        return s

    def col_of(self, d):
        return (lax.axis_index("col") + d) % self.n_col

    def move(self, value, target):
        pairs = []
        for r in range(self.n_row):
            for c in range(self.n_col):
                to = target(r, c)
                if to is not None:
                    pairs.append((r * self.n_col + c, to[0] * self.n_col + to[1]))
        return lax.ppermute(value, ("row", "col"), pairs)

    def shift_col(self, value, d):
        return self.move(value, lambda r, c: (r, (c - d) % self.n_col))

    def flip_row(self, value, bit):
        return self.move(value, lambda r, c: (r ^ bit, c))

    def gather(self, own):
        if not self.fast:
            stacked = lax.all_gather(own, "row", axis=0)
            stacked = lax.all_to_all(stacked, "col", split_axis=0, concat_axis=0, tiled=True)
            stacked = stacked.reshape((self.n_col, self.n_blk) + own.shape)
            order = (lax.axis_index("col") + jnp.arange(self.n_col)) % self.n_col
            stacked = jnp.take(stacked, order, axis=0)
            return [stacked[:, s] for s in range(self.n_blk)]
        half = self.n_row // 2
        same = lax.axis_index("row") // half == lax.axis_index("col")

        def first(r, c):
            return (r ^ half, c) if r // half == c else (r, 1 - c)

        def second(r, c):
            return None if r // half == c else (r ^ half, 1 - c)

        near = self.move(own, first)
        far = self.move(own, second)
        pair = jnp.where(same, jnp.stack([own, near]), jnp.stack([near, far]))
        blocks = [pair]
        bit = self.n_blk // 2
        while bit:
            moved = []
            for block in blocks:
                moved.append(self.flip_row(block, bit))
            blocks = blocks + moved
            bit //= 2
        return blocks


def make_body(grid):
    def body(
        pair_rep, chain_len, tri_gain, tri_in, sum_gain, tri_out, att_gain, att_in, att_bias, att_out
    ):
        rows, cols, width = pair_rep.shape
        n_col, n_blk = grid.n_col, grid.n_blk
        whole = (rows, cols, width)
        tri_gain = tri_gain.reshape(1, width)
        sum_gain = sum_gain.reshape(1, width)
        att_gain = att_gain.reshape(1, width)

        left, right = pl.pallas_call(
            functools.partial(edge_kernel, cols=cols),
            name="edges",
            grid=(1,),
            out_shape=(
                jax.ShapeDtypeStruct((rows, KCD, width), BF16),
                jax.ShapeDtypeStruct((KCD, rows, width), BF16),
            ),
            in_specs=[
                pl.BlockSpec(memory_space=pltpu.SMEM),
                pl.BlockSpec((rows, KCD, width), lambda g: (0, 0, 0)),
                pl.BlockSpec((1, width), lambda g: (0, 0)),
                pl.BlockSpec((width, 4 * CH), lambda g: (0, 0)),
            ],
            out_specs=(
                pl.BlockSpec((rows, KCD, width), lambda g: (0, 0, 0)),
                pl.BlockSpec((KCD, rows, width), lambda g: (0, 0, 0)),
            ),
            scratch_shapes=[pltpu.VMEM((rows * KCD, width), F32)],
        )(chain_len, pair_rep, tri_gain, tri_in)
        rights = grid.gather(right)
        lefts = [left] + [grid.shift_col(left, d) for d in range(1, n_col)]
        gate = call(gate_kernel, jax.ShapeDtypeStruct(whole, F32), 0, 3)(pair_rep, tri_gain, tri_in)
        mid, normed, bias = call(
            make_tri_kernel(n_col, n_blk, grid.place),
            (
                jax.ShapeDtypeStruct(whole, BF16),
                jax.ShapeDtypeStruct(whole, BF16),
                jax.ShapeDtypeStruct((H, rows, cols), BF16),
            ),
            0,
            n_col + n_blk + 6,
            [
                pltpu.VMEM((n_col, rows * KCD, width), F32),
                pltpu.VMEM(whole, F32),
                pltpu.VMEM((rows, H, cols), F32),
            ],
        )(*lefts, *rights, pair_rep, gate, sum_gain, tri_out, att_gain, att_bias)
        biases = grid.gather(bias)
        others = [grid.shift_col(mid, d) for d in range(1, n_col)]
        wide = jax.ShapeDtypeStruct(whole, BF16)
        query, key, value, att_gate = call(
            project_kernel, (wide, wide, wide, jax.ShapeDtypeStruct(whole, F32)), 0, 2
        )(normed, att_in)
        return call(
            make_attend_kernel(n_col, n_blk, grid.place, grid.col_of),
            wide,
            1,
            n_blk + n_col - 1 + 8,
            [
                pltpu.VMEM((H * cols, n_col * cols), F32),
                pltpu.VMEM((rows, n_col * cols, width), BF16),
                pltpu.VMEM((rows, n_col * cols, width), BF16),
            ],
        )(chain_len, *biases, *others, query, key, value, att_gate, mid, att_gain, att_in, att_out)

    return body


def solution(mesh):
    grid = Grid(mesh.shape["row"], mesh.shape["col"])
    placed = (P("row", "col", None), P(), P(), P(), P(), P(), P(), P(), P(), P())
    return jax.shard_map(
        make_body(grid), mesh=mesh, in_specs=placed, out_specs=P("row", "col", None), check_vma=False
    )
```

profile of v0, /device:TPU:0, one launch (start us, length us, event | category | flops | bytes accessed | tf_op | source)
XLA Modules:
  0.0 77.9 jit_solution(18225025020671586912)
XLA Ops:
  0.0 2.0 %edges.1 = (bf16[16,16,128]{2,1,0:T(8,128)(2,1)}, bf16[16,16,128]{2,1,0:T(8,128)(2,1)}) custom-call(s32[4]{0:T(128)} %refs_0_.1, bf16[16,128,128]{2,1,0:T(8,128)(2,1)} %refs_10_.1, f32[1,128]{1,0:T(1,128)} %bitcast.15, bf16[128,640]{1,0:T(8,128)(2,1)} %w_ref.4), custom_call_target="tpu_custom_call" | custom-call | tf_op jit(solution)/shard_map/edges/pallas_call | solution.py:323
  2.0 4.1 %collective-permute-start.1 = (bf16[16,16,128]{2,1,0:T(8,128)(2,1)}, bf16[16,16,128]{2,1,0:T(8,128)(2,1)S(1)}, u32[]{:S(2)}, u32[]{:S(2)}) collective-permute-start(bf16[16,16,128]{2,1,0:T(8,128)(2,1)} %get-tuple-element.15), channel_id=1, source_target_pairs={{0,16},{1,0},{2,18},{3,2},{4,20},{5,4},{6,22},{7,6},{8,24},{9,8},{... | collective-permute-start | bytes 196616 | tf_op jit(solution)/shard_map/ppermute | solution.py:273
  6.1 0.7 collective-permute-start.2
  6.8 1.5 %collective-permute-done.1 = bf16[16,16,128]{2,1,0:T(8,128)(2,1)S(1)} collective-permute-done((bf16[16,16,128]{2,1,0:T(8,128)(2,1)}, bf16[16,16,128]{2,1,0:T(8,128)(2,1)S(1)}, u32[]{:S(2)}, u32[]{:S(2)}) %collective-permute-start.1) | collective-permute-done | bytes 65568 | tf_op jit(solution)/shard_map/ppermute | solution.py:273
  8.3 0.0 collective-permute-done.2
  8.3 0.9 %maximum_select_fusion.refs_2_ = bf16[2,16,16,128]{3,2,1,0:T(8,128)(2,1)S(1)} fusion(bf16[1,16,16,128]{3,2,1,0:T(8,128)(2,1)S(1)} %bitcast.10, bf16[1,16,16,128]{3,2,1,0:T(8,128)(2,1)} %bitcast.9, bf16[1,16,16,128]{3,2,1,0:T(8,128)(2,1)S(1)} %bitcast.11, pred[]{:T(512)S(6)} %eq.4), kind=kLoop, calls=%fused_computation | loop fusion | flops 196608 | bytes 327681 | tf_op jit(solution)/shard_map/jit(_where)/select_n | solution.py:300
  9.2 2.4 %collective-permute-start.3 = (bf16[2,16,16,128]{3,2,1,0:T(8,128)(2,1)S(1)}, bf16[2,16,16,128]{3,2,1,0:T(8,128)(2,1)S(1)}, u32[]{:S(2)}, u32[]{:S(2)}) collective-permute-start(bf16[2,16,16,128]{3,2,1,0:T(8,128)(2,1)S(1)} %maximum_select_fusion.refs_2_), channel_id=1, source_target_pairs={{0,8},{1,9},{2,10},{3,11},{4,12},{5,13},{6,14},{7,15},{8,0},{9,1},... | collective-permute-start | bytes 393224 | tf_op jit(solution)/shard_map/ppermute | solution.py:273
  11.6 1.5 %collective-permute-start.4 = (bf16[2,16,16,128]{3,2,1,0:T(8,128)(2,1)S(1)}, bf16[2,16,16,128]{3,2,1,0:T(8,128)(2,1)S(1)}, u32[]{:S(2)}, u32[]{:S(2)}) collective-permute-start(bf16[2,16,16,128]{3,2,1,0:T(8,128)(2,1)S(1)} %maximum_select_fusion.refs_2_), channel_id=1, source_target_pairs={{0,4},{1,5},{2,6},{3,7},{4,0},{5,1},{6,2},{7,3},{8,12},{9,13},{10,... | collective-permute-start | bytes 393224 | tf_op jit(solution)/shard_map/ppermute | solution.py:273
  13.1 2.3 %collective-permute-done.3.refs_3_ = bf16[2,16,16,128]{3,2,1,0:T(8,128)(2,1)S(1)} collective-permute-done((bf16[2,16,16,128]{3,2,1,0:T(8,128)(2,1)S(1)}, bf16[2,16,16,128]{3,2,1,0:T(8,128)(2,1)S(1)}, u32[]{:S(2)}, u32[]{:S(2)}) %collective-permute-start.3) | collective-permute-done | bytes 131104 | tf_op jit(solution)/shard_map/ppermute | solution.py:273
  15.4 1.5 %collective-permute-start.5 = (bf16[2,16,16,128]{3,2,1,0:T(8,128)(2,1)S(1)}, bf16[2,16,16,128]{3,2,1,0:T(8,128)(2,1)S(1)}, u32[]{:S(2)}, u32[]{:S(2)}) collective-permute-start(bf16[2,16,16,128]{3,2,1,0:T(8,128)(2,1)S(1)} %collective-permute-done.3.refs_3_), channel_id=1, source_target_pairs={{0,4},{1,5},{2,6},{3,7},{4,0},{5,1},{6,2},{7,3},{8,12},{9,13},{10,... | collective-permute-start | bytes 393224 | tf_op jit(solution)/shard_map/ppermute | solution.py:273
  16.9 0.0 collective-permute-start.6
  16.9 0.5 collective-permute-start.7
  17.4 0.0 collective-permute-done.4.refs_4_
  17.4 0.1 collective-permute-start.8
  17.4 2.9 %collective-permute-done.5.refs_5_ = bf16[2,16,16,128]{3,2,1,0:T(8,128)(2,1)S(1)} collective-permute-done((bf16[2,16,16,128]{3,2,1,0:T(8,128)(2,1)S(1)}, bf16[2,16,16,128]{3,2,1,0:T(8,128)(2,1)S(1)}, u32[]{:S(2)}, u32[]{:S(2)}) %collective-permute-start.5) | collective-permute-done | bytes 131104 | tf_op jit(solution)/shard_map/ppermute | solution.py:273
  20.3 0.0 copy-start.19
  20.4 4.7 %collective-permute-start = (bf16[16,16,128]{2,1,0:T(8,128)(2,1)S(1)}, bf16[16,16,128]{2,1,0:T(8,128)(2,1)S(1)}, u32[]{:S(2)}, u32[]{:S(2)}) collective-permute-start(bf16[16,16,128]{2,1,0:T(8,128)(2,1)S(1)} %copy-done.10), channel_id=1, source_target_pairs={{0,1},{1,0},{2,3},{3,2},{4,5},{5,4},{6,7},{7,6},{8,9},{9,8},{10,11... | collective-permute-start | bytes 196616 | tf_op jit(solution)/shard_map/ppermute | solution.py:273
  25.1 3.5 %shard_map.100.refs_11_ = f32[16,128,128]{2,1,0:T(8,128)} custom-call(bf16[16,128,128]{2,1,0:T(8,128)(2,1)} %refs_10_.1, f32[1,128]{1,0:T(1,128)} %bitcast.16, bf16[128,640]{1,0:T(8,128)(2,1)} %w_ref.4), custom_call_target="tpu_custom_call" | custom-call | tf_op jit(solution)/shard_map/pallas_call | solution.py:345
  28.6 0.7 copy.11.refs_15_
  29.4 0.0 collective-permute-done.7.refs_7_
  29.4 0.5 copy-done.11
  30.0 0.1 copy-done.6
  30.0 0.1 copy-done.7
  30.1 0.0 copy-done.8
  30.2 0.0 copy-done.9
  30.2 8.1 %shard_map.101 = (bf16[16,128,128]{2,1,0:T(8,128)(2,1)}, bf16[16,128,128]{2,1,0:T(8,128)(2,1)}, bf16[4,16,128]{2,1,0:T(8,128)(2,1)}) custom-call(bf16[16,16,128]{2,1,0:T(8,128)(2,1)} %get-tuple-element.14.refs_0_, bf16[16,16,128]{2,1,0:T(8,128)(2,1)} %copy-done.11, bf16[2,16,16,128]{3,2,1,0:T(8,128)(2,1)} %copy-done.1, bf16[2,16,16,128]{3,2,1,0:T(8,128)(2,1)} %copy-done.3, ...), custom_call_target="tpu_custom_call" | custom-call | tf_op jit(solution)/shard_map/pallas_call | solution.py:346
  38.3 0.1 collective-permute-start.19
  38.4 3.8 %collective-permute-start.10 = (bf16[4,16,128]{2,1,0:T(8,128)(2,1)}, bf16[4,16,128]{2,1,0:T(8,128)(2,1)S(1)}, u32[]{:S(2)}, u32[]{:S(2)}) collective-permute-start(bf16[4,16,128]{2,1,0:T(8,128)(2,1)} %get-tuple-element.16), channel_id=1, source_target_pairs={{0,16},{1,0},{2,18},{3,2},{4,20},{5,4},{6,22},{7,6},{8,24},{9,8},{... | collective-permute-start | bytes 49160 | tf_op jit(solution)/shard_map/ppermute | solution.py:273
  42.2 0.7 collective-permute-start.11
  42.8 10.0 %collective-permute-done.10 = bf16[4,16,128]{2,1,0:T(8,128)(2,1)S(1)} collective-permute-done((bf16[4,16,128]{2,1,0:T(8,128)(2,1)}, bf16[4,16,128]{2,1,0:T(8,128)(2,1)S(1)}, u32[]{:S(2)}, u32[]{:S(2)}) %collective-permute-start.10) | collective-permute-done | bytes 16416 | tf_op jit(solution)/shard_map/ppermute | solution.py:273
  52.8 0.7 maximum_select_fusion.1.refs_1_
  53.5 1.2 %collective-permute-start.12 = (bf16[2,4,16,128]{3,2,1,0:T(8,128)(2,1)S(1)}, bf16[2,4,16,128]{3,2,1,0:T(8,128)(2,1)S(1)}, u32[]{:S(2)}, u32[]{:S(2)}) collective-permute-start(bf16[2,4,16,128]{3,2,1,0:T(8,128)(2,1)S(1)} %maximum_select_fusion.1.refs_1_), channel_id=1, source_target_pairs={{0,8},{1,9},{2,10},{3,11},{4,12},{5,13},{6,14},{7,15},{8,0},{9,1},... | collective-permute-start | bytes 98312 | tf_op jit(solution)/shard_map/ppermute | solution.py:273
  54.7 1.5 %collective-permute-start.13 = (bf16[2,4,16,128]{3,2,1,0:T(8,128)(2,1)S(1)}, bf16[2,4,16,128]{3,2,1,0:T(8,128)(2,1)S(1)}, u32[]{:S(2)}, u32[]{:S(2)}) collective-permute-start(bf16[2,4,16,128]{3,2,1,0:T(8,128)(2,1)S(1)} %maximum_select_fusion.1.refs_1_), channel_id=1, source_target_pairs={{0,4},{1,5},{2,6},{3,7},{4,0},{5,1},{6,2},{7,3},{8,12},{9,13},{10,... | collective-permute-start | bytes 98312 | tf_op jit(solution)/shard_map/ppermute | solution.py:273
  56.2 1.2 %collective-permute-done.12.refs_2_ = bf16[2,4,16,128]{3,2,1,0:T(8,128)(2,1)S(1)} collective-permute-done((bf16[2,4,16,128]{3,2,1,0:T(8,128)(2,1)S(1)}, bf16[2,4,16,128]{3,2,1,0:T(8,128)(2,1)S(1)}, u32[]{:S(2)}, u32[]{:S(2)}) %collective-permute-start.12) | collective-permute-done | bytes 32800 | tf_op jit(solution)/shard_map/ppermute | solution.py:273
  57.5 1.5 %collective-permute-start.14 = (bf16[2,4,16,128]{3,2,1,0:T(8,128)(2,1)S(1)}, bf16[2,4,16,128]{3,2,1,0:T(8,128)(2,1)S(1)}, u32[]{:S(2)}, u32[]{:S(2)}) collective-permute-start(bf16[2,4,16,128]{3,2,1,0:T(8,128)(2,1)S(1)} %collective-permute-done.12.refs_2_), channel_id=1, source_target_pairs={{0,4},{1,5},{2,6},{3,7},{4,0},{5,1},{6,2},{7,3},{8,12},{9,13},{10,... | collective-permute-start | bytes 98312 | tf_op jit(solution)/shard_map/ppermute | solution.py:273
  58.9 0.0 collective-permute-start.15
  58.9 0.5 collective-permute-start.16
  59.5 0.0 collective-permute-done.13.refs_3_
  59.5 0.1 collective-permute-start.17
  59.5 1.8 %collective-permute-done.14.refs_4_ = bf16[2,4,16,128]{3,2,1,0:T(8,128)(2,1)S(1)} collective-permute-done((bf16[2,4,16,128]{3,2,1,0:T(8,128)(2,1)S(1)}, bf16[2,4,16,128]{3,2,1,0:T(8,128)(2,1)S(1)}, u32[]{:S(2)}, u32[]{:S(2)}) %collective-permute-start.14) | collective-permute-done | bytes 32800 | tf_op jit(solution)/shard_map/ppermute | solution.py:273
  61.4 0.0 collective-permute-start.18
  61.4 4.3 %shard_map.102 = (bf16[16,128,128]{2,1,0:T(8,128)(2,1)}, bf16[16,128,128]{2,1,0:T(8,128)(2,1)}, bf16[16,128,128]{2,1,0:T(8,128)(2,1)}, f32[16,128,128]{2,1,0:T(8,128)}) custom-call(bf16[16,128,128]{2,1,0:T(8,128)(2,1)} %get-tuple-element.18.norm_ref, bf16[128,512]{1,0:T(8,128)(2,1)} %refs_16_.1), custom_call_target="tpu_custom_call" | custom-call | tf_op jit(solution)/shard_map/pallas_call | solution.py:364
  65.8 0.5 copy-done.15
  66.3 0.0 copy-done.16
  66.3 0.0 copy-done.17
  66.4 0.0 copy-done.18
  66.4 0.2 copy-done
  66.6 11.3 %shard_map.103 = bf16[16,128,128]{2,1,0:T(8,128)(2,1)} custom-call(s32[4]{0:T(128)} %refs_0_.1, bf16[2,4,16,128]{3,2,1,0:T(8,128)(2,1)} %copy-done.2, bf16[2,4,16,128]{3,2,1,0:T(8,128)(2,1)} %copy-done.12, bf16[2,4,16,128]{3,2,1,0:T(8,128)(2,1)} %copy-done.13, bf16[2,4,16,128]{3,2,1,0:T(8,128)(2,1)} %copy-done.14, bf16[2,4,16,128]{3,2,1,0:T(8,128)(2,1)} %copy-done.15, ...), custom_call_target="tpu_custom_call" | custom-call | tf_op jit(solution)/shard_map/pallas_call | solution.py:367
  (40 shorter events, 0.1 us)
Async XLA Ops:
  2.0 6.3 %collective-permute-start.1 = (bf16[16,16,128]{2,1,0:T(8,128)(2,1)}, bf16[16,16,128]{2,1,0:T(8,128)(2,1)S(1)}, u32[]{:S(2)}, u32[]{:S(2)}) collective-permute-start(bf16[16,16,128]{2,1,0:T(8,128)(2,1)} %get-tuple-element.15), channel_id=1, source_target_pairs={{0,16},{1,0},{2,18},{3,2},{4,20},{5,4},{6,22},{7,6},{8,24},{9,8},{... | collective-permute-start | bytes 196616 | tf_op jit(solution)/shard_map/ppermute | solution.py:273
  6.1 2.2 %collective-permute-start.2 = (bf16[16,16,128]{2,1,0:T(8,128)(2,1)}, bf16[16,16,128]{2,1,0:T(8,128)(2,1)S(1)}, u32[]{:S(2)}, u32[]{:S(2)}) collective-permute-start(bf16[16,16,128]{2,1,0:T(8,128)(2,1)} %get-tuple-element.15), channel_id=1, source_target_pairs={{1,16},{3,18},{5,20},{7,22},{9,24},{11,26},{13,28},{15,30},{16,1},... | collective-permute-start | bytes 196616 | tf_op jit(solution)/shard_map/ppermute | solution.py:273
  8.3 12.0 %copy-start.10 = (bf16[16,16,128]{2,1,0:T(8,128)(2,1)S(1)}, bf16[16,16,128]{2,1,0:T(8,128)(2,1)}, u32[]{:S(2)}) copy-start(bf16[16,16,128]{2,1,0:T(8,128)(2,1)} %get-tuple-element.14.refs_0_) | copy-start | bytes 196612
  9.2 19.4 %copy-start.1 = (bf16[2,16,16,128]{3,2,1,0:T(8,128)(2,1)}, bf16[2,16,16,128]{3,2,1,0:T(8,128)(2,1)S(1)}, u32[]{:S(2)}) copy-start(bf16[2,16,16,128]{3,2,1,0:T(8,128)(2,1)S(1)} %maximum_select_fusion.refs_2_) | copy-start | bytes 393220
  9.2 6.1 %collective-permute-start.3 = (bf16[2,16,16,128]{3,2,1,0:T(8,128)(2,1)S(1)}, bf16[2,16,16,128]{3,2,1,0:T(8,128)(2,1)S(1)}, u32[]{:S(2)}, u32[]{:S(2)}) collective-permute-start(bf16[2,16,16,128]{3,2,1,0:T(8,128)(2,1)S(1)} %maximum_select_fusion.refs_2_), channel_id=1, source_target_pairs={{0,8},{1,9},{2,10},{3,11},{4,12},{5,13},{6,14},{7,15},{8,0},{9,1},... | collective-permute-start | bytes 393224 | tf_op jit(solution)/shard_map/ppermute | solution.py:273
  11.6 5.8 %collective-permute-start.4 = (bf16[2,16,16,128]{3,2,1,0:T(8,128)(2,1)S(1)}, bf16[2,16,16,128]{3,2,1,0:T(8,128)(2,1)S(1)}, u32[]{:S(2)}, u32[]{:S(2)}) collective-permute-start(bf16[2,16,16,128]{3,2,1,0:T(8,128)(2,1)S(1)} %maximum_select_fusion.refs_2_), channel_id=1, source_target_pairs={{0,4},{1,5},{2,6},{3,7},{4,0},{5,1},{6,2},{7,3},{8,12},{9,13},{10,... | collective-permute-start | bytes 393224 | tf_op jit(solution)/shard_map/ppermute | solution.py:273
  15.4 13.2 %copy-start.3 = (bf16[2,16,16,128]{3,2,1,0:T(8,128)(2,1)}, bf16[2,16,16,128]{3,2,1,0:T(8,128)(2,1)S(1)}, u32[]{:S(2)}) copy-start(bf16[2,16,16,128]{3,2,1,0:T(8,128)(2,1)S(1)} %collective-permute-done.3.refs_3_) | copy-start | bytes 393220
  15.4 5.0 %collective-permute-start.5 = (bf16[2,16,16,128]{3,2,1,0:T(8,128)(2,1)S(1)}, bf16[2,16,16,128]{3,2,1,0:T(8,128)(2,1)S(1)}, u32[]{:S(2)}, u32[]{:S(2)}) collective-permute-start(bf16[2,16,16,128]{3,2,1,0:T(8,128)(2,1)S(1)} %collective-permute-done.3.refs_3_), channel_id=1, source_target_pairs={{0,4},{1,5},{2,6},{3,7},{4,0},{5,1},{6,2},{7,3},{8,12},{9,13},{10,... | collective-permute-start | bytes 393224 | tf_op jit(solution)/shard_map/ppermute | solution.py:273
  16.9 12.5 %collective-permute-start.6 = (bf16[2,16,16,128]{3,2,1,0:T(8,128)(2,1)S(1)}, bf16[2,16,16,128]{3,2,1,0:T(8,128)(2,1)S(1)}, u32[]{:S(2)}, u32[]{:S(2)}) collective-permute-start(bf16[2,16,16,128]{3,2,1,0:T(8,128)(2,1)S(1)} %maximum_select_fusion.refs_2_), channel_id=1, source_target_pairs={{0,2},{1,3},{2,0},{3,1},{4,6},{5,7},{6,4},{7,5},{8,10},{9,11},{10,... | collective-permute-start | bytes 393224 | tf_op jit(solution)/shard_map/ppermute | solution.py:273
  16.9 12.5 %collective-permute-start.7 = (bf16[2,16,16,128]{3,2,1,0:T(8,128)(2,1)S(1)}, bf16[2,16,16,128]{3,2,1,0:T(8,128)(2,1)S(1)}, u32[]{:S(2)}, u32[]{:S(2)}) collective-permute-start(bf16[2,16,16,128]{3,2,1,0:T(8,128)(2,1)S(1)} %collective-permute-done.3.refs_3_), channel_id=1, source_target_pairs={{0,2},{1,3},{2,0},{3,1},{4,6},{5,7},{6,4},{7,5},{8,10},{9,11},{10,... | collective-permute-start | bytes 393224 | tf_op jit(solution)/shard_map/ppermute | solution.py:273
  17.4 11.2 %copy-start.4 = (bf16[2,16,16,128]{3,2,1,0:T(8,128)(2,1)}, bf16[2,16,16,128]{3,2,1,0:T(8,128)(2,1)S(1)}, u32[]{:S(2)}) copy-start(bf16[2,16,16,128]{3,2,1,0:T(8,128)(2,1)S(1)} %collective-permute-done.4.refs_4_) | copy-start | bytes 393220
  17.4 12.0 %collective-permute-start.8 = (bf16[2,16,16,128]{3,2,1,0:T(8,128)(2,1)S(1)}, bf16[2,16,16,128]{3,2,1,0:T(8,128)(2,1)S(1)}, u32[]{:S(2)}, u32[]{:S(2)}) collective-permute-start(bf16[2,16,16,128]{3,2,1,0:T(8,128)(2,1)S(1)} %collective-permute-done.4.refs_4_), channel_id=1, source_target_pairs={{0,2},{1,3},{2,0},{3,1},{4,6},{5,7},{6,4},{7,5},{8,10},{9,11},{10,... | collective-permute-start | bytes 393224 | tf_op jit(solution)/shard_map/ppermute | solution.py:273
  20.3 8.3 %copy-start.5 = (bf16[2,16,16,128]{3,2,1,0:T(8,128)(2,1)}, bf16[2,16,16,128]{3,2,1,0:T(8,128)(2,1)S(1)}, u32[]{:S(2)}) copy-start(bf16[2,16,16,128]{3,2,1,0:T(8,128)(2,1)S(1)} %collective-permute-done.5.refs_5_) | copy-start | bytes 393220
  20.3 9.1 %collective-permute-start.9 = (bf16[2,16,16,128]{3,2,1,0:T(8,128)(2,1)S(1)}, bf16[2,16,16,128]{3,2,1,0:T(8,128)(2,1)S(1)}, u32[]{:S(2)}, u32[]{:S(2)}) collective-permute-start(bf16[2,16,16,128]{3,2,1,0:T(8,128)(2,1)S(1)} %collective-permute-done.5.refs_5_), channel_id=1, source_target_pairs={{0,2},{1,3},{2,0},{3,1},{4,6},{5,7},{6,4},{7,5},{8,10},{9,11},{10,... | collective-permute-start | bytes 393224 | tf_op jit(solution)/shard_map/ppermute | solution.py:273
  20.3 8.3 %copy-start.19 = (bf16[128,4]{0,1:T(4,128)(2,1)S(1)}, bf16[128,4]{0,1:T(4,128)(2,1)}, u32[]{:S(2)}) copy-start(bf16[128,4]{0,1:T(4,128)(2,1)} %param.18) | copy-start | bytes 3076
  20.4 9.0 %collective-permute-start = (bf16[16,16,128]{2,1,0:T(8,128)(2,1)S(1)}, bf16[16,16,128]{2,1,0:T(8,128)(2,1)S(1)}, u32[]{:S(2)}, u32[]{:S(2)}) collective-permute-start(bf16[16,16,128]{2,1,0:T(8,128)(2,1)S(1)} %copy-done.10), channel_id=1, source_target_pairs={{0,1},{1,0},{2,3},{3,2},{4,5},{5,4},{6,7},{7,6},{8,9},{9,8},{10,11... | collective-permute-start | bytes 196616 | tf_op jit(solution)/shard_map/ppermute | solution.py:273
  29.4 0.6 copy-start.11
  29.4 0.7 copy-start.6
  29.4 0.7 copy-start.7
  29.4 0.7 copy-start.8
  29.4 0.8 copy-start.9
  38.3 27.5 %collective-permute-start.19 = (bf16[16,128,128]{2,1,0:T(8,128)(2,1)}, bf16[16,128,128]{2,1,0:T(8,128)(2,1)S(1)}, u32[]{:S(2)}, u32[]{:S(2)}) collective-permute-start(bf16[16,128,128]{2,1,0:T(8,128)(2,1)} %get-tuple-element.17.refs_14_), channel_id=1, source_target_pairs={{0,1},{1,0},{2,3},{3,2},{4,5},{5,4},{6,7},{7,6},{8,9},{9,8},{10,11... | collective-permute-start | bytes 1572872 | tf_op jit(solution)/shard_map/ppermute | solution.py:273
  38.4 14.4 %collective-permute-start.10 = (bf16[4,16,128]{2,1,0:T(8,128)(2,1)}, bf16[4,16,128]{2,1,0:T(8,128)(2,1)S(1)}, u32[]{:S(2)}, u32[]{:S(2)}) collective-permute-start(bf16[4,16,128]{2,1,0:T(8,128)(2,1)} %get-tuple-element.16), channel_id=1, source_target_pairs={{0,16},{1,0},{2,18},{3,2},{4,20},{5,4},{6,22},{7,6},{8,24},{9,8},{... | collective-permute-start | bytes 49160 | tf_op jit(solution)/shard_map/ppermute | solution.py:273
  42.2 10.7 %collective-permute-start.11 = (bf16[4,16,128]{2,1,0:T(8,128)(2,1)}, bf16[4,16,128]{2,1,0:T(8,128)(2,1)S(1)}, u32[]{:S(2)}, u32[]{:S(2)}) collective-permute-start(bf16[4,16,128]{2,1,0:T(8,128)(2,1)} %get-tuple-element.16), channel_id=1, source_target_pairs={{1,16},{3,18},{5,20},{7,22},{9,24},{11,26},{13,28},{15,30},{16,1},... | collective-permute-start | bytes 49160 | tf_op jit(solution)/shard_map/ppermute | solution.py:273
  53.5 12.1 %copy-start.2 = (bf16[2,4,16,128]{3,2,1,0:T(8,128)(2,1)}, bf16[2,4,16,128]{3,2,1,0:T(8,128)(2,1)S(1)}, u32[]{:S(2)}) copy-start(bf16[2,4,16,128]{3,2,1,0:T(8,128)(2,1)S(1)} %maximum_select_fusion.1.refs_1_) | copy-start | bytes 98308
  53.5 3.9 %collective-permute-start.12 = (bf16[2,4,16,128]{3,2,1,0:T(8,128)(2,1)S(1)}, bf16[2,4,16,128]{3,2,1,0:T(8,128)(2,1)S(1)}, u32[]{:S(2)}, u32[]{:S(2)}) collective-permute-start(bf16[2,4,16,128]{3,2,1,0:T(8,128)(2,1)S(1)} %maximum_select_fusion.1.refs_1_), channel_id=1, source_target_pairs={{0,8},{1,9},{2,10},{3,11},{4,12},{5,13},{6,14},{7,15},{8,0},{9,1},... | collective-permute-start | bytes 98312 | tf_op jit(solution)/shard_map/ppermute | solution.py:273
  54.7 4.7 %collective-permute-start.13 = (bf16[2,4,16,128]{3,2,1,0:T(8,128)(2,1)S(1)}, bf16[2,4,16,128]{3,2,1,0:T(8,128)(2,1)S(1)}, u32[]{:S(2)}, u32[]{:S(2)}) collective-permute-start(bf16[2,4,16,128]{3,2,1,0:T(8,128)(2,1)S(1)} %maximum_select_fusion.1.refs_1_), channel_id=1, source_target_pairs={{0,4},{1,5},{2,6},{3,7},{4,0},{5,1},{6,2},{7,3},{8,12},{9,13},{10,... | collective-permute-start | bytes 98312 | tf_op jit(solution)/shard_map/ppermute | solution.py:273
  57.5 8.2 %copy-start.12 = (bf16[2,4,16,128]{3,2,1,0:T(8,128)(2,1)}, bf16[2,4,16,128]{3,2,1,0:T(8,128)(2,1)S(1)}, u32[]{:S(2)}) copy-start(bf16[2,4,16,128]{3,2,1,0:T(8,128)(2,1)S(1)} %collective-permute-done.12.refs_2_) | copy-start | bytes 98308
  57.5 3.9 %collective-permute-start.14 = (bf16[2,4,16,128]{3,2,1,0:T(8,128)(2,1)S(1)}, bf16[2,4,16,128]{3,2,1,0:T(8,128)(2,1)S(1)}, u32[]{:S(2)}, u32[]{:S(2)}) collective-permute-start(bf16[2,4,16,128]{3,2,1,0:T(8,128)(2,1)S(1)} %collective-permute-done.12.refs_2_), channel_id=1, source_target_pairs={{0,4},{1,5},{2,6},{3,7},{4,0},{5,1},{6,2},{7,3},{8,12},{9,13},{10,... | collective-permute-start | bytes 98312 | tf_op jit(solution)/shard_map/ppermute | solution.py:273
  58.9 6.8 %collective-permute-start.15 = (bf16[2,4,16,128]{3,2,1,0:T(8,128)(2,1)S(1)}, bf16[2,4,16,128]{3,2,1,0:T(8,128)(2,1)S(1)}, u32[]{:S(2)}, u32[]{:S(2)}) collective-permute-start(bf16[2,4,16,128]{3,2,1,0:T(8,128)(2,1)S(1)} %maximum_select_fusion.1.refs_1_), channel_id=1, source_target_pairs={{0,2},{1,3},{2,0},{3,1},{4,6},{5,7},{6,4},{7,5},{8,10},{9,11},{10,... | collective-permute-start | bytes 98312 | tf_op jit(solution)/shard_map/ppermute | solution.py:273
  58.9 6.8 %collective-permute-start.16 = (bf16[2,4,16,128]{3,2,1,0:T(8,128)(2,1)S(1)}, bf16[2,4,16,128]{3,2,1,0:T(8,128)(2,1)S(1)}, u32[]{:S(2)}, u32[]{:S(2)}) collective-permute-start(bf16[2,4,16,128]{3,2,1,0:T(8,128)(2,1)S(1)} %collective-permute-done.12.refs_2_), channel_id=1, source_target_pairs={{0,2},{1,3},{2,0},{3,1},{4,6},{5,7},{6,4},{7,5},{8,10},{9,11},{10,... | collective-permute-start | bytes 98312 | tf_op jit(solution)/shard_map/ppermute | solution.py:273
  59.5 6.2 %copy-start.13 = (bf16[2,4,16,128]{3,2,1,0:T(8,128)(2,1)}, bf16[2,4,16,128]{3,2,1,0:T(8,128)(2,1)S(1)}, u32[]{:S(2)}) copy-start(bf16[2,4,16,128]{3,2,1,0:T(8,128)(2,1)S(1)} %collective-permute-done.13.refs_3_) | copy-start | bytes 98308
  59.5 6.3 %collective-permute-start.17 = (bf16[2,4,16,128]{3,2,1,0:T(8,128)(2,1)S(1)}, bf16[2,4,16,128]{3,2,1,0:T(8,128)(2,1)S(1)}, u32[]{:S(2)}, u32[]{:S(2)}) collective-permute-start(bf16[2,4,16,128]{3,2,1,0:T(8,128)(2,1)S(1)} %collective-permute-done.13.refs_3_), channel_id=1, source_target_pairs={{0,2},{1,3},{2,0},{3,1},{4,6},{5,7},{6,4},{7,5},{8,10},{9,11},{10,... | collective-permute-start | bytes 98312 | tf_op jit(solution)/shard_map/ppermute | solution.py:273
  61.4 4.3 %copy-start.14 = (bf16[2,4,16,128]{3,2,1,0:T(8,128)(2,1)}, bf16[2,4,16,128]{3,2,1,0:T(8,128)(2,1)S(1)}, u32[]{:S(2)}) copy-start(bf16[2,4,16,128]{3,2,1,0:T(8,128)(2,1)S(1)} %collective-permute-done.14.refs_4_) | copy-start | bytes 98308
  61.4 4.4 %collective-permute-start.18 = (bf16[2,4,16,128]{3,2,1,0:T(8,128)(2,1)S(1)}, bf16[2,4,16,128]{3,2,1,0:T(8,128)(2,1)S(1)}, u32[]{:S(2)}, u32[]{:S(2)}) collective-permute-start(bf16[2,4,16,128]{3,2,1,0:T(8,128)(2,1)S(1)} %collective-permute-done.14.refs_4_), channel_id=1, source_target_pairs={{0,2},{1,3},{2,0},{3,1},{4,6},{5,7},{6,4},{7,5},{8,10},{9,11},{10,... | collective-permute-start | bytes 98312 | tf_op jit(solution)/shard_map/ppermute | solution.py:273
  65.7 0.6 copy-start.15
  65.7 0.6 copy-start.16
  65.7 0.6 copy-start.17
  65.8 0.6 copy-start.18
  65.8 0.8 %copy-start = (bf16[16,128,128]{2,1,0:T(8,128)(2,1)}, bf16[16,128,128]{2,1,0:T(8,128)(2,1)S(1)}, u32[]{:S(2)}) copy-start(bf16[16,128,128]{2,1,0:T(8,128)(2,1)S(1)} %collective-permute-done.19.refs_9_) | copy-start | bytes 1572868
where the time goes:
time: 78.3 us; the launch traced here: 77.9 us
  Pallas kernels  29.3 us (37%)
  starting transfers between devices  24.7 us (32%)
  waiting for transfers between devices  19.8 us (25%)
  local copies, waits for them, and re-layouts  2.34 us (3%)
  other arithmetic  1.62 us (2%)
    ppermute x20, starting transfers between devices, move(): return lax.ppermute(value, ('row', 'col'), pairs)  24.7 us
    ppermute x20, waiting for transfers between devices, move(): return lax.ppermute(value, ('row', 'col'), pairs)  19.8 us
    pallas_call x1, Pallas kernels, body(): call(make_attend_kernel(n_col, n_blk, grid.place, grid.col_of), wide, 1,...  11.3 us
    pallas_call x1, Pallas kernels, body(): call(make_tri_kernel(n_col, n_blk, grid.place), (jax.ShapeDtypeStruct(who...  8.08 us
    pallas_call x1, Pallas kernels, body(): call(project_kernel, (wide, wide, wide, jax.ShapeDtypeStruct(whole, F32))...  4.3 us
    pallas_call x1, Pallas kernels, body(): call(gate_kernel, jax.ShapeDtypeStruct(whole, F32), 0, 3)  3.53 us
    unnamed x41, local copies, waits for them, and re-layouts  2.34 us
    pallas_call x1, Pallas kernels, body(): pl.pallas_call(functools.partial(edge_kernel, cols=cols), name='edges', g...  2.04 us
  transfers between devices with their start and end apart: 20, of which 6 were waited for; matrix products, arithmetic and copies ran while one was open for 2% of the time, Pallas kernels for 10%

commit v1 on v0

--- a/solution.py
+++ b/solution.py
@@ -17,7 +17,8 @@
 
 EPSILON = 1e-05
 NEG_SCORE = -1e30
-VMEM_LIMIT = 60 * 1024 * 1024
+MIB = 1024 * 1024
+RESIDENT_LIMIT = 32 * MIB
 
 F32 = jnp.float32
 BF16 = jnp.bfloat16
@@ -41,18 +42,29 @@
     return lax.dot_general(a, b, (((1,), (1,)), ((), ())), preferred_element_type=F32)
 
 
-def call(kernel, out_shape, n_smem, n_in, scratch=()):
+def call(kernel, out_shape, n_smem, n_in, limit, scratch=(), held_out=True):
     smem = pl.BlockSpec(memory_space=pltpu.SMEM)
     vmem = pl.BlockSpec(memory_space=pltpu.VMEM)
     outs = jax.tree.map(lambda _: vmem, out_shape)
-    return pl.pallas_call(
+    resident = limit < RESIDENT_LIMIT
+    if resident and held_out:
+        out_shape = jax.tree.map(lambda o: pltpu.VMEM(o.shape, o.dtype), out_shape)
+    run = pl.pallas_call(
         kernel,
         out_shape=out_shape,
         in_specs=[smem] * n_smem + [vmem] * n_in,
         out_specs=outs,
         scratch_shapes=list(scratch),
-        compiler_params=pltpu.CompilerParams(vmem_limit_bytes=VMEM_LIMIT),
+        compiler_params=pltpu.CompilerParams(vmem_limit_bytes=limit),
     )
+
+    def apply(*args):
+        if not resident:
+            return run(*args)
+        held = [pltpu.with_memory_space_constraint(a, pltpu.VMEM) for a in args[n_smem:]]
+        return run(*args[:n_smem], *held)
+
+    return apply
 
 
 def edge_kernel(len_ref, pair_ref, gain_ref, w_ref, left_ref, right_ref, scratch_ref, *, cols):
@@ -133,9 +145,7 @@
             mid_ref[at] = mid.reshape(step, cols, width)
             att = layer_norm(mid.astype(F32), att_gain_ref[...]).astype(BF16)
             norm_ref[at] = att.reshape(step, cols, width)
-            bias = lax.dot_general(
-                bias_w_ref[...], att, (((0,), (1,)), ((), ())), preferred_element_type=F32
-            )
+            bias = dot_nt(bias_w_ref[...], att)
             for u in range(step):
                 bias_scr[t * step + u] = bias[:, u * cols : (u + 1) * cols]
             return carry
@@ -161,7 +171,7 @@
         gate_ref[at] = sigmoid(out[:, 3 * width :]).reshape(shape)
         return carry
 
-    lax.fori_loop(0, rows // step, body, 0)
+    lax.fori_loop(0, rows // step, body, 0, unroll=2)
 
 
 def make_attend_kernel(n_col, n_blk, place, col_of):
@@ -316,6 +326,7 @@
         rows, cols, width = pair_rep.shape
         n_col, n_blk = grid.n_col, grid.n_blk
         whole = (rows, cols, width)
+        limit = min(60 * MIB, 12 * MIB + 24 * H * cols * n_col * cols * 4)
         tri_gain = tri_gain.reshape(1, width)
         sum_gain = sum_gain.reshape(1, width)
         att_gain = att_gain.reshape(1, width)
@@ -342,7 +353,9 @@
         )(chain_len, pair_rep, tri_gain, tri_in)
         rights = grid.gather(right)
         lefts = [left] + [grid.shift_col(left, d) for d in range(1, n_col)]
-        gate = call(gate_kernel, jax.ShapeDtypeStruct(whole, F32), 0, 3)(pair_rep, tri_gain, tri_in)
+        gate = call(gate_kernel, jax.ShapeDtypeStruct(whole, F32), 0, 3, limit)(
+            pair_rep, tri_gain, tri_in
+        )
         mid, normed, bias = call(
             make_tri_kernel(n_col, n_blk, grid.place),
             (
@@ -352,28 +365,31 @@
             ),
             0,
             n_col + n_blk + 6,
+            limit,
             [
                 pltpu.VMEM((n_col, rows * KCD, width), F32),
                 pltpu.VMEM(whole, F32),
                 pltpu.VMEM((rows, H, cols), F32),
             ],
-        )(*lefts, *rights, pair_rep, gate, sum_gain, tri_out, att_gain, att_bias)
+        )(*lefts, *rights, pair_rep, gate, sum_gain, tri_out, att_gain, att_bias.T)
         biases = grid.gather(bias)
         others = [grid.shift_col(mid, d) for d in range(1, n_col)]
         wide = jax.ShapeDtypeStruct(whole, BF16)
         query, key, value, att_gate = call(
-            project_kernel, (wide, wide, wide, jax.ShapeDtypeStruct(whole, F32)), 0, 2
+            project_kernel, (wide, wide, wide, jax.ShapeDtypeStruct(whole, F32)), 0, 2, limit
         )(normed, att_in)
         return call(
             make_attend_kernel(n_col, n_blk, grid.place, grid.col_of),
             wide,
             1,
             n_blk + n_col - 1 + 8,
+            limit,
             [
                 pltpu.VMEM((H * cols, n_col * cols), F32),
                 pltpu.VMEM((rows, n_col * cols, width), BF16),
                 pltpu.VMEM((rows, n_col * cols, width), BF16),
             ],
+            held_out=False,
         )(chain_len, *biases, *others, query, key, value, att_gate, mid, att_gain, att_in, att_out)
 
     return body

time: 78.3 us -> 67.9 us (0.87)
  Pallas kernels: 29.3 us -> 19.9 us
  local copies, waits for them, and re-layouts: 2.34 us -> 1.33 us
  waiting for transfers between devices: 19.8 us -> 20.6 us
    pallas_call x4, Pallas kernels: 27.2 us -> 17.9 us  [apply(): return run(*args[:n_smem], *held)]
    unnamed x41 -> x22, local copies, waits for them, and re-layouts: 2.34 us -> 1.33 us
    ppermute x20, waiting for transfers between devices: 19.8 us -> 20.6 us  [move(): return lax.ppermute(value, ('row', 'col'), pairs)]
  transfers between devices with their start and end apart: 20 -> 20, of which waited for: 6 -> 7; matrix products, arithmetic and copies ran while one was open for 2% -> 0% of each run, Pallas kernels for 10% -> 4%
where the time goes in v1:
time: 67.9 us; the launch traced here: 67.7 us
  starting transfers between devices  24.7 us (36%)
  waiting for transfers between devices  20.6 us (30%)
  Pallas kernels  19.9 us (29%)
  local copies, waits for them, and re-layouts  1.33 us (2%)
  other arithmetic  0.91 us (1%)
    ppermute x20, starting transfers between devices, move(): return lax.ppermute(value, ('row', 'col'), pairs)  24.7 us
    ppermute x20, waiting for transfers between devices, move(): return lax.ppermute(value, ('row', 'col'), pairs)  20.6 us
    pallas_call x4, Pallas kernels, apply(): return run(*args[:n_smem], *held)  17.9 us
    pallas_call x1, Pallas kernels, body(): pl.pallas_call(functools.partial(edge_kernel, cols=cols), name='edges', g...  2.08 us
  transfers between devices with their start and end apart: 20, of which 7 were waited for; matrix products, arithmetic and copies ran while one was open for 0% of the time, Pallas kernels for 4%

profile of v1, /device:TPU:0, one launch (start us, length us, event | category | flops | bytes accessed | tf_op | source)
XLA Modules:
  0.0 67.7 jit_solution(16559722139716454706)
XLA Ops:
  0.0 2.1 %edges.1 = (bf16[16,16,128]{2,1,0:T(8,128)(2,1)}, bf16[16,16,128]{2,1,0:T(8,128)(2,1)}) custom-call(s32[4]{0:T(128)} %refs_0_.1, bf16[16,128,128]{2,1,0:T(8,128)(2,1)} %refs_10_.1, f32[1,128]{1,0:T(1,128)} %bitcast.11, bf16[128,640]{1,0:T(8,128)(2,1)} %w_ref.4), custom_call_target="tpu_custom_call" | custom-call | tf_op jit(solution)/shard_map/edges/pallas_call | solution.py:334
  2.1 4.1 %collective-permute-start.1 = (bf16[16,16,128]{2,1,0:T(8,128)(2,1)}, bf16[16,16,128]{2,1,0:T(8,128)(2,1)S(1)}, u32[]{:S(2)}, u32[]{:S(2)}) collective-permute-start(bf16[16,16,128]{2,1,0:T(8,128)(2,1)} %get-tuple-element.15), channel_id=1, source_target_pairs={{0,16},{1,0},{2,18},{3,2},{4,20},{5,4},{6,22},{7,6},{8,24},{9,8},{... | collective-permute-start | bytes 196616 | tf_op jit(solution)/shard_map/ppermute | solution.py:283
  6.2 0.7 collective-permute-start.2
  6.8 1.5 %collective-permute-done.1 = bf16[16,16,128]{2,1,0:T(8,128)(2,1)S(1)} collective-permute-done((bf16[16,16,128]{2,1,0:T(8,128)(2,1)}, bf16[16,16,128]{2,1,0:T(8,128)(2,1)S(1)}, u32[]{:S(2)}, u32[]{:S(2)}) %collective-permute-start.1) | collective-permute-done | bytes 65568 | tf_op jit(solution)/shard_map/ppermute | solution.py:283
  8.4 0.0 collective-permute-done.2
  8.4 0.9 %maximum_select_fusion.refs_2_ = bf16[2,16,16,128]{3,2,1,0:T(8,128)(2,1)S(1)} fusion(bf16[1,16,16,128]{3,2,1,0:T(8,128)(2,1)S(1)} %bitcast.18, bf16[1,16,16,128]{3,2,1,0:T(8,128)(2,1)} %bitcast.17, bf16[1,16,16,128]{3,2,1,0:T(8,128)(2,1)S(1)} %bitcast.19, pred[]{:T(512)S(6)} %eq.4), kind=kLoop, calls=%fused_computation | loop fusion | flops 196608 | bytes 327681 | tf_op jit(solution)/shard_map/jit(_where)/select_n | solution.py:310
  9.3 0.0 copy-start.6
  9.3 2.4 %collective-permute-start.3 = (bf16[2,16,16,128]{3,2,1,0:T(8,128)(2,1)S(1)}, bf16[2,16,16,128]{3,2,1,0:T(8,128)(2,1)S(1)}, u32[]{:S(2)}, u32[]{:S(2)}) collective-permute-start(bf16[2,16,16,128]{3,2,1,0:T(8,128)(2,1)S(1)} %maximum_select_fusion.refs_2_), channel_id=1, source_target_pairs={{0,8},{1,9},{2,10},{3,11},{4,12},{5,13},{6,14},{7,15},{8,0},{9,1},... | collective-permute-start | bytes 393224 | tf_op jit(solution)/shard_map/ppermute | solution.py:283
  11.7 1.5 %collective-permute-start.4 = (bf16[2,16,16,128]{3,2,1,0:T(8,128)(2,1)S(1)}, bf16[2,16,16,128]{3,2,1,0:T(8,128)(2,1)S(1)}, u32[]{:S(2)}, u32[]{:S(2)}) collective-permute-start(bf16[2,16,16,128]{3,2,1,0:T(8,128)(2,1)S(1)} %maximum_select_fusion.refs_2_), channel_id=1, source_target_pairs={{0,4},{1,5},{2,6},{3,7},{4,0},{5,1},{6,2},{7,3},{8,12},{9,13},{10,... | collective-permute-start | bytes 393224 | tf_op jit(solution)/shard_map/ppermute | solution.py:283
  13.2 2.2 %collective-permute-done.3.refs_3_ = bf16[2,16,16,128]{3,2,1,0:T(8,128)(2,1)S(1)} collective-permute-done((bf16[2,16,16,128]{3,2,1,0:T(8,128)(2,1)S(1)}, bf16[2,16,16,128]{3,2,1,0:T(8,128)(2,1)S(1)}, u32[]{:S(2)}, u32[]{:S(2)}) %collective-permute-start.3) | collective-permute-done | bytes 131104 | tf_op jit(solution)/shard_map/ppermute | solution.py:283
  15.4 1.5 %collective-permute-start.5 = (bf16[2,16,16,128]{3,2,1,0:T(8,128)(2,1)S(1)}, bf16[2,16,16,128]{3,2,1,0:T(8,128)(2,1)S(1)}, u32[]{:S(2)}, u32[]{:S(2)}) collective-permute-start(bf16[2,16,16,128]{3,2,1,0:T(8,128)(2,1)S(1)} %collective-permute-done.3.refs_3_), channel_id=1, source_target_pairs={{0,4},{1,5},{2,6},{3,7},{4,0},{5,1},{6,2},{7,3},{8,12},{9,13},{10,... | collective-permute-start | bytes 393224 | tf_op jit(solution)/shard_map/ppermute | solution.py:283
  16.9 0.0 collective-permute-start.6
  16.9 0.5 collective-permute-start.7
  17.4 0.0 collective-permute-done.4.refs_4_
  17.4 0.0 collective-permute-start.8
  17.4 3.0 %collective-permute-done.5.refs_5_ = bf16[2,16,16,128]{3,2,1,0:T(8,128)(2,1)S(1)} collective-permute-done((bf16[2,16,16,128]{3,2,1,0:T(8,128)(2,1)S(1)}, bf16[2,16,16,128]{3,2,1,0:T(8,128)(2,1)S(1)}, u32[]{:S(2)}, u32[]{:S(2)}) %collective-permute-start.5) | collective-permute-done | bytes 131104 | tf_op jit(solution)/shard_map/ppermute | solution.py:283
  20.4 0.0 collective-permute-start.9
  20.4 4.7 %collective-permute-start = (bf16[16,16,128]{2,1,0:T(8,128)(2,1)S(1)}, bf16[16,16,128]{2,1,0:T(8,128)(2,1)S(1)}, u32[]{:S(2)}, u32[]{:S(2)}) collective-permute-start(bf16[16,16,128]{2,1,0:T(8,128)(2,1)S(1)} %copy-done.3), channel_id=1, source_target_pairs={{0,1},{1,0},{2,3},{3,2},{4,5},{5,4},{6,7},{7,6},{8,9},{9,8},{10,11... | collective-permute-start | bytes 196616 | tf_op jit(solution)/shard_map/ppermute | solution.py:283
  25.1 1.4 %shard_map.100.refs_11_ = f32[16,128,128]{2,1,0:T(8,128)S(1)} custom-call(bf16[16,128,128]{2,1,0:T(8,128)(2,1)S(1)} %copy-done, f32[1,128]{1,0:T(1,128)S(1)} %bitcast.12, bf16[128,640]{1,0:T(8,128)(2,1)S(1)} %copy-done.1), custom_call_target="tpu_custom_call" | custom-call | tf_op jit(solution)/shard_map/pallas_call | solution.py:65
  26.6 1.2 %collective-permute-done.refs_1_ = bf16[16,16,128]{2,1,0:T(8,128)(2,1)S(1)} collective-permute-done((bf16[16,16,128]{2,1,0:T(8,128)(2,1)S(1)}, bf16[16,16,128]{2,1,0:T(8,128)(2,1)S(1)}, u32[]{:S(2)}, u32[]{:S(2)}) %collective-permute-start) | collective-permute-done | bytes 65568 | tf_op jit(solution)/shard_map/ppermute | solution.py:283
  27.8 0.0 collective-permute-done.6.refs_6_
  27.8 0.0 collective-permute-done.7.refs_7_
  27.8 0.0 collective-permute-done.8.refs_8_
  27.8 0.0 copy-start.7
  27.8 0.0 copy-start.9
  27.9 0.6 copy-done.7
  28.5 0.0 copy-done.9
  28.5 5.6 %shard_map.101 = (bf16[16,128,128]{2,1,0:T(8,128)(2,1)S(1)}, bf16[16,128,128]{2,1,0:T(8,128)(2,1)S(1)}, bf16[4,16,128]{2,1,0:T(8,128)(2,1)S(1)}) custom-call(bf16[16,16,128]{2,1,0:T(8,128)(2,1)S(1)} %copy-done.3, bf16[16,16,128]{2,1,0:T(8,128)(2,1)S(1)} %collective-permute-done.refs_1_, bf16[2,16,16,128]{3,2,1,0:T(8,128)(2,1)S(1)} %maximum_select_fusion.refs_2_, ...), custom_call_target="tpu_custom_call" | custom-call | tf_op jit(solution)/shard_map/pallas_call | solution.py:65
  34.1 1.8 %collective-permute-start.19 = (bf16[16,128,128]{2,1,0:T(8,128)(2,1)S(1)}, bf16[16,128,128]{2,1,0:T(8,128)(2,1)S(1)}, u32[]{:S(2)}, u32[]{:S(2)}) collective-permute-start(bf16[16,128,128]{2,1,0:T(8,128)(2,1)S(1)} %get-tuple-element.17.refs_14_), channel_id=1, source_target_pairs={{0,1},{1,0},{2,3},{3,2},{4,5},{5,4},{6,7},{7,6},{8,9},{9,8},{10,11... | collective-permute-start | bytes 1572872 | tf_op jit(solution)/shard_map/ppermute | solution.py:283
  35.9 2.1 %collective-permute-start.10 = (bf16[4,16,128]{2,1,0:T(8,128)(2,1)S(1)}, bf16[4,16,128]{2,1,0:T(8,128)(2,1)S(1)}, u32[]{:S(2)}, u32[]{:S(2)}) collective-permute-start(bf16[4,16,128]{2,1,0:T(8,128)(2,1)S(1)} %get-tuple-element.16), channel_id=1, source_target_pairs={{0,16},{1,0},{2,18},{3,2},{4,20},{5,4},{6,22},{7,6},{8,24},{9,8},{... | collective-permute-start | bytes 49160 | tf_op jit(solution)/shard_map/ppermute | solution.py:283
  38.0 0.7 collective-permute-start.11
  38.7 9.5 %collective-permute-done.10 = bf16[4,16,128]{2,1,0:T(8,128)(2,1)S(1)} collective-permute-done((bf16[4,16,128]{2,1,0:T(8,128)(2,1)S(1)}, bf16[4,16,128]{2,1,0:T(8,128)(2,1)S(1)}, u32[]{:S(2)}, u32[]{:S(2)}) %collective-permute-start.10) | collective-permute-done | bytes 16416 | tf_op jit(solution)/shard_map/ppermute | solution.py:283
  48.2 1.3 %collective-permute-start.12 = (bf16[2,4,16,128]{3,2,1,0:T(8,128)(2,1)S(1)}, bf16[2,4,16,128]{3,2,1,0:T(8,128)(2,1)S(1)}, u32[]{:S(2)}, u32[]{:S(2)}) collective-permute-start(bf16[2,4,16,128]{3,2,1,0:T(8,128)(2,1)S(1)} %maximum_select_fusion.1.refs_1_), channel_id=1, source_target_pairs={{0,8},{1,9},{2,10},{3,11},{4,12},{5,13},{6,14},{7,15},{8,0},{9,1},... | collective-permute-start | bytes 98312 | tf_op jit(solution)/shard_map/ppermute | solution.py:283
  49.5 1.5 %collective-permute-start.13 = (bf16[2,4,16,128]{3,2,1,0:T(8,128)(2,1)S(1)}, bf16[2,4,16,128]{3,2,1,0:T(8,128)(2,1)S(1)}, u32[]{:S(2)}, u32[]{:S(2)}) collective-permute-start(bf16[2,4,16,128]{3,2,1,0:T(8,128)(2,1)S(1)} %maximum_select_fusion.1.refs_1_), channel_id=1, source_target_pairs={{0,4},{1,5},{2,6},{3,7},{4,0},{5,1},{6,2},{7,3},{8,12},{9,13},{10,... | collective-permute-start | bytes 98312 | tf_op jit(solution)/shard_map/ppermute | solution.py:283
  51.0 1.2 %collective-permute-done.12.refs_2_ = bf16[2,4,16,128]{3,2,1,0:T(8,128)(2,1)S(1)} collective-permute-done((bf16[2,4,16,128]{3,2,1,0:T(8,128)(2,1)S(1)}, bf16[2,4,16,128]{3,2,1,0:T(8,128)(2,1)S(1)}, u32[]{:S(2)}, u32[]{:S(2)}) %collective-permute-start.12) | collective-permute-done | bytes 32800 | tf_op jit(solution)/shard_map/ppermute | solution.py:283
  52.2 1.5 %collective-permute-start.14 = (bf16[2,4,16,128]{3,2,1,0:T(8,128)(2,1)S(1)}, bf16[2,4,16,128]{3,2,1,0:T(8,128)(2,1)S(1)}, u32[]{:S(2)}, u32[]{:S(2)}) collective-permute-start(bf16[2,4,16,128]{3,2,1,0:T(8,128)(2,1)S(1)} %collective-permute-done.12.refs_2_), channel_id=1, source_target_pairs={{0,4},{1,5},{2,6},{3,7},{4,0},{5,1},{6,2},{7,3},{8,12},{9,13},{10,... | collective-permute-start | bytes 98312 | tf_op jit(solution)/shard_map/ppermute | solution.py:283
  53.7 0.0 collective-permute-start.15
  53.7 0.5 collective-permute-start.16
  54.2 0.0 collective-permute-done.13.refs_3_
  54.2 0.0 collective-permute-start.17
  54.2 1.9 %collective-permute-done.14.refs_4_ = bf16[2,4,16,128]{3,2,1,0:T(8,128)(2,1)S(1)} collective-permute-done((bf16[2,4,16,128]{3,2,1,0:T(8,128)(2,1)S(1)}, bf16[2,4,16,128]{3,2,1,0:T(8,128)(2,1)S(1)}, u32[]{:S(2)}, u32[]{:S(2)}) %collective-permute-start.14) | collective-permute-done | bytes 32800 | tf_op jit(solution)/shard_map/ppermute | solution.py:283
  56.1 0.0 collective-permute-start.18
  56.1 1.2 %shard_map.102 = (bf16[16,128,128]{2,1,0:T(8,128)(2,1)S(1)}, bf16[16,128,128]{2,1,0:T(8,128)(2,1)S(1)}, bf16[16,128,128]{2,1,0:T(8,128)(2,1)S(1)}, f32[16,128,128]{2,1,0:T(8,128)S(1)}) custom-call(bf16[16,128,128]{2,1,0:T(8,128)(2,1)S(1)} %get-tuple-element.18.norm_ref, bf16[128,512]{1,0:T(8,128)(2,1)S(1)} %copy-done.2), custom_call_target="tpu_custom_call" | custom-call | tf_op jit(solution)/shard_map/pallas_call | solution.py:65
  57.3 0.0 collective-permute-done.17.refs_7_
  57.3 0.0 collective-permute-done.18.refs_8_
  57.3 0.0 copy-start.8
  57.4 0.6 copy-done.8
  58.0 9.7 %shard_map.103 = bf16[16,128,128]{2,1,0:T(8,128)(2,1)} custom-call(s32[4]{0:T(128)S(1)} %copy-done.8, bf16[2,4,16,128]{3,2,1,0:T(8,128)(2,1)S(1)} %maximum_select_fusion.1.refs_1_, bf16[2,4,16,128]{3,2,1,0:T(8,128)(2,1)S(1)} %collective-permute-done.12.refs_2_, bf16[2,4,16,128]{3,2,1,0:T(8,128)(2,1)S(1)} %collective-permute-done.13.refs_3_, ...), custom_call_target="tpu_custom_call" | custom-call | tf_op jit(solution)/shard_map/pallas_call | solution.py:65
  (21 shorter events, 0.0 us)
Async XLA Ops:
  0.0 25.1 %copy-start = (bf16[16,128,128]{2,1,0:T(8,128)(2,1)S(1)}, bf16[16,128,128]{2,1,0:T(8,128)(2,1)}, u32[]{:S(2)}) copy-start(bf16[16,128,128]{2,1,0:T(8,128)(2,1)} %refs_10_.1) | copy-start | bytes 1572868
  2.1 6.3 %collective-permute-start.1 = (bf16[16,16,128]{2,1,0:T(8,128)(2,1)}, bf16[16,16,128]{2,1,0:T(8,128)(2,1)S(1)}, u32[]{:S(2)}, u32[]{:S(2)}) collective-permute-start(bf16[16,16,128]{2,1,0:T(8,128)(2,1)} %get-tuple-element.15), channel_id=1, source_target_pairs={{0,16},{1,0},{2,18},{3,2},{4,20},{5,4},{6,22},{7,6},{8,24},{9,8},{... | collective-permute-start | bytes 196616 | tf_op jit(solution)/shard_map/ppermute | solution.py:283
  6.2 2.2 %collective-permute-start.2 = (bf16[16,16,128]{2,1,0:T(8,128)(2,1)}, bf16[16,16,128]{2,1,0:T(8,128)(2,1)S(1)}, u32[]{:S(2)}, u32[]{:S(2)}) collective-permute-start(bf16[16,16,128]{2,1,0:T(8,128)(2,1)} %get-tuple-element.15), channel_id=1, source_target_pairs={{1,16},{3,18},{5,20},{7,22},{9,24},{11,26},{13,28},{15,30},{16,1},... | collective-permute-start | bytes 196616 | tf_op jit(solution)/shard_map/ppermute | solution.py:283
  8.4 12.0 %copy-start.3 = (bf16[16,16,128]{2,1,0:T(8,128)(2,1)S(1)}, bf16[16,16,128]{2,1,0:T(8,128)(2,1)}, u32[]{:S(2)}) copy-start(bf16[16,16,128]{2,1,0:T(8,128)(2,1)} %get-tuple-element.14.refs_0_) | copy-start | bytes 196612
  8.4 16.7 %copy-start.1 = (bf16[128,640]{1,0:T(8,128)(2,1)S(1)}, bf16[128,640]{1,0:T(8,128)(2,1)}, u32[]{:S(2)}) copy-start(bf16[128,640]{1,0:T(8,128)(2,1)} %w_ref.4) | copy-start | bytes 491524
  9.3 15.8 %copy-start.6 = (f32[128]{0:T(128)S(1)}, f32[128]{0:T(128)}, u32[]{:S(2)}) copy-start(f32[128]{0:T(128)} %param.12) | copy-start | bytes 1540
  9.3 6.1 %collective-permute-start.3 = (bf16[2,16,16,128]{3,2,1,0:T(8,128)(2,1)S(1)}, bf16[2,16,16,128]{3,2,1,0:T(8,128)(2,1)S(1)}, u32[]{:S(2)}, u32[]{:S(2)}) collective-permute-start(bf16[2,16,16,128]{3,2,1,0:T(8,128)(2,1)S(1)} %maximum_select_fusion.refs_2_), channel_id=1, source_target_pairs={{0,8},{1,9},{2,10},{3,11},{4,12},{5,13},{6,14},{7,15},{8,0},{9,1},... | collective-permute-start | bytes 393224 | tf_op jit(solution)/shard_map/ppermute | solution.py:283
  11.7 5.7 %collective-permute-start.4 = (bf16[2,16,16,128]{3,2,1,0:T(8,128)(2,1)S(1)}, bf16[2,16,16,128]{3,2,1,0:T(8,128)(2,1)S(1)}, u32[]{:S(2)}, u32[]{:S(2)}) collective-permute-start(bf16[2,16,16,128]{3,2,1,0:T(8,128)(2,1)S(1)} %maximum_select_fusion.refs_2_), channel_id=1, source_target_pairs={{0,4},{1,5},{2,6},{3,7},{4,0},{5,1},{6,2},{7,3},{8,12},{9,13},{10,... | collective-permute-start | bytes 393224 | tf_op jit(solution)/shard_map/ppermute | solution.py:283
  15.4 5.0 %collective-permute-start.5 = (bf16[2,16,16,128]{3,2,1,0:T(8,128)(2,1)S(1)}, bf16[2,16,16,128]{3,2,1,0:T(8,128)(2,1)S(1)}, u32[]{:S(2)}, u32[]{:S(2)}) collective-permute-start(bf16[2,16,16,128]{3,2,1,0:T(8,128)(2,1)S(1)} %collective-permute-done.3.refs_3_), channel_id=1, source_target_pairs={{0,4},{1,5},{2,6},{3,7},{4,0},{5,1},{6,2},{7,3},{8,12},{9,13},{10,... | collective-permute-start | bytes 393224 | tf_op jit(solution)/shard_map/ppermute | solution.py:283
  16.9 10.9 %collective-permute-start.6 = (bf16[2,16,16,128]{3,2,1,0:T(8,128)(2,1)S(1)}, bf16[2,16,16,128]{3,2,1,0:T(8,128)(2,1)S(1)}, u32[]{:S(2)}, u32[]{:S(2)}) collective-permute-start(bf16[2,16,16,128]{3,2,1,0:T(8,128)(2,1)S(1)} %maximum_select_fusion.refs_2_), channel_id=1, source_target_pairs={{0,2},{1,3},{2,0},{3,1},{4,6},{5,7},{6,4},{7,5},{8,10},{9,11},{10,... | collective-permute-start | bytes 393224 | tf_op jit(solution)/shard_map/ppermute | solution.py:283
  16.9 10.9 %collective-permute-start.7 = (bf16[2,16,16,128]{3,2,1,0:T(8,128)(2,1)S(1)}, bf16[2,16,16,128]{3,2,1,0:T(8,128)(2,1)S(1)}, u32[]{:S(2)}, u32[]{:S(2)}) collective-permute-start(bf16[2,16,16,128]{3,2,1,0:T(8,128)(2,1)S(1)} %collective-permute-done.3.refs_3_), channel_id=1, source_target_pairs={{0,2},{1,3},{2,0},{3,1},{4,6},{5,7},{6,4},{7,5},{8,10},{9,11},{10,... | collective-permute-start | bytes 393224 | tf_op jit(solution)/shard_map/ppermute | solution.py:283
  17.4 10.4 %collective-permute-start.8 = (bf16[2,16,16,128]{3,2,1,0:T(8,128)(2,1)S(1)}, bf16[2,16,16,128]{3,2,1,0:T(8,128)(2,1)S(1)}, u32[]{:S(2)}, u32[]{:S(2)}) collective-permute-start(bf16[2,16,16,128]{3,2,1,0:T(8,128)(2,1)S(1)} %collective-permute-done.4.refs_4_), channel_id=1, source_target_pairs={{0,2},{1,3},{2,0},{3,1},{4,6},{5,7},{6,4},{7,5},{8,10},{9,11},{10,... | collective-permute-start | bytes 393224 | tf_op jit(solution)/shard_map/ppermute | solution.py:283
  20.4 7.4 %collective-permute-start.9 = (bf16[2,16,16,128]{3,2,1,0:T(8,128)(2,1)S(1)}, bf16[2,16,16,128]{3,2,1,0:T(8,128)(2,1)S(1)}, u32[]{:S(2)}, u32[]{:S(2)}) collective-permute-start(bf16[2,16,16,128]{3,2,1,0:T(8,128)(2,1)S(1)} %collective-permute-done.5.refs_5_), channel_id=1, source_target_pairs={{0,2},{1,3},{2,0},{3,1},{4,6},{5,7},{6,4},{7,5},{8,10},{9,11},{10,... | collective-permute-start | bytes 393224 | tf_op jit(solution)/shard_map/ppermute | solution.py:283
  20.4 7.5 %copy-start.4 = (bf16[128,128]{1,0:T(8,128)(2,1)S(1)}, bf16[128,128]{1,0:T(8,128)(2,1)}, u32[]{:S(2)}) copy-start(bf16[128,128]{1,0:T(8,128)(2,1)} %refs_13_.1) | copy-start | bytes 98308
  20.4 7.4 %collective-permute-start = (bf16[16,16,128]{2,1,0:T(8,128)(2,1)S(1)}, bf16[16,16,128]{2,1,0:T(8,128)(2,1)S(1)}, u32[]{:S(2)}, u32[]{:S(2)}) collective-permute-start(bf16[16,16,128]{2,1,0:T(8,128)(2,1)S(1)} %copy-done.3), channel_id=1, source_target_pairs={{0,1},{1,0},{2,3},{3,2},{4,5},{5,4},{6,7},{7,6},{8,9},{9,8},{10,11... | collective-permute-start | bytes 196616 | tf_op jit(solution)/shard_map/ppermute | solution.py:283
  25.1 2.7 %copy-start.10 = (f32[128]{0:T(128)S(1)}, f32[128]{0:T(128)}, u32[]{:S(2)}) copy-start(f32[128]{0:T(128)} %param.14) | copy-start | bytes 1540
  27.8 0.7 copy-start.7
  27.8 0.7 %copy-start.9 = (bf16[128,4]{0,1:T(4,128)(2,1)S(1)}, bf16[128,4]{0,1:T(4,128)(2,1)}, u32[]{:S(2)}) copy-start(bf16[128,4]{0,1:T(4,128)(2,1)} %param.18) | copy-start | bytes 3076
  28.5 27.6 %copy-start.2 = (bf16[128,512]{1,0:T(8,128)(2,1)S(1)}, bf16[128,512]{1,0:T(8,128)(2,1)}, u32[]{:S(2)}) copy-start(bf16[128,512]{1,0:T(8,128)(2,1)} %refs_16_.1) | copy-start | bytes 393220
  34.1 23.2 %collective-permute-start.19 = (bf16[16,128,128]{2,1,0:T(8,128)(2,1)S(1)}, bf16[16,128,128]{2,1,0:T(8,128)(2,1)S(1)}, u32[]{:S(2)}, u32[]{:S(2)}) collective-permute-start(bf16[16,128,128]{2,1,0:T(8,128)(2,1)S(1)} %get-tuple-element.17.refs_14_), channel_id=1, source_target_pairs={{0,1},{1,0},{2,3},{3,2},{4,5},{5,4},{6,7},{7,6},{8,9},{9,8},{10,11... | collective-permute-start | bytes 1572872 | tf_op jit(solution)/shard_map/ppermute | solution.py:283
  35.9 12.3 %collective-permute-start.10 = (bf16[4,16,128]{2,1,0:T(8,128)(2,1)S(1)}, bf16[4,16,128]{2,1,0:T(8,128)(2,1)S(1)}, u32[]{:S(2)}, u32[]{:S(2)}) collective-permute-start(bf16[4,16,128]{2,1,0:T(8,128)(2,1)S(1)} %get-tuple-element.16), channel_id=1, source_target_pairs={{0,16},{1,0},{2,18},{3,2},{4,20},{5,4},{6,22},{7,6},{8,24},{9,8},{... | collective-permute-start | bytes 49160 | tf_op jit(solution)/shard_map/ppermute | solution.py:283
  38.0 10.2 %collective-permute-start.11 = (bf16[4,16,128]{2,1,0:T(8,128)(2,1)S(1)}, bf16[4,16,128]{2,1,0:T(8,128)(2,1)S(1)}, u32[]{:S(2)}, u32[]{:S(2)}) collective-permute-start(bf16[4,16,128]{2,1,0:T(8,128)(2,1)S(1)} %get-tuple-element.16), channel_id=1, source_target_pairs={{1,16},{3,18},{5,20},{7,22},{9,24},{11,26},{13,28},{15,30},{16,1},... | collective-permute-start | bytes 49160 | tf_op jit(solution)/shard_map/ppermute | solution.py:283
  48.2 4.0 %collective-permute-start.12 = (bf16[2,4,16,128]{3,2,1,0:T(8,128)(2,1)S(1)}, bf16[2,4,16,128]{3,2,1,0:T(8,128)(2,1)S(1)}, u32[]{:S(2)}, u32[]{:S(2)}) collective-permute-start(bf16[2,4,16,128]{3,2,1,0:T(8,128)(2,1)S(1)} %maximum_select_fusion.1.refs_1_), channel_id=1, source_target_pairs={{0,8},{1,9},{2,10},{3,11},{4,12},{5,13},{6,14},{7,15},{8,0},{9,1},... | collective-permute-start | bytes 98312 | tf_op jit(solution)/shard_map/ppermute | solution.py:283
  49.5 4.7 %collective-permute-start.13 = (bf16[2,4,16,128]{3,2,1,0:T(8,128)(2,1)S(1)}, bf16[2,4,16,128]{3,2,1,0:T(8,128)(2,1)S(1)}, u32[]{:S(2)}, u32[]{:S(2)}) collective-permute-start(bf16[2,4,16,128]{3,2,1,0:T(8,128)(2,1)S(1)} %maximum_select_fusion.1.refs_1_), channel_id=1, source_target_pairs={{0,4},{1,5},{2,6},{3,7},{4,0},{5,1},{6,2},{7,3},{8,12},{9,13},{10,... | collective-permute-start | bytes 98312 | tf_op jit(solution)/shard_map/ppermute | solution.py:283
  52.2 3.9 %collective-permute-start.14 = (bf16[2,4,16,128]{3,2,1,0:T(8,128)(2,1)S(1)}, bf16[2,4,16,128]{3,2,1,0:T(8,128)(2,1)S(1)}, u32[]{:S(2)}, u32[]{:S(2)}) collective-permute-start(bf16[2,4,16,128]{3,2,1,0:T(8,128)(2,1)S(1)} %collective-permute-done.12.refs_2_), channel_id=1, source_target_pairs={{0,4},{1,5},{2,6},{3,7},{4,0},{5,1},{6,2},{7,3},{8,12},{9,13},{10,... | collective-permute-start | bytes 98312 | tf_op jit(solution)/shard_map/ppermute | solution.py:283
  53.7 3.6 %collective-permute-start.15 = (bf16[2,4,16,128]{3,2,1,0:T(8,128)(2,1)S(1)}, bf16[2,4,16,128]{3,2,1,0:T(8,128)(2,1)S(1)}, u32[]{:S(2)}, u32[]{:S(2)}) collective-permute-start(bf16[2,4,16,128]{3,2,1,0:T(8,128)(2,1)S(1)} %maximum_select_fusion.1.refs_1_), channel_id=1, source_target_pairs={{0,2},{1,3},{2,0},{3,1},{4,6},{5,7},{6,4},{7,5},{8,10},{9,11},{10,... | collective-permute-start | bytes 98312 | tf_op jit(solution)/shard_map/ppermute | solution.py:283
  53.7 3.6 %collective-permute-start.16 = (bf16[2,4,16,128]{3,2,1,0:T(8,128)(2,1)S(1)}, bf16[2,4,16,128]{3,2,1,0:T(8,128)(2,1)S(1)}, u32[]{:S(2)}, u32[]{:S(2)}) collective-permute-start(bf16[2,4,16,128]{3,2,1,0:T(8,128)(2,1)S(1)} %collective-permute-done.12.refs_2_), channel_id=1, source_target_pairs={{0,2},{1,3},{2,0},{3,1},{4,6},{5,7},{6,4},{7,5},{8,10},{9,11},{10,... | collective-permute-start | bytes 98312 | tf_op jit(solution)/shard_map/ppermute | solution.py:283
  54.2 3.1 %collective-permute-start.17 = (bf16[2,4,16,128]{3,2,1,0:T(8,128)(2,1)S(1)}, bf16[2,4,16,128]{3,2,1,0:T(8,128)(2,1)S(1)}, u32[]{:S(2)}, u32[]{:S(2)}) collective-permute-start(bf16[2,4,16,128]{3,2,1,0:T(8,128)(2,1)S(1)} %collective-permute-done.13.refs_3_), channel_id=1, source_target_pairs={{0,2},{1,3},{2,0},{3,1},{4,6},{5,7},{6,4},{7,5},{8,10},{9,11},{10,... | collective-permute-start | bytes 98312 | tf_op jit(solution)/shard_map/ppermute | solution.py:283
  56.1 1.2 %collective-permute-start.18 = (bf16[2,4,16,128]{3,2,1,0:T(8,128)(2,1)S(1)}, bf16[2,4,16,128]{3,2,1,0:T(8,128)(2,1)S(1)}, u32[]{:S(2)}, u32[]{:S(2)}) collective-permute-start(bf16[2,4,16,128]{3,2,1,0:T(8,128)(2,1)S(1)} %collective-permute-done.14.refs_4_), channel_id=1, source_target_pairs={{0,2},{1,3},{2,0},{3,1},{4,6},{5,7},{6,4},{7,5},{8,10},{9,11},{10,... | collective-permute-start | bytes 98312 | tf_op jit(solution)/shard_map/ppermute | solution.py:283
  56.1 1.2 %copy-start.5 = (bf16[128,128]{1,0:T(8,128)(2,1)S(1)}, bf16[128,128]{1,0:T(8,128)(2,1)}, u32[]{:S(2)}) copy-start(bf16[128,128]{1,0:T(8,128)(2,1)} %refs_17_.1) | copy-start | bytes 98308
  57.3 0.7 copy-start.8

commit v2 on v1

v2 whole, which is shorter than its diff:
```python
import math

import jax
import jax.numpy as jnp
from jax import lax
from jax.experimental import pallas as pl
from jax.experimental.pallas import tpu as pltpu
from jax.sharding import PartitionSpec as P


CH = 128
H = 4
DH = 32
KCD = 16
SLOT = 64

EPSILON = 1e-05
NEG_SCORE = -1e30
MIB = 1024 * 1024
RESIDENT_LIMIT = 32 * MIB

F32 = jnp.float32
BF16 = jnp.bfloat16


def layer_norm(values, norm_gain):
    centre = values - jnp.mean(values, axis=-1, keepdims=True)
    spread = jnp.mean(centre * centre, axis=-1, keepdims=True)
    return centre * lax.rsqrt(spread + EPSILON) * norm_gain


def sigmoid(values):
    return jax.nn.sigmoid(values)


def unroll_of(count, cols):
    return max(1, min(count, 1024 // cols))


def dot(a, b):
    return jnp.dot(a, b, preferred_element_type=F32)


def dot_nt(a, b):
    return lax.dot_general(a, b, (((1,), (1,)), ((), ())), preferred_element_type=F32)


def call(kernel, out_shape, n_smem, n_in, limit, scratch=(), held_out=True, aliases=None):
    smem = pl.BlockSpec(memory_space=pltpu.SMEM)
    vmem = pl.BlockSpec(memory_space=pltpu.VMEM)
    outs = jax.tree.map(lambda _: vmem, out_shape)
    resident = limit < RESIDENT_LIMIT
    if resident and held_out:
        out_shape = jax.tree.map(lambda o: pltpu.VMEM(o.shape, o.dtype), out_shape)
    run = pl.pallas_call(
        kernel,
        out_shape=out_shape,
        in_specs=[smem] * n_smem + [vmem] * n_in,
        out_specs=outs,
        scratch_shapes=list(scratch),
        input_output_aliases=aliases or {},
        compiler_params=pltpu.CompilerParams(vmem_limit_bytes=limit),
    )

    def apply(*args):
        if not resident:
            return run(*args)
        held = [pltpu.with_memory_space_constraint(a, pltpu.VMEM) for a in args[n_smem:]]
        return run(*args[:n_smem], *held)

    return apply


def make_edge_kernel(cols, n_col, col_of):
    def kernel(len_ref, pair_ref, gain_ref, sum_gain_ref, att_gain_ref, w_ref, *rest):
        left_ref, right_ref, gains_ref, live_ref, scratch_ref, group_ref, proj_ref, sems = rest
        rows, kcd, width = group_ref.shape
        group_copy = pltpu.make_async_copy(pair_ref.at[:, 0:kcd, :], group_ref, sems.at[0])
        proj_copy = pltpu.make_async_copy(w_ref.at[:, 0 : 4 * CH], proj_ref, sems.at[1])
        group_copy.start()
        proj_copy.start()
        row_start = lax.axis_index("row") * rows
        col_start = lax.axis_index("col") * cols
        cells = rows * kcd
        gains_ref[0:1, :] = sum_gain_ref[...]
        gains_ref[1:2, :] = att_gain_ref[...]
        gains_ref[2:3, :] = gain_ref[...]
        chains = cols // SLOT
        lane = lax.broadcasted_iota(jnp.int32, (1, cols), 1)
        for d in range(n_col):
            limit = jnp.zeros((1, cols), jnp.int32)
            for q in range(chains):
                length = len_ref[col_of(d) * chains + q]
                limit = jnp.where(lane // SLOT == q, q * SLOT + length, limit)
            live_ref[:, d * cols : (d + 1) * cols] = jnp.where(lane < limit, 1.0, 0.0).astype(F32)
        group_copy.wait()
        normed = layer_norm(group_ref[...].reshape(cells, width).astype(F32), gain_ref[...])
        proj_copy.wait()
        proj = dot(normed.astype(BF16), proj_ref[...])
        row_len = len_ref[row_start // SLOT]
        row_base = row_start % SLOT
        col_len = len_ref[col_start // SLOT]
        cell = lax.broadcasted_iota(jnp.int32, (cells, width), 0)
        row_live = (cell // kcd + row_base) < row_len
        live = jnp.where(row_live & (cell % kcd < col_len), 1.0, 0.0).astype(F32)
        right = sigmoid(proj[:, 2 * CH : 3 * CH]) * proj[:, 3 * CH : 4 * CH] * live
        scratch_ref[...] = right
        for k in range(kcd):
            right_ref[k] = scratch_ref[pl.ds(k, rows, stride=kcd), :].astype(BF16)
        left = sigmoid(proj[:, :CH]) * proj[:, CH : 2 * CH] * live
        left_ref[...] = left.astype(BF16).reshape(rows, kcd, width)

    return kernel


def gate_kernel(pair_ref, gains_ref, w_ref, out_ref):
    rows, cols, width = pair_ref.shape
    step = 2

    def body(t, carry):
        at = pl.ds(t * step, step)
        x = pair_ref[at].reshape(step * cols, width).astype(F32)
        normed = layer_norm(x, gains_ref[2:3, :]).astype(BF16)
        out_ref[at] = sigmoid(dot(normed, w_ref[:, 4 * CH :])).reshape(step, cols, width)
        return carry

    lax.fori_loop(0, rows // step, body, 0, unroll=unroll_of(rows // step, cols))


def add_sums(left_ref, lefts, rights, sum_ref, places):
    rows = sum_ref.shape[0]
    kcd, width = lefts[0].shape[1:]
    blk = rights[0].shape[2]
    group = 8
    for d, left in enumerate(lefts):
        left_ref[d] = left[...].reshape(rows * kcd, width).astype(F32)
    for right_ref, place in zip(rights, places):
        first = pl.multiple_of(place * blk, blk)

        def sums(g, carry, right_ref=right_ref, first=first):
            acc = [jnp.zeros((blk, width), F32) for _ in range(group)]
            for d in range(len(lefts)):
                for k in range(kcd):
                    right = right_ref[d, k].astype(F32)
                    for u in range(group):
                        left = left_ref[d, pl.ds((g * group + u) * kcd + k, 1), :]
                        acc[u] = acc[u] + left * right
            for u in range(group):
                sum_ref[g * group + u, pl.ds(first, blk), :] = acc[u]
            return carry

        lax.fori_loop(0, rows // group, sums, 0)


def make_sum_kernel(n_col, blocks, place):
    def kernel(*refs):
        lefts = refs[:n_col]
        rights = refs[n_col : n_col + len(blocks)]
        sum_ref, left_ref = refs[-2:]
        add_sums(left_ref, lefts, rights, sum_ref, [place(s) for s in blocks])

    return kernel


def make_tri_kernel(n_col, blocks, place):
    def kernel(*refs):
        lefts = refs[:n_col]
        rights = refs[n_col : n_col + len(blocks)]
        pair_ref, gate_ref, gains_ref, w_ref, bias_w_ref = refs[
            n_col + len(blocks) : n_col + len(blocks) + 5
        ]
        mid_ref, norm_ref, bias_ref, sum_ref, left_ref, bias_scr = refs[-6:]
        rows, cols, width = pair_ref.shape
        add_sums(left_ref, lefts, rights, sum_ref, [place(s) for s in blocks])
        step = 2

        def finish(t, carry):
            at = pl.ds(t * step, step)
            total = sum_ref[at].reshape(step * cols, width)
            normed = layer_norm(total, gains_ref[0:1, :]).astype(BF16)
            update = dot(normed, w_ref[...])
            pair = pair_ref[at].reshape(step * cols, width).astype(F32)
            gate = gate_ref[at].reshape(step * cols, width)
            mid = (pair + gate * update).astype(BF16)
            mid_ref[at] = mid.reshape(step, cols, width)
            att = layer_norm(mid.astype(F32), gains_ref[1:2, :]).astype(BF16)
            norm_ref[at] = att.reshape(step, cols, width)
            bias = dot_nt(bias_w_ref[...], att)
            for u in range(step):
                bias_scr[t * step + u] = bias[:, u * cols : (u + 1) * cols]
            return carry

        lax.fori_loop(0, rows // step, finish, 0, unroll=unroll_of(rows // step, cols))
        for h in range(H):
            bias_ref[h] = bias_scr[:, h, :].astype(BF16)

    return kernel


def project_kernel(norm_ref, w_ref, q_ref, k_ref, v_ref, gate_ref):
    rows, cols, width = norm_ref.shape
    step = 2

    def body(t, carry):
        at = pl.ds(t * step, step)
        out = dot(norm_ref[at].reshape(step * cols, width), w_ref[...])
        shape = (step, cols, width)
        q_ref[at] = out[:, :width].astype(BF16).reshape(shape)
        k_ref[at] = out[:, width : 2 * width].astype(BF16).reshape(shape)
        v_ref[at] = out[:, 2 * width : 3 * width].astype(BF16).reshape(shape)
        gate_ref[at] = sigmoid(out[:, 3 * width :]).reshape(shape)
        return carry

    lax.fori_loop(0, rows // step, body, 0, unroll=unroll_of(rows // step, cols))


def make_attend_kernel(n_col, n_blk, place):
    def kernel(*refs):
        biases = refs[:n_blk]
        others = refs[n_blk : n_blk + n_col - 1]
        q_ref, k_ref, v_ref, gate_ref, mid_ref, gains_ref, live_ref, kv_w_ref, out_w_ref = refs[
            n_blk + n_col - 1 : n_blk + n_col + 8
        ]
        out_ref, bias_ref, keys_ref, values_ref = refs[n_blk + n_col + 8 :]
        rows, cols, width = q_ref.shape
        blk = biases[0].shape[2]
        for d in range(n_col):
            live = jnp.broadcast_to(live_ref[:, d * cols : (d + 1) * cols], (blk, cols)) > 0.5
            for s in range(n_blk):
                first = place(s) * blk
                for h in range(H):
                    at = pl.multiple_of(h * cols + first, blk)
                    value = biases[s][d, h].astype(F32)
                    bias_ref[pl.ds(at, blk), d * cols : (d + 1) * cols] = jnp.where(
                        live, value, NEG_SCORE
                    )
        head = lax.broadcasted_iota(jnp.int32, (cols, width), 1) // DH
        scale = 1.0 / math.sqrt(DH)
        ones = jnp.ones((n_col * cols, width), BF16)

        step = 2

        def spread(t, carry):
            at = pl.ds(t * step, step)
            keys_ref[at, 0:cols] = k_ref[at]
            values_ref[at, 0:cols] = v_ref[at]
            for d in range(n_col - 1):
                there = others[d][at].reshape(step * cols, width).astype(F32)
                normed = layer_norm(there, gains_ref[1:2, :]).astype(BF16)
                kv = dot(normed, kv_w_ref[:, width : 3 * width]).astype(BF16)
                low = (d + 1) * cols
                keys_ref[at, low : low + cols] = kv[:, :width].reshape(step, cols, width)
                values_ref[at, low : low + cols] = kv[:, width:].reshape(step, cols, width)
            return carry

        lax.fori_loop(0, rows // step, spread, 0, unroll=unroll_of(rows // step, cols))

        def attend(i, carry):
            key = keys_ref[i]
            value = jnp.concatenate([values_ref[i], ones], axis=1)
            query = q_ref[i]
            stack = jnp.concatenate(
                [jnp.where(head == h, query, jnp.zeros_like(query)) for h in range(H)], axis=0
            )
            scores = dot_nt(stack, key) * scale + bias_ref[...]
            top = jnp.max(scores, axis=-1, keepdims=True)
            weights = jnp.exp(scores - top).astype(BF16)
            both = dot(weights, value)
            summed = both[:cols, :width]
            totals = both[:cols, width:]
            for h in range(1, H):
                mine = head == h
                part = both[h * cols : (h + 1) * cols]
                summed = jnp.where(mine, part[:, :width], summed)
                totals = jnp.where(mine, part[:, width:], totals)
            out_ref[i] = (summed / totals * gate_ref[i]).astype(BF16)
            return carry

        lax.fori_loop(0, rows, attend, 0, unroll=max(1, min(rows, 2**18 // (cols * n_col * cols))))

        def finish(t, carry):
            at = pl.ds(t * step, step)
            attended = out_ref[at].reshape(step * cols, width)
            new = mid_ref[at].reshape(step * cols, width).astype(F32) + dot(attended, out_w_ref[...])
            out_ref[at] = new.astype(BF16).reshape(step, cols, width)
            return carry

        lax.fori_loop(0, rows // step, finish, 0, unroll=unroll_of(rows // step, cols))

    return kernel


class Grid:
    def __init__(self, n_row, n_col):
        self.n_row = n_row
        self.n_col = n_col
        self.n_blk = n_row // n_col
        self.fast = n_col == 2 and n_row & (n_row - 1) == 0
        self.offsets = [0]
        if self.fast:
            bit = self.n_blk // 2
            while bit:
                self.offsets = self.offsets + [o ^ bit for o in self.offsets]
                bit //= 2

    def groups(self):
        if not self.fast or self.n_blk < 8:
            return [], list(range(self.n_blk))
        half = self.n_blk // 2
        parts = [range(half // 2), range(half // 2, half - 1), range(half - 1, half)]
        groups = [[t for s in part for t in (s, s + half)] for part in parts]
        return groups[:-1], groups[-1]

    def place(self, s):
        if self.fast:
            return (lax.axis_index("row") & (self.n_blk - 1)) ^ self.offsets[s]
        return s

    def col_of(self, d):
        return (lax.axis_index("col") + d) % self.n_col

    def move(self, value, target):
        pairs = []
        for r in range(self.n_row):
            for c in range(self.n_col):
                to = target(r, c)
                if to is not None:
                    pairs.append((r * self.n_col + c, to[0] * self.n_col + to[1]))
        return lax.ppermute(value, ("row", "col"), pairs)

    def shift_col(self, value, d):
        return self.move(value, lambda r, c: (r, (c - d) % self.n_col))

    def flip_row(self, value, bit):
        return self.move(value, lambda r, c: (r ^ bit, c))

    def gather(self, own):
        if not self.fast:
            stacked = lax.all_gather(own, "row", axis=0)
            stacked = lax.all_to_all(stacked, "col", split_axis=0, concat_axis=0, tiled=True)
            stacked = stacked.reshape((self.n_col, self.n_blk) + own.shape)
            order = (lax.axis_index("col") + jnp.arange(self.n_col)) % self.n_col
            stacked = jnp.take(stacked, order, axis=0)
            return [stacked[:, s] for s in range(self.n_blk)]
        half = self.n_row // 2
        same = lax.axis_index("row") // half == lax.axis_index("col")

        def first(r, c):
            return (r ^ half, c) if r // half == c else (r, 1 - c)

        def second(r, c):
            return None if r // half == c else (r ^ half, 1 - c)

        near = self.move(own, first)
        far = self.move(own, second)
        pair = jnp.where(same, jnp.stack([own, near]), jnp.stack([near, far]))
        blocks = [pair]
        bit = self.n_blk // 2
        while bit:
            moved = []
            for block in blocks:
                moved.append(self.flip_row(block, bit))
            blocks = blocks + moved
            bit //= 2
        return blocks


def make_body(grid):
    def body(
        pair_rep, chain_len, tri_gain, tri_in, sum_gain, tri_out, att_gain, att_in, att_bias, att_out
    ):
        rows, cols, width = pair_rep.shape
        n_col, n_blk = grid.n_col, grid.n_blk
        whole = (rows, cols, width)
        limit = min(60 * MIB, 12 * MIB + 24 * H * cols * n_col * cols * 4)
        tri_gain = tri_gain.reshape(1, width)
        sum_gain = sum_gain.reshape(1, width)
        att_gain = att_gain.reshape(1, width)

        anywhere = pl.BlockSpec(memory_space=pl.ANY)
        small = pl.BlockSpec(memory_space=pltpu.VMEM)
        held = limit < RESIDENT_LIMIT
        shape = pltpu.VMEM if held else jax.ShapeDtypeStruct
        left, right, gains, live = pl.pallas_call(
            make_edge_kernel(cols, n_col, grid.col_of),
            name="edges",
            out_shape=(
                shape((rows, KCD, width), BF16),
                shape((KCD, rows, width), BF16),
                shape((3, width), F32),
                shape((1, n_col * cols), F32),
            ),
            in_specs=[
                pl.BlockSpec(memory_space=pltpu.SMEM),
                anywhere,
                small,
                small,
                small,
                anywhere,
            ],
            out_specs=(small, small, small, small),
            scratch_shapes=[
                pltpu.VMEM((rows * KCD, width), F32),
                pltpu.VMEM((rows, KCD, width), BF16),
                pltpu.VMEM((width, 4 * CH), BF16),
                pltpu.SemaphoreType.DMA((2,)),
            ],
        )(chain_len, pair_rep, tri_gain, sum_gain, att_gain, tri_in)
        rights = grid.gather(right)
        lefts = [left] + [grid.shift_col(left, d) for d in range(1, n_col)]
        gate = call(gate_kernel, jax.ShapeDtypeStruct(whole, F32), 0, 3, limit)(
            pair_rep, gains, tri_in
        )
        early, last = grid.groups()
        left_scr = pltpu.VMEM((n_col, rows * KCD, width), F32)
        sums = []
        for blocks in early:
            sums = [
                call(
                    make_sum_kernel(n_col, blocks, grid.place),
                    jax.ShapeDtypeStruct(whole, F32),
                    0,
                    n_col + len(blocks) + len(sums),
                    limit,
                    [left_scr],
                    aliases={n_col + len(blocks): 0} if sums else {},
                )(*lefts, *[rights[s] for s in blocks], *sums)
            ]
        mid, normed, bias, _ = call(
            make_tri_kernel(n_col, last, grid.place),
            (
                jax.ShapeDtypeStruct(whole, BF16),
                jax.ShapeDtypeStruct(whole, BF16),
                jax.ShapeDtypeStruct((H, rows, cols), BF16),
                jax.ShapeDtypeStruct(whole, F32),
            ),
            0,
            n_col + len(last) + 5 + len(sums),
            limit,
            [left_scr, pltpu.VMEM((rows, H, cols), F32)],
            aliases={n_col + len(last) + 5: 3} if sums else {},
        )(*lefts, *[rights[s] for s in last], pair_rep, gate, gains, tri_out, att_bias.T, *sums)
        biases = grid.gather(bias)
        others = [grid.shift_col(mid, d) for d in range(1, n_col)]
        wide = jax.ShapeDtypeStruct(whole, BF16)
        query, key, value, att_gate = call(
            project_kernel, (wide, wide, wide, jax.ShapeDtypeStruct(whole, F32)), 0, 2, limit
        )(normed, att_in)
        return call(
            make_attend_kernel(n_col, n_blk, grid.place),
            wide,
            0,
            n_blk + n_col - 1 + 9,
            limit,
            [
                pltpu.VMEM((H * cols, n_col * cols), F32),
                pltpu.VMEM((rows, n_col * cols, width), BF16),
                pltpu.VMEM((rows, n_col * cols, width), BF16),
            ],
            held_out=False,
        )(
            *biases,
            *others,
            query,
            key,
            value,
            att_gate,
            mid,
            gains,
            live,
            att_in,
            att_out,
        )

    return body


def solution(mesh):
    grid = Grid(mesh.shape["row"], mesh.shape["col"])
    placed = (P("row", "col", None), P(), P(), P(), P(), P(), P(), P(), P(), P())
    return jax.shard_map(
        make_body(grid), mesh=mesh, in_specs=placed, out_specs=P("row", "col", None), check_vma=False
    )
```

time: 67.9 us -> 61.6 us (0.907)
  Pallas kernels: 19.9 us -> 13.3 us
  starting transfers between devices: 24.7 us -> 27.4 us
  other arithmetic: 0.91 us -> 0.03 us
  waiting for transfers between devices: 20.6 us -> 19.9 us
    pallas_call x4 -> x6, Pallas kernels: 17.9 us -> 11.1 us  [apply(): return run(*args[:n_smem], *held)]
    ppermute x20, starting transfers between devices: 24.7 us -> 27.4 us  [move(): return lax.ppermute(value, ('row', 'col'), pairs)]
    select_n x2, other arithmetic: 0.91 us -> 0.03 us  [gather(): pair = jnp.where(same, jnp.stack([own, near]), jnp.stack([near, far]))]
    ppermute x20, waiting for transfers between devices: 20.6 us -> 19.9 us  [move(): return lax.ppermute(value, ('row', 'col'), pairs)]
  transfers between devices with their start and end apart: 20 -> 20, of which waited for: 7 -> 9; matrix products, arithmetic and copies ran while one was open for 0% -> 0% of each run, Pallas kernels for 4% -> 6%
where the time goes in v2:
time: 61.6 us; the launch traced here: 61.4 us
  starting transfers between devices  27.4 us (44%)
  waiting for transfers between devices  19.9 us (32%)
  Pallas kernels  13.3 us (22%)
  local copies, waits for them, and re-layouts  0.68 us (1%)
    ppermute x20, starting transfers between devices, move(): return lax.ppermute(value, ('row', 'col'), pairs)  27.4 us
    ppermute x20, waiting for transfers between devices, move(): return lax.ppermute(value, ('row', 'col'), pairs)  19.9 us
    pallas_call x6, Pallas kernels, apply(): return run(*args[:n_smem], *held)  11.1 us
    pallas_call x1, Pallas kernels, body(): pl.pallas_call(make_edge_kernel(cols, n_col, grid.col_of), name='edges',...  2.11 us
  transfers between devices with their start and end apart: 20, of which 9 were waited for; matrix products, arithmetic and copies ran while one was open for 0% of the time, Pallas kernels for 6%

profile of v2, /device:TPU:0, one launch (start us, length us, event | category | flops | bytes accessed | tf_op | source)
XLA Modules:
  0.0 61.4 jit_solution(331967715811514597)
XLA Ops:
  0.0 2.1 %edges.1 = (bf16[16,16,128]{2,1,0:T(8,128)(2,1)S(1)}, bf16[16,16,128]{2,1,0:T(8,128)(2,1)S(1)}, f32[3,128]{1,0:T(4,128)S(1)}, f32[1,256]{1,0:T(1,128)S(1)}) custom-call(s32[4]{0:T(128)} %len_ref.1, bf16[16,128,128]{2,1,0:T(8,128)(2,1)} %refs_4_.1, f32[1,128]{1,0:T(1,128)} %bitcast.17, f32[1,128]{1,0:T(1,128)} %bitcast.18, f32[1,128]{1,0:T(1,128)} %bitcast.19, ...), custom_call_target="tpu_custom_call" | custom-call | tf_op jit(solution)/shard_map/edges/pallas_call | solution.py:384
  2.1 0.7 %collective-permute-start.2 = (bf16[16,16,128]{2,1,0:T(8,128)(2,1)S(1)}, bf16[16,16,128]{2,1,0:T(8,128)(2,1)S(1)}, u32[]{:S(2)}, u32[]{:S(2)}) collective-permute-start(bf16[16,16,128]{2,1,0:T(8,128)(2,1)S(1)} %get-tuple-element.17), channel_id=1, source_target_pairs={{1,16},{3,18},{5,20},{7,22},{9,24},{11,26},{13,28},{15,30},{16,1},... | collective-permute-start | bytes 196616 | tf_op jit(solution)/shard_map/ppermute | solution.py:329
  2.8 6.6 %collective-permute-start.1 = (bf16[16,16,128]{2,1,0:T(8,128)(2,1)S(1)}, bf16[16,16,128]{2,1,0:T(8,128)(2,1)S(1)}, u32[]{:S(2)}, u32[]{:S(2)}) collective-permute-start(bf16[16,16,128]{2,1,0:T(8,128)(2,1)S(1)} %get-tuple-element.17), channel_id=1, source_target_pairs={{0,16},{1,0},{2,18},{3,2},{4,20},{5,4},{6,22},{7,6},{8,24},{9,8},{... | collective-permute-start | bytes 196616 | tf_op jit(solution)/shard_map/ppermute | solution.py:329
  9.4 0.0 collective-permute-done.2
  9.4 2.4 %collective-permute-done.1 = bf16[16,16,128]{2,1,0:T(8,128)(2,1)S(1)} collective-permute-done((bf16[16,16,128]{2,1,0:T(8,128)(2,1)S(1)}, bf16[16,16,128]{2,1,0:T(8,128)(2,1)S(1)}, u32[]{:S(2)}, u32[]{:S(2)}) %collective-permute-start.1) | collective-permute-done | bytes 65568 | tf_op jit(solution)/shard_map/ppermute | solution.py:329
  11.9 1.6 %collective-permute-start.3 = (bf16[2,16,16,128]{3,2,1,0:T(8,128)(2,1)S(1)}, bf16[2,16,16,128]{3,2,1,0:T(8,128)(2,1)S(1)}, u32[]{:S(2)}, u32[]{:S(2)}) collective-permute-start(bf16[2,16,16,128]{3,2,1,0:T(8,128)(2,1)S(1)} %maximum_select_fusion.refs_2_), channel_id=1, source_target_pairs={{0,8},{1,9},{2,10},{3,11},{4,12},{5,13},{6,14},{7,15},{8,0},{9,1},... | collective-permute-start | bytes 393224 | tf_op jit(solution)/shard_map/ppermute | solution.py:329
  13.5 1.5 %collective-permute-start.6 = (bf16[2,16,16,128]{3,2,1,0:T(8,128)(2,1)S(1)}, bf16[2,16,16,128]{3,2,1,0:T(8,128)(2,1)S(1)}, u32[]{:S(2)}, u32[]{:S(2)}) collective-permute-start(bf16[2,16,16,128]{3,2,1,0:T(8,128)(2,1)S(1)} %maximum_select_fusion.refs_2_), channel_id=1, source_target_pairs={{0,4},{1,5},{2,6},{3,7},{4,0},{5,1},{6,2},{7,3},{8,12},{9,13},{10,... | collective-permute-start | bytes 393224 | tf_op jit(solution)/shard_map/ppermute | solution.py:329
  15.0 1.9 %collective-permute-done.3.refs_4_ = bf16[2,16,16,128]{3,2,1,0:T(8,128)(2,1)S(1)} collective-permute-done((bf16[2,16,16,128]{3,2,1,0:T(8,128)(2,1)S(1)}, bf16[2,16,16,128]{3,2,1,0:T(8,128)(2,1)S(1)}, u32[]{:S(2)}, u32[]{:S(2)}) %collective-permute-start.3) | collective-permute-done | bytes 131104 | tf_op jit(solution)/shard_map/ppermute | solution.py:329
  16.9 1.5 %collective-permute-start.4 = (bf16[2,16,16,128]{3,2,1,0:T(8,128)(2,1)S(1)}, bf16[2,16,16,128]{3,2,1,0:T(8,128)(2,1)S(1)}, u32[]{:S(2)}, u32[]{:S(2)}) collective-permute-start(bf16[2,16,16,128]{3,2,1,0:T(8,128)(2,1)S(1)} %collective-permute-done.3.refs_4_), channel_id=1, source_target_pairs={{0,4},{1,5},{2,6},{3,7},{4,0},{5,1},{6,2},{7,3},{8,12},{9,13},{10,... | collective-permute-start | bytes 393224 | tf_op jit(solution)/shard_map/ppermute | solution.py:329
  18.4 0.0 collective-permute-start.8
  18.4 0.5 collective-permute-start.9
  18.9 0.9 %collective-permute-done.6.refs_2_ = bf16[2,16,16,128]{3,2,1,0:T(8,128)(2,1)S(1)} collective-permute-done((bf16[2,16,16,128]{3,2,1,0:T(8,128)(2,1)S(1)}, bf16[2,16,16,128]{3,2,1,0:T(8,128)(2,1)S(1)}, u32[]{:S(2)}, u32[]{:S(2)}) %collective-permute-start.6) | collective-permute-done | bytes 131104 | tf_op jit(solution)/shard_map/ppermute | solution.py:329
  19.9 0.0 collective-permute-start.7
  19.9 2.0 %collective-permute-done.4.refs_2_ = bf16[2,16,16,128]{3,2,1,0:T(8,128)(2,1)S(1)} collective-permute-done((bf16[2,16,16,128]{3,2,1,0:T(8,128)(2,1)S(1)}, bf16[2,16,16,128]{3,2,1,0:T(8,128)(2,1)S(1)}, u32[]{:S(2)}, u32[]{:S(2)}) %collective-permute-start.4) | collective-permute-done | bytes 131104 | tf_op jit(solution)/shard_map/ppermute | solution.py:329
  21.9 0.0 collective-permute-start.5
  21.9 3.2 %collective-permute-start = (bf16[16,16,128]{2,1,0:T(8,128)(2,1)S(1)}, bf16[16,16,128]{2,1,0:T(8,128)(2,1)S(1)}, u32[]{:S(2)}, u32[]{:S(2)}) collective-permute-start(bf16[16,16,128]{2,1,0:T(8,128)(2,1)S(1)} %get-tuple-element.16.refs_0_), channel_id=1, source_target_pairs={{0,1},{1,0},{2,3},{3,2},{4,5},{5,4},{6,7},{7,6},{8,9},{9,8},{10,11... | collective-permute-start | bytes 196616 | tf_op jit(solution)/shard_map/ppermute | solution.py:329
  25.1 0.9 %shard_map.100.refs_5_ = f32[16,128,128]{2,1,0:T(8,128)S(1)} custom-call(bf16[16,128,128]{2,1,0:T(8,128)(2,1)S(1)} %copy-done, f32[3,128]{1,0:T(4,128)S(1)} %get-tuple-element.18.gains_ref.refs_6_.refs_14_, bf16[128,640]{1,0:T(8,128)(2,1)S(1)} %copy-done.1), custom_call_target="tpu_custom_call" | custom-call | tf_op jit(solution)/shard_map/pallas_call | solution.py:69
  26.1 1.8 %collective-permute-done.refs_1_ = bf16[16,16,128]{2,1,0:T(8,128)(2,1)S(1)} collective-permute-done((bf16[16,16,128]{2,1,0:T(8,128)(2,1)S(1)}, bf16[16,16,128]{2,1,0:T(8,128)(2,1)S(1)}, u32[]{:S(2)}, u32[]{:S(2)}) %collective-permute-start) | collective-permute-done | bytes 65568 | tf_op jit(solution)/shard_map/ppermute | solution.py:329
  27.9 0.0 collective-permute-done.8.refs_3_
  27.9 0.0 collective-permute-done.9.refs_5_
  27.9 1.3 %shard_map.101.refs_4_ = f32[16,128,128]{2,1,0:T(8,128)S(1)} custom-call(bf16[16,16,128]{2,1,0:T(8,128)(2,1)S(1)} %get-tuple-element.16.refs_0_, bf16[16,16,128]{2,1,0:T(8,128)(2,1)S(1)} %collective-permute-done.refs_1_, bf16[2,16,16,128]{3,2,1,0:T(8,128)(2,1)S(1)} %maximum_select_fusion.refs_2_, ...), custom_call_target="tpu_custom_call" | custom-call | tf_op jit(solution)/shard_map/pallas_call | solution.py:69
  29.2 0.0 copy-start.3
  29.2 0.0 collective-permute-done.7.refs_3_
  29.2 0.7 %shard_map.102.refs_9_ = f32[16,128,128]{2,1,0:T(8,128)S(1)} custom-call(bf16[16,16,128]{2,1,0:T(8,128)(2,1)S(1)} %get-tuple-element.16.refs_0_, bf16[16,16,128]{2,1,0:T(8,128)(2,1)S(1)} %collective-permute-done.refs_1_, bf16[2,16,16,128]{3,2,1,0:T(8,128)(2,1)S(1)} %collective-permute-done.6.refs_2_, ...), custom_call_target="tpu_custom_call", output_to_operand_aliasing={{}: (4, {})} | custom-call | tf_op jit(solution)/shard_map/pallas_call | solution.py:69
  29.9 0.0 collective-permute-done.5.refs_3_
  29.9 0.0 copy-done.3
  30.0 0.6 %copy-done.5 = bf16[128,4]{0,1:T(4,128)(2,1)S(1)} copy-done((bf16[128,4]{0,1:T(4,128)(2,1)S(1)}, bf16[128,4]{0,1:T(4,128)(2,1)}, u32[]{:S(2)}) %copy-start.5) | copy-done | bytes 1048
  30.6 2.5 %shard_map.103 = (bf16[16,128,128]{2,1,0:T(8,128)(2,1)S(1)}, bf16[16,128,128]{2,1,0:T(8,128)(2,1)S(1)}, bf16[4,16,128]{2,1,0:T(8,128)(2,1)S(1)}, f32[16,128,128]{2,1,0:T(8,128)S(1)}) custom-call(bf16[16,16,128]{2,1,0:T(8,128)(2,1)S(1)} %get-tuple-element.16.refs_0_, ...), custom_call_target="tpu_custom_call", output_to_operand_aliasing={{3}: (9, {})} | custom-call | tf_op jit(solution)/shard_map/pallas_call | solution.py:69
  33.1 1.8 %collective-permute-start.19 = (bf16[16,128,128]{2,1,0:T(8,128)(2,1)S(1)}, bf16[16,128,128]{2,1,0:T(8,128)(2,1)S(1)}, u32[]{:S(2)}, u32[]{:S(2)}) collective-permute-start(bf16[16,128,128]{2,1,0:T(8,128)(2,1)S(1)} %get-tuple-element.20.refs_13_), channel_id=1, source_target_pairs={{0,1},{1,0},{2,3},{3,2},{4,5},{5,4},{6,7},{7,6},{8,9},{9,8},{10,11... | collective-permute-start | bytes 1572872 | tf_op jit(solution)/shard_map/ppermute | solution.py:329
  34.9 0.7 %collective-permute-start.11 = (bf16[4,16,128]{2,1,0:T(8,128)(2,1)S(1)}, bf16[4,16,128]{2,1,0:T(8,128)(2,1)S(1)}, u32[]{:S(2)}, u32[]{:S(2)}) collective-permute-start(bf16[4,16,128]{2,1,0:T(8,128)(2,1)S(1)} %get-tuple-element.19), channel_id=1, source_target_pairs={{1,16},{3,18},{5,20},{7,22},{9,24},{11,26},{13,28},{15,30},{16,1},... | collective-permute-start | bytes 49160 | tf_op jit(solution)/shard_map/ppermute | solution.py:329
  35.5 3.9 %collective-permute-start.10 = (bf16[4,16,128]{2,1,0:T(8,128)(2,1)S(1)}, bf16[4,16,128]{2,1,0:T(8,128)(2,1)S(1)}, u32[]{:S(2)}, u32[]{:S(2)}) collective-permute-start(bf16[4,16,128]{2,1,0:T(8,128)(2,1)S(1)} %get-tuple-element.19), channel_id=1, source_target_pairs={{0,16},{1,0},{2,18},{3,2},{4,20},{5,4},{6,22},{7,6},{8,24},{9,8},{... | collective-permute-start | bytes 49160 | tf_op jit(solution)/shard_map/ppermute | solution.py:329
  39.5 0.0 collective-permute-done.11
  39.5 7.8 %collective-permute-done.10 = bf16[4,16,128]{2,1,0:T(8,128)(2,1)S(1)} collective-permute-done((bf16[4,16,128]{2,1,0:T(8,128)(2,1)S(1)}, bf16[4,16,128]{2,1,0:T(8,128)(2,1)S(1)}, u32[]{:S(2)}, u32[]{:S(2)}) %collective-permute-start.10) | collective-permute-done | bytes 16416 | tf_op jit(solution)/shard_map/ppermute | solution.py:329
  47.2 1.9 %collective-permute-start.12 = (bf16[2,4,16,128]{3,2,1,0:T(8,128)(2,1)S(1)}, bf16[2,4,16,128]{3,2,1,0:T(8,128)(2,1)S(1)}, u32[]{:S(2)}, u32[]{:S(2)}) collective-permute-start(bf16[2,4,16,128]{3,2,1,0:T(8,128)(2,1)S(1)} %maximum_select_fusion.1.refs_0_), channel_id=1, source_target_pairs={{0,8},{1,9},{2,10},{3,11},{4,12},{5,13},{6,14},{7,15},{8,0},{9,1},... | collective-permute-start | bytes 98312 | tf_op jit(solution)/shard_map/ppermute | solution.py:329
  49.1 1.5 %collective-permute-start.13 = (bf16[2,4,16,128]{3,2,1,0:T(8,128)(2,1)S(1)}, bf16[2,4,16,128]{3,2,1,0:T(8,128)(2,1)S(1)}, u32[]{:S(2)}, u32[]{:S(2)}) collective-permute-start(bf16[2,4,16,128]{3,2,1,0:T(8,128)(2,1)S(1)} %maximum_select_fusion.1.refs_0_), channel_id=1, source_target_pairs={{0,4},{1,5},{2,6},{3,7},{4,0},{5,1},{6,2},{7,3},{8,12},{9,13},{10,... | collective-permute-start | bytes 98312 | tf_op jit(solution)/shard_map/ppermute | solution.py:329
  50.6 0.6 %collective-permute-done.12.refs_1_ = bf16[2,4,16,128]{3,2,1,0:T(8,128)(2,1)S(1)} collective-permute-done((bf16[2,4,16,128]{3,2,1,0:T(8,128)(2,1)S(1)}, bf16[2,4,16,128]{3,2,1,0:T(8,128)(2,1)S(1)}, u32[]{:S(2)}, u32[]{:S(2)}) %collective-permute-start.12) | collective-permute-done | bytes 32800 | tf_op jit(solution)/shard_map/ppermute | solution.py:329
  51.2 1.5 %collective-permute-start.14 = (bf16[2,4,16,128]{3,2,1,0:T(8,128)(2,1)S(1)}, bf16[2,4,16,128]{3,2,1,0:T(8,128)(2,1)S(1)}, u32[]{:S(2)}, u32[]{:S(2)}) collective-permute-start(bf16[2,4,16,128]{3,2,1,0:T(8,128)(2,1)S(1)} %collective-permute-done.12.refs_1_), channel_id=1, source_target_pairs={{0,4},{1,5},{2,6},{3,7},{4,0},{5,1},{6,2},{7,3},{8,12},{9,13},{10,... | collective-permute-start | bytes 98312 | tf_op jit(solution)/shard_map/ppermute | solution.py:329
  52.7 0.0 collective-permute-start.15
  52.7 0.5 collective-permute-start.16
  53.2 0.0 collective-permute-done.13.refs_2_
  53.2 0.0 collective-permute-start.17
  53.2 1.9 %collective-permute-done.14.refs_3_ = bf16[2,4,16,128]{3,2,1,0:T(8,128)(2,1)S(1)} collective-permute-done((bf16[2,4,16,128]{3,2,1,0:T(8,128)(2,1)S(1)}, bf16[2,4,16,128]{3,2,1,0:T(8,128)(2,1)S(1)}, u32[]{:S(2)}, u32[]{:S(2)}) %collective-permute-start.14) | collective-permute-done | bytes 32800 | tf_op jit(solution)/shard_map/ppermute | solution.py:329
  55.1 0.0 collective-permute-start.18
  55.1 0.7 %shard_map.104 = (bf16[16,128,128]{2,1,0:T(8,128)(2,1)S(1)}, bf16[16,128,128]{2,1,0:T(8,128)(2,1)S(1)}, bf16[16,128,128]{2,1,0:T(8,128)(2,1)S(1)}, f32[16,128,128]{2,1,0:T(8,128)S(1)}) custom-call(bf16[16,128,128]{2,1,0:T(8,128)(2,1)S(1)} %get-tuple-element.21.norm_ref, bf16[128,512]{1,0:T(8,128)(2,1)S(1)} %copy-done.2), custom_call_target="tpu_custom_call" | custom-call | tf_op jit(solution)/shard_map/pallas_call | solution.py:69
  55.9 0.0 collective-permute-done.17.refs_6_
  55.9 0.0 collective-permute-done.16.refs_5_
  55.9 0.5 collective-permute-done.18.refs_7_
  56.4 5.0 %shard_map.105 = bf16[16,128,128]{2,1,0:T(8,128)(2,1)} custom-call(bf16[2,4,16,128]{3,2,1,0:T(8,128)(2,1)S(1)} %maximum_select_fusion.1.refs_0_, bf16[2,4,16,128]{3,2,1,0:T(8,128)(2,1)S(1)} %collective-permute-done.12.refs_1_, bf16[2,4,16,128]{3,2,1,0:T(8,128)(2,1)S(1)} %collective-permute-done.13.refs_2_, ...), custom_call_target="tpu_custom_call" | custom-call | tf_op jit(solution)/shard_map/pallas_call | solution.py:69
  (13 shorter events, 0.0 us)
Async XLA Ops:
  0.0 25.1 %copy-start = (bf16[16,128,128]{2,1,0:T(8,128)(2,1)S(1)}, bf16[16,128,128]{2,1,0:T(8,128)(2,1)}, u32[]{:S(2)}) copy-start(bf16[16,128,128]{2,1,0:T(8,128)(2,1)} %refs_4_.1) | copy-start | bytes 1572868
  2.1 7.3 %collective-permute-start.2 = (bf16[16,16,128]{2,1,0:T(8,128)(2,1)S(1)}, bf16[16,16,128]{2,1,0:T(8,128)(2,1)S(1)}, u32[]{:S(2)}, u32[]{:S(2)}) collective-permute-start(bf16[16,16,128]{2,1,0:T(8,128)(2,1)S(1)} %get-tuple-element.17), channel_id=1, source_target_pairs={{1,16},{3,18},{5,20},{7,22},{9,24},{11,26},{13,28},{15,30},{16,1},... | collective-permute-start | bytes 196616 | tf_op jit(solution)/shard_map/ppermute | solution.py:329
  2.8 9.1 %collective-permute-start.1 = (bf16[16,16,128]{2,1,0:T(8,128)(2,1)S(1)}, bf16[16,16,128]{2,1,0:T(8,128)(2,1)S(1)}, u32[]{:S(2)}, u32[]{:S(2)}) collective-permute-start(bf16[16,16,128]{2,1,0:T(8,128)(2,1)S(1)} %get-tuple-element.17), channel_id=1, source_target_pairs={{0,16},{1,0},{2,18},{3,2},{4,20},{5,4},{6,22},{7,6},{8,24},{9,8},{... | collective-permute-start | bytes 196616 | tf_op jit(solution)/shard_map/ppermute | solution.py:329
  11.9 13.3 %copy-start.1 = (bf16[128,640]{1,0:T(8,128)(2,1)S(1)}, bf16[128,640]{1,0:T(8,128)(2,1)}, u32[]{:S(2)}) copy-start(bf16[128,640]{1,0:T(8,128)(2,1)} %w_ref.4) | copy-start | bytes 491524
  11.9 5.0 %collective-permute-start.3 = (bf16[2,16,16,128]{3,2,1,0:T(8,128)(2,1)S(1)}, bf16[2,16,16,128]{3,2,1,0:T(8,128)(2,1)S(1)}, u32[]{:S(2)}, u32[]{:S(2)}) collective-permute-start(bf16[2,16,16,128]{3,2,1,0:T(8,128)(2,1)S(1)} %maximum_select_fusion.refs_2_), channel_id=1, source_target_pairs={{0,8},{1,9},{2,10},{3,11},{4,12},{5,13},{6,14},{7,15},{8,0},{9,1},... | collective-permute-start | bytes 393224 | tf_op jit(solution)/shard_map/ppermute | solution.py:329
  13.5 6.3 %collective-permute-start.6 = (bf16[2,16,16,128]{3,2,1,0:T(8,128)(2,1)S(1)}, bf16[2,16,16,128]{3,2,1,0:T(8,128)(2,1)S(1)}, u32[]{:S(2)}, u32[]{:S(2)}) collective-permute-start(bf16[2,16,16,128]{3,2,1,0:T(8,128)(2,1)S(1)} %maximum_select_fusion.refs_2_), channel_id=1, source_target_pairs={{0,4},{1,5},{2,6},{3,7},{4,0},{5,1},{6,2},{7,3},{8,12},{9,13},{10,... | collective-permute-start | bytes 393224 | tf_op jit(solution)/shard_map/ppermute | solution.py:329
  16.9 5.0 %collective-permute-start.4 = (bf16[2,16,16,128]{3,2,1,0:T(8,128)(2,1)S(1)}, bf16[2,16,16,128]{3,2,1,0:T(8,128)(2,1)S(1)}, u32[]{:S(2)}, u32[]{:S(2)}) collective-permute-start(bf16[2,16,16,128]{3,2,1,0:T(8,128)(2,1)S(1)} %collective-permute-done.3.refs_4_), channel_id=1, source_target_pairs={{0,4},{1,5},{2,6},{3,7},{4,0},{5,1},{6,2},{7,3},{8,12},{9,13},{10,... | collective-permute-start | bytes 393224 | tf_op jit(solution)/shard_map/ppermute | solution.py:329
  18.4 9.5 %collective-permute-start.8 = (bf16[2,16,16,128]{3,2,1,0:T(8,128)(2,1)S(1)}, bf16[2,16,16,128]{3,2,1,0:T(8,128)(2,1)S(1)}, u32[]{:S(2)}, u32[]{:S(2)}) collective-permute-start(bf16[2,16,16,128]{3,2,1,0:T(8,128)(2,1)S(1)} %maximum_select_fusion.refs_2_), channel_id=1, source_target_pairs={{0,2},{1,3},{2,0},{3,1},{4,6},{5,7},{6,4},{7,5},{8,10},{9,11},{10,... | collective-permute-start | bytes 393224 | tf_op jit(solution)/shard_map/ppermute | solution.py:329
  18.4 9.5 %collective-permute-start.9 = (bf16[2,16,16,128]{3,2,1,0:T(8,128)(2,1)S(1)}, bf16[2,16,16,128]{3,2,1,0:T(8,128)(2,1)S(1)}, u32[]{:S(2)}, u32[]{:S(2)}) collective-permute-start(bf16[2,16,16,128]{3,2,1,0:T(8,128)(2,1)S(1)} %collective-permute-done.3.refs_4_), channel_id=1, source_target_pairs={{0,2},{1,3},{2,0},{3,1},{4,6},{5,7},{6,4},{7,5},{8,10},{9,11},{10,... | collective-permute-start | bytes 393224 | tf_op jit(solution)/shard_map/ppermute | solution.py:329
  19.9 9.3 %collective-permute-start.7 = (bf16[2,16,16,128]{3,2,1,0:T(8,128)(2,1)S(1)}, bf16[2,16,16,128]{3,2,1,0:T(8,128)(2,1)S(1)}, u32[]{:S(2)}, u32[]{:S(2)}) collective-permute-start(bf16[2,16,16,128]{3,2,1,0:T(8,128)(2,1)S(1)} %collective-permute-done.6.refs_2_), channel_id=1, source_target_pairs={{0,2},{1,3},{2,0},{3,1},{4,6},{5,7},{6,4},{7,5},{8,10},{9,11},{10,... | collective-permute-start | bytes 393224 | tf_op jit(solution)/shard_map/ppermute | solution.py:329
  21.9 8.0 %collective-permute-start.5 = (bf16[2,16,16,128]{3,2,1,0:T(8,128)(2,1)S(1)}, bf16[2,16,16,128]{3,2,1,0:T(8,128)(2,1)S(1)}, u32[]{:S(2)}, u32[]{:S(2)}) collective-permute-start(bf16[2,16,16,128]{3,2,1,0:T(8,128)(2,1)S(1)} %collective-permute-done.4.refs_2_), channel_id=1, source_target_pairs={{0,2},{1,3},{2,0},{3,1},{4,6},{5,7},{6,4},{7,5},{8,10},{9,11},{10,... | collective-permute-start | bytes 393224 | tf_op jit(solution)/shard_map/ppermute | solution.py:329
  21.9 6.0 %collective-permute-start = (bf16[16,16,128]{2,1,0:T(8,128)(2,1)S(1)}, bf16[16,16,128]{2,1,0:T(8,128)(2,1)S(1)}, u32[]{:S(2)}, u32[]{:S(2)}) collective-permute-start(bf16[16,16,128]{2,1,0:T(8,128)(2,1)S(1)} %get-tuple-element.16.refs_0_), channel_id=1, source_target_pairs={{0,1},{1,0},{2,3},{3,2},{4,5},{5,4},{6,7},{7,6},{8,9},{9,8},{10,11... | collective-permute-start | bytes 196616 | tf_op jit(solution)/shard_map/ppermute | solution.py:329
  29.2 0.8 %copy-start.3 = (bf16[128,128]{1,0:T(8,128)(2,1)S(1)}, bf16[128,128]{1,0:T(8,128)(2,1)}, u32[]{:S(2)}) copy-start(bf16[128,128]{1,0:T(8,128)(2,1)} %refs_7_.1) | copy-start | bytes 98308
  29.9 0.7 %copy-start.5 = (bf16[128,4]{0,1:T(4,128)(2,1)S(1)}, bf16[128,4]{0,1:T(4,128)(2,1)}, u32[]{:S(2)}) copy-start(bf16[128,4]{0,1:T(4,128)(2,1)} %param.18) | copy-start | bytes 3076
  30.6 24.6 %copy-start.2 = (bf16[128,512]{1,0:T(8,128)(2,1)S(1)}, bf16[128,512]{1,0:T(8,128)(2,1)}, u32[]{:S(2)}) copy-start(bf16[128,512]{1,0:T(8,128)(2,1)} %refs_16_.1) | copy-start | bytes 393220
  33.1 23.3 %collective-permute-start.19 = (bf16[16,128,128]{2,1,0:T(8,128)(2,1)S(1)}, bf16[16,128,128]{2,1,0:T(8,128)(2,1)S(1)}, u32[]{:S(2)}, u32[]{:S(2)}) collective-permute-start(bf16[16,128,128]{2,1,0:T(8,128)(2,1)S(1)} %get-tuple-element.20.refs_13_), channel_id=1, source_target_pairs={{0,1},{1,0},{2,3},{3,2},{4,5},{5,4},{6,7},{7,6},{8,9},{9,8},{10,11... | collective-permute-start | bytes 1572872 | tf_op jit(solution)/shard_map/ppermute | solution.py:329
  34.9 4.6 %collective-permute-start.11 = (bf16[4,16,128]{2,1,0:T(8,128)(2,1)S(1)}, bf16[4,16,128]{2,1,0:T(8,128)(2,1)S(1)}, u32[]{:S(2)}, u32[]{:S(2)}) collective-permute-start(bf16[4,16,128]{2,1,0:T(8,128)(2,1)S(1)} %get-tuple-element.19), channel_id=1, source_target_pairs={{1,16},{3,18},{5,20},{7,22},{9,24},{11,26},{13,28},{15,30},{16,1},... | collective-permute-start | bytes 49160 | tf_op jit(solution)/shard_map/ppermute | solution.py:329
  35.5 11.7 %collective-permute-start.10 = (bf16[4,16,128]{2,1,0:T(8,128)(2,1)S(1)}, bf16[4,16,128]{2,1,0:T(8,128)(2,1)S(1)}, u32[]{:S(2)}, u32[]{:S(2)}) collective-permute-start(bf16[4,16,128]{2,1,0:T(8,128)(2,1)S(1)} %get-tuple-element.19), channel_id=1, source_target_pairs={{0,16},{1,0},{2,18},{3,2},{4,20},{5,4},{6,22},{7,6},{8,24},{9,8},{... | collective-permute-start | bytes 49160 | tf_op jit(solution)/shard_map/ppermute | solution.py:329
  47.2 4.0 %collective-permute-start.12 = (bf16[2,4,16,128]{3,2,1,0:T(8,128)(2,1)S(1)}, bf16[2,4,16,128]{3,2,1,0:T(8,128)(2,1)S(1)}, u32[]{:S(2)}, u32[]{:S(2)}) collective-permute-start(bf16[2,4,16,128]{3,2,1,0:T(8,128)(2,1)S(1)} %maximum_select_fusion.1.refs_0_), channel_id=1, source_target_pairs={{0,8},{1,9},{2,10},{3,11},{4,12},{5,13},{6,14},{7,15},{8,0},{9,1},... | collective-permute-start | bytes 98312 | tf_op jit(solution)/shard_map/ppermute | solution.py:329
  49.1 4.1 %collective-permute-start.13 = (bf16[2,4,16,128]{3,2,1,0:T(8,128)(2,1)S(1)}, bf16[2,4,16,128]{3,2,1,0:T(8,128)(2,1)S(1)}, u32[]{:S(2)}, u32[]{:S(2)}) collective-permute-start(bf16[2,4,16,128]{3,2,1,0:T(8,128)(2,1)S(1)} %maximum_select_fusion.1.refs_0_), channel_id=1, source_target_pairs={{0,4},{1,5},{2,6},{3,7},{4,0},{5,1},{6,2},{7,3},{8,12},{9,13},{10,... | collective-permute-start | bytes 98312 | tf_op jit(solution)/shard_map/ppermute | solution.py:329
  51.2 3.9 %collective-permute-start.14 = (bf16[2,4,16,128]{3,2,1,0:T(8,128)(2,1)S(1)}, bf16[2,4,16,128]{3,2,1,0:T(8,128)(2,1)S(1)}, u32[]{:S(2)}, u32[]{:S(2)}) collective-permute-start(bf16[2,4,16,128]{3,2,1,0:T(8,128)(2,1)S(1)} %collective-permute-done.12.refs_1_), channel_id=1, source_target_pairs={{0,4},{1,5},{2,6},{3,7},{4,0},{5,1},{6,2},{7,3},{8,12},{9,13},{10,... | collective-permute-start | bytes 98312 | tf_op jit(solution)/shard_map/ppermute | solution.py:329
  52.7 3.1 %collective-permute-start.15 = (bf16[2,4,16,128]{3,2,1,0:T(8,128)(2,1)S(1)}, bf16[2,4,16,128]{3,2,1,0:T(8,128)(2,1)S(1)}, u32[]{:S(2)}, u32[]{:S(2)}) collective-permute-start(bf16[2,4,16,128]{3,2,1,0:T(8,128)(2,1)S(1)} %maximum_select_fusion.1.refs_0_), channel_id=1, source_target_pairs={{0,2},{1,3},{2,0},{3,1},{4,6},{5,7},{6,4},{7,5},{8,10},{9,11},{10,... | collective-permute-start | bytes 98312 | tf_op jit(solution)/shard_map/ppermute | solution.py:329
  52.7 3.2 %collective-permute-start.16 = (bf16[2,4,16,128]{3,2,1,0:T(8,128)(2,1)S(1)}, bf16[2,4,16,128]{3,2,1,0:T(8,128)(2,1)S(1)}, u32[]{:S(2)}, u32[]{:S(2)}) collective-permute-start(bf16[2,4,16,128]{3,2,1,0:T(8,128)(2,1)S(1)} %collective-permute-done.12.refs_1_), channel_id=1, source_target_pairs={{0,2},{1,3},{2,0},{3,1},{4,6},{5,7},{6,4},{7,5},{8,10},{9,11},{10,... | collective-permute-start | bytes 98312 | tf_op jit(solution)/shard_map/ppermute | solution.py:329
  53.2 2.6 %collective-permute-start.17 = (bf16[2,4,16,128]{3,2,1,0:T(8,128)(2,1)S(1)}, bf16[2,4,16,128]{3,2,1,0:T(8,128)(2,1)S(1)}, u32[]{:S(2)}, u32[]{:S(2)}) collective-permute-start(bf16[2,4,16,128]{3,2,1,0:T(8,128)(2,1)S(1)} %collective-permute-done.13.refs_2_), channel_id=1, source_target_pairs={{0,2},{1,3},{2,0},{3,1},{4,6},{5,7},{6,4},{7,5},{8,10},{9,11},{10,... | collective-permute-start | bytes 98312 | tf_op jit(solution)/shard_map/ppermute | solution.py:329
  55.1 1.2 %collective-permute-start.18 = (bf16[2,4,16,128]{3,2,1,0:T(8,128)(2,1)S(1)}, bf16[2,4,16,128]{3,2,1,0:T(8,128)(2,1)S(1)}, u32[]{:S(2)}, u32[]{:S(2)}) collective-permute-start(bf16[2,4,16,128]{3,2,1,0:T(8,128)(2,1)S(1)} %collective-permute-done.14.refs_3_), channel_id=1, source_target_pairs={{0,2},{1,3},{2,0},{3,1},{4,6},{5,7},{6,4},{7,5},{8,10},{9,11},{10,... | collective-permute-start | bytes 98312 | tf_op jit(solution)/shard_map/ppermute | solution.py:329
  55.1 1.2 %copy-start.4 = (bf16[128,128]{1,0:T(8,128)(2,1)S(1)}, bf16[128,128]{1,0:T(8,128)(2,1)}, u32[]{:S(2)}) copy-start(bf16[128,128]{1,0:T(8,128)(2,1)} %refs_17_.1) | copy-start | bytes 98308

commit v3 on v2

--- a/solution.py
+++ b/solution.py
@@ -309,7 +309,7 @@
         half = self.n_blk // 2
         parts = [range(half // 2), range(half // 2, half - 1), range(half - 1, half)]
         groups = [[t for s in part for t in (s, s + half)] for part in parts]
-        return groups[:-1], groups[-1]
+        return groups[:-1] + [groups[-1][:1]], groups[-1][1:]
 
     def place(self, s):
         if self.fast:
@@ -334,7 +334,7 @@
     def flip_row(self, value, bit):
         return self.move(value, lambda r, c: (r ^ bit, c))
 
-    def gather(self, own):
+    def gather(self, own, relay):
         if not self.fast:
             stacked = lax.all_gather(own, "row", axis=0)
             stacked = lax.all_to_all(stacked, "col", split_axis=0, concat_axis=0, tiled=True)
@@ -345,15 +345,25 @@
         half = self.n_row // 2
         same = lax.axis_index("row") // half == lax.axis_index("col")
 
-        def first(r, c):
-            return (r ^ half, c) if r // half == c else (r, 1 - c)
-
-        def second(r, c):
-            return None if r // half == c else (r ^ half, 1 - c)
-
-        near = self.move(own, first)
-        far = self.move(own, second)
-        pair = jnp.where(same, jnp.stack([own, near]), jnp.stack([near, far]))
+        def inside(r, c):
+            return r // half == c
+
+        if relay:
+            near = self.move(own, lambda r, c: None if inside(r, c) else (r, 1 - c))
+            both = jnp.stack([own, near])
+            far = self.move(both, lambda r, c: (r ^ half, c) if inside(r, c) else None)
+            pair = jnp.where(same, both, far)
+        else:
+
+            def first(r, c):
+                return (r ^ half, c) if inside(r, c) else (r, 1 - c)
+
+            def second(r, c):
+                return None if inside(r, c) else (r ^ half, 1 - c)
+
+            near = self.move(own, first)
+            far = self.move(own, second)
+            pair = jnp.where(same, jnp.stack([own, near]), jnp.stack([near, far]))
         blocks = [pair]
         bit = self.n_blk // 2
         while bit:
@@ -406,7 +416,7 @@
                 pltpu.SemaphoreType.DMA((2,)),
             ],
         )(chain_len, pair_rep, tri_gain, sum_gain, att_gain, tri_in)
-        rights = grid.gather(right)
+        rights = grid.gather(right, False)
         lefts = [left] + [grid.shift_col(left, d) for d in range(1, n_col)]
         gate = call(gate_kernel, jax.ShapeDtypeStruct(whole, F32), 0, 3, limit)(
             pair_rep, gains, tri_in
@@ -440,7 +450,7 @@
             [left_scr, pltpu.VMEM((rows, H, cols), F32)],
             aliases={n_col + len(last) + 5: 3} if sums else {},
         )(*lefts, *[rights[s] for s in last], pair_rep, gate, gains, tri_out, att_bias.T, *sums)
-        biases = grid.gather(bias)
+        biases = grid.gather(bias, True)
         others = [grid.shift_col(mid, d) for d in range(1, n_col)]
         wide = jax.ShapeDtypeStruct(whole, BF16)
         query, key, value, att_gate = call(

time: 61.6 us -> 65.5 us (1.063); the launches traced: 61.4 us -> 64.3 us
  waiting for transfers between devices: 19.9 us -> 24.8 us
  starting transfers between devices: 27.4 us -> 25.4 us
    ppermute x20, waiting for transfers between devices: 19.9 us -> 24.8 us  [move(): return lax.ppermute(value, ('row', 'col'), pairs)]
    ppermute x20, starting transfers between devices: 27.4 us -> 25.4 us  [move(): return lax.ppermute(value, ('row', 'col'), pairs)]
    pallas_call x6 -> x7, Pallas kernels: 11.1 us -> 11.2 us  [apply(): return run(*args[:n_smem], *held)]
  transfers between devices with their start and end apart: 20 -> 20, of which waited for: 9 -> 10; matrix products, arithmetic and copies ran while one was open for 0% -> 0% of each run, Pallas kernels for 6% -> 6%
where the time goes in v3:
time: 65.5 us; the launch traced here: 64.3 us
  starting transfers between devices  25.4 us (39%)
  waiting for transfers between devices  24.8 us (38%)
  Pallas kernels  13.3 us (20%)
  local copies, waits for them, and re-layouts  0.68 us (1%)
    ppermute x20, starting transfers between devices, move(): return lax.ppermute(value, ('row', 'col'), pairs)  25.4 us
    ppermute x20, waiting for transfers between devices, move(): return lax.ppermute(value, ('row', 'col'), pairs)  24.8 us
    pallas_call x7, Pallas kernels, apply(): return run(*args[:n_smem], *held)  11.2 us
    pallas_call x1, Pallas kernels, body(): pl.pallas_call(make_edge_kernel(cols, n_col, grid.col_of), name='edges',...  2.11 us
  transfers between devices with their start and end apart: 20, of which 10 were waited for; matrix products, arithmetic and copies ran while one was open for 0% of the time, Pallas kernels for 6%

profile of v3, /device:TPU:0, one launch (start us, length us, event | category | flops | bytes accessed | tf_op | source)
XLA Modules:
  0.0 64.3 jit_solution(16823211745060632135)
XLA Ops:
  0.0 2.1 %edges.1 = (bf16[16,16,128]{2,1,0:T(8,128)(2,1)S(1)}, bf16[16,16,128]{2,1,0:T(8,128)(2,1)S(1)}, f32[3,128]{1,0:T(4,128)S(1)}, f32[1,256]{1,0:T(1,128)S(1)}) custom-call(s32[4]{0:T(128)} %len_ref.1, bf16[16,128,128]{2,1,0:T(8,128)(2,1)} %refs_3_.1, f32[1,128]{1,0:T(1,128)} %bitcast.17, f32[1,128]{1,0:T(1,128)} %bitcast.18, f32[1,128]{1,0:T(1,128)} %bitcast.19, ...), custom_call_target="tpu_custom_call" | custom-call | tf_op jit(solution)/shard_map/edges/pallas_call | solution.py:394
  2.1 0.7 %collective-permute-start.2 = (bf16[16,16,128]{2,1,0:T(8,128)(2,1)S(1)}, bf16[16,16,128]{2,1,0:T(8,128)(2,1)S(1)}, u32[]{:S(2)}, u32[]{:S(2)}) collective-permute-start(bf16[16,16,128]{2,1,0:T(8,128)(2,1)S(1)} %get-tuple-element.17), channel_id=1, source_target_pairs={{1,16},{3,18},{5,20},{7,22},{9,24},{11,26},{13,28},{15,30},{16,1},... | collective-permute-start | bytes 196616 | tf_op jit(solution)/shard_map/ppermute | solution.py:329
  2.8 6.6 %collective-permute-start.1 = (bf16[16,16,128]{2,1,0:T(8,128)(2,1)S(1)}, bf16[16,16,128]{2,1,0:T(8,128)(2,1)S(1)}, u32[]{:S(2)}, u32[]{:S(2)}) collective-permute-start(bf16[16,16,128]{2,1,0:T(8,128)(2,1)S(1)} %get-tuple-element.17), channel_id=1, source_target_pairs={{0,16},{1,0},{2,18},{3,2},{4,20},{5,4},{6,22},{7,6},{8,24},{9,8},{... | collective-permute-start | bytes 196616 | tf_op jit(solution)/shard_map/ppermute | solution.py:329
  9.4 2.4 %collective-permute-done.1 = bf16[16,16,128]{2,1,0:T(8,128)(2,1)S(1)} collective-permute-done((bf16[16,16,128]{2,1,0:T(8,128)(2,1)S(1)}, bf16[16,16,128]{2,1,0:T(8,128)(2,1)S(1)}, u32[]{:S(2)}, u32[]{:S(2)}) %collective-permute-start.1) | collective-permute-done | bytes 65568 | tf_op jit(solution)/shard_map/ppermute | solution.py:329
  11.9 1.6 %collective-permute-start.3 = (bf16[2,16,16,128]{3,2,1,0:T(8,128)(2,1)S(1)}, bf16[2,16,16,128]{3,2,1,0:T(8,128)(2,1)S(1)}, u32[]{:S(2)}, u32[]{:S(2)}) collective-permute-start(bf16[2,16,16,128]{3,2,1,0:T(8,128)(2,1)S(1)} %maximum_select_fusion.refs_2_), channel_id=1, source_target_pairs={{0,8},{1,9},{2,10},{3,11},{4,12},{5,13},{6,14},{7,15},{8,0},{9,1},... | collective-permute-start | bytes 393224 | tf_op jit(solution)/shard_map/ppermute | solution.py:329
  13.5 1.5 %collective-permute-start.6 = (bf16[2,16,16,128]{3,2,1,0:T(8,128)(2,1)S(1)}, bf16[2,16,16,128]{3,2,1,0:T(8,128)(2,1)S(1)}, u32[]{:S(2)}, u32[]{:S(2)}) collective-permute-start(bf16[2,16,16,128]{3,2,1,0:T(8,128)(2,1)S(1)} %maximum_select_fusion.refs_2_), channel_id=1, source_target_pairs={{0,4},{1,5},{2,6},{3,7},{4,0},{5,1},{6,2},{7,3},{8,12},{9,13},{10,... | collective-permute-start | bytes 393224 | tf_op jit(solution)/shard_map/ppermute | solution.py:329
  15.0 1.9 %collective-permute-done.3.refs_4_ = bf16[2,16,16,128]{3,2,1,0:T(8,128)(2,1)S(1)} collective-permute-done((bf16[2,16,16,128]{3,2,1,0:T(8,128)(2,1)S(1)}, bf16[2,16,16,128]{3,2,1,0:T(8,128)(2,1)S(1)}, u32[]{:S(2)}, u32[]{:S(2)}) %collective-permute-start.3) | collective-permute-done | bytes 131104 | tf_op jit(solution)/shard_map/ppermute | solution.py:329
  16.9 1.5 %collective-permute-start.4 = (bf16[2,16,16,128]{3,2,1,0:T(8,128)(2,1)S(1)}, bf16[2,16,16,128]{3,2,1,0:T(8,128)(2,1)S(1)}, u32[]{:S(2)}, u32[]{:S(2)}) collective-permute-start(bf16[2,16,16,128]{3,2,1,0:T(8,128)(2,1)S(1)} %collective-permute-done.3.refs_4_), channel_id=1, source_target_pairs={{0,4},{1,5},{2,6},{3,7},{4,0},{5,1},{6,2},{7,3},{8,12},{9,13},{10,... | collective-permute-start | bytes 393224 | tf_op jit(solution)/shard_map/ppermute | solution.py:329
  18.4 0.0 collective-permute-start.8
  18.4 0.5 collective-permute-start.9
  18.9 0.9 %collective-permute-done.6.refs_2_ = bf16[2,16,16,128]{3,2,1,0:T(8,128)(2,1)S(1)} collective-permute-done((bf16[2,16,16,128]{3,2,1,0:T(8,128)(2,1)S(1)}, bf16[2,16,16,128]{3,2,1,0:T(8,128)(2,1)S(1)}, u32[]{:S(2)}, u32[]{:S(2)}) %collective-permute-start.6) | collective-permute-done | bytes 131104 | tf_op jit(solution)/shard_map/ppermute | solution.py:329
  19.9 0.0 collective-permute-start.7
  19.9 2.0 %collective-permute-done.4.refs_2_ = bf16[2,16,16,128]{3,2,1,0:T(8,128)(2,1)S(1)} collective-permute-done((bf16[2,16,16,128]{3,2,1,0:T(8,128)(2,1)S(1)}, bf16[2,16,16,128]{3,2,1,0:T(8,128)(2,1)S(1)}, u32[]{:S(2)}, u32[]{:S(2)}) %collective-permute-start.4) | collective-permute-done | bytes 131104 | tf_op jit(solution)/shard_map/ppermute | solution.py:329
  21.9 0.0 collective-permute-start.5
  21.9 3.2 %collective-permute-start = (bf16[16,16,128]{2,1,0:T(8,128)(2,1)S(1)}, bf16[16,16,128]{2,1,0:T(8,128)(2,1)S(1)}, u32[]{:S(2)}, u32[]{:S(2)}) collective-permute-start(bf16[16,16,128]{2,1,0:T(8,128)(2,1)S(1)} %get-tuple-element.16.refs_0_), channel_id=1, source_target_pairs={{0,1},{1,0},{2,3},{3,2},{4,5},{5,4},{6,7},{7,6},{8,9},{9,8},{10,11... | collective-permute-start | bytes 196616 | tf_op jit(solution)/shard_map/ppermute | solution.py:329
  25.1 0.9 %shard_map.100.refs_4_ = f32[16,128,128]{2,1,0:T(8,128)S(1)} custom-call(bf16[16,128,128]{2,1,0:T(8,128)(2,1)S(1)} %copy-done, f32[3,128]{1,0:T(4,128)S(1)} %get-tuple-element.18.gains_ref.refs_5_.refs_14_, bf16[128,640]{1,0:T(8,128)(2,1)S(1)} %copy-done.1), custom_call_target="tpu_custom_call" | custom-call | tf_op jit(solution)/shard_map/pallas_call | solution.py:69
  26.1 1.8 %collective-permute-done.refs_1_ = bf16[16,16,128]{2,1,0:T(8,128)(2,1)S(1)} collective-permute-done((bf16[16,16,128]{2,1,0:T(8,128)(2,1)S(1)}, bf16[16,16,128]{2,1,0:T(8,128)(2,1)S(1)}, u32[]{:S(2)}, u32[]{:S(2)}) %collective-permute-start) | collective-permute-done | bytes 65568 | tf_op jit(solution)/shard_map/ppermute | solution.py:329
  27.9 0.0 collective-permute-done.8.refs_3_
  27.9 0.0 collective-permute-done.9.refs_5_
  27.9 1.3 %shard_map.101.refs_4_ = f32[16,128,128]{2,1,0:T(8,128)S(1)} custom-call(bf16[16,16,128]{2,1,0:T(8,128)(2,1)S(1)} %get-tuple-element.16.refs_0_, bf16[16,16,128]{2,1,0:T(8,128)(2,1)S(1)} %collective-permute-done.refs_1_, bf16[2,16,16,128]{3,2,1,0:T(8,128)(2,1)S(1)} %maximum_select_fusion.refs_2_, ...), custom_call_target="tpu_custom_call" | custom-call | tf_op jit(solution)/shard_map/pallas_call | solution.py:69
  29.2 0.0 collective-permute-done.7.refs_3_
  29.2 0.7 %shard_map.102.refs_3_ = f32[16,128,128]{2,1,0:T(8,128)S(1)} custom-call(bf16[16,16,128]{2,1,0:T(8,128)(2,1)S(1)} %get-tuple-element.16.refs_0_, bf16[16,16,128]{2,1,0:T(8,128)(2,1)S(1)} %collective-permute-done.refs_1_, bf16[2,16,16,128]{3,2,1,0:T(8,128)(2,1)S(1)} %collective-permute-done.6.refs_2_, ...), custom_call_target="tpu_custom_call", output_to_operand_aliasing={{}: (4, {})} | custom-call | tf_op jit(solution)/shard_map/pallas_call | solution.py:69
  29.9 0.3 shard_map.103.refs_8_
  30.2 0.0 copy-start.5
  30.3 0.0 collective-permute-done.5.refs_2_
  30.3 0.4 copy-done.3
  30.6 0.3 copy-done.5
  30.9 2.2 %shard_map.104 = (bf16[16,128,128]{2,1,0:T(8,128)(2,1)S(1)}, bf16[16,128,128]{2,1,0:T(8,128)(2,1)S(1)}, bf16[4,16,128]{2,1,0:T(8,128)(2,1)S(1)}, f32[16,128,128]{2,1,0:T(8,128)S(1)}) custom-call(bf16[16,16,128]{2,1,0:T(8,128)(2,1)S(1)} %get-tuple-element.16.refs_0_, ...), custom_call_target="tpu_custom_call", output_to_operand_aliasing={{3}: (8, {})} | custom-call | tf_op jit(solution)/shard_map/pallas_call | solution.py:69
  33.1 0.0 copy-start.2
  33.1 1.8 %collective-permute-start.19 = (bf16[16,128,128]{2,1,0:T(8,128)(2,1)S(1)}, bf16[16,128,128]{2,1,0:T(8,128)(2,1)S(1)}, u32[]{:S(2)}, u32[]{:S(2)}) collective-permute-start(bf16[16,128,128]{2,1,0:T(8,128)(2,1)S(1)} %get-tuple-element.20.refs_13_), channel_id=1, source_target_pairs={{0,1},{1,0},{2,3},{3,2},{4,5},{5,4},{6,7},{7,6},{8,9},{9,8},{10,11... | collective-permute-start | bytes 1572872 | tf_op jit(solution)/shard_map/ppermute | solution.py:329
  34.9 1.3 %collective-permute-start.10 = (bf16[4,16,128]{2,1,0:T(8,128)(2,1)S(1)}, bf16[4,16,128]{2,1,0:T(8,128)(2,1)S(1)}, u32[]{:S(2)}, u32[]{:S(2)}) collective-permute-start(bf16[4,16,128]{2,1,0:T(8,128)(2,1)S(1)} %get-tuple-element.19), channel_id=1, source_target_pairs={{1,0},{3,2},{5,4},{7,6},{9,8},{11,10},{13,12},{15,14},{16,17},{18,... | collective-permute-start | bytes 49160 | tf_op jit(solution)/shard_map/ppermute | solution.py:329
  36.2 11.1 %collective-permute-done.10 = bf16[4,16,128]{2,1,0:T(8,128)(2,1)S(1)} collective-permute-done((bf16[4,16,128]{2,1,0:T(8,128)(2,1)S(1)}, bf16[4,16,128]{2,1,0:T(8,128)(2,1)S(1)}, u32[]{:S(2)}, u32[]{:S(2)}) %collective-permute-start.10) | collective-permute-done | bytes 16416 | tf_op jit(solution)/shard_map/ppermute | solution.py:329
  47.3 1.3 %collective-permute-start.11 = (bf16[2,4,16,128]{3,2,1,0:T(8,128)(2,1)S(1)}, bf16[2,4,16,128]{3,2,1,0:T(8,128)(2,1)S(1)}, u32[]{:S(2)}, u32[]{:S(2)}) collective-permute-start(bf16[2,4,16,128]{3,2,1,0:T(8,128)(2,1)S(1)} %pad_maximum_fusion), channel_id=1, source_target_pairs={{0,16},{2,18},{4,20},{6,22},{8,24},{10,26},{12,28},{14,30},{17,1},... | collective-permute-start | bytes 98312 | tf_op jit(solution)/shard_map/ppermute | solution.py:329
  48.6 1.6 %collective-permute-done.11 = bf16[2,4,16,128]{3,2,1,0:T(8,128)(2,1)S(1)} collective-permute-done((bf16[2,4,16,128]{3,2,1,0:T(8,128)(2,1)S(1)}, bf16[2,4,16,128]{3,2,1,0:T(8,128)(2,1)S(1)}, u32[]{:S(2)}, u32[]{:S(2)}) %collective-permute-start.11) | collective-permute-done | bytes 32800 | tf_op jit(solution)/shard_map/ppermute | solution.py:329
  50.2 1.8 %collective-permute-start.12 = (bf16[2,4,16,128]{3,2,1,0:T(8,128)(2,1)S(1)}, bf16[2,4,16,128]{3,2,1,0:T(8,128)(2,1)S(1)}, u32[]{:S(2)}, u32[]{:S(2)}) collective-permute-start(bf16[2,4,16,128]{3,2,1,0:T(8,128)(2,1)S(1)} %broadcast_select_fusion.refs_0_), channel_id=1, source_target_pairs={{0,8},{1,9},{2,10},{3,11},{4,12},{5,13},{6,14},{7,15},{8,0},{9,1},... | collective-permute-start | bytes 98312 | tf_op jit(solution)/shard_map/ppermute | solution.py:329
  52.0 1.5 %collective-permute-start.13 = (bf16[2,4,16,128]{3,2,1,0:T(8,128)(2,1)S(1)}, bf16[2,4,16,128]{3,2,1,0:T(8,128)(2,1)S(1)}, u32[]{:S(2)}, u32[]{:S(2)}) collective-permute-start(bf16[2,4,16,128]{3,2,1,0:T(8,128)(2,1)S(1)} %broadcast_select_fusion.refs_0_), channel_id=1, source_target_pairs={{0,4},{1,5},{2,6},{3,7},{4,0},{5,1},{6,2},{7,3},{8,12},{9,13},{10,... | collective-permute-start | bytes 98312 | tf_op jit(solution)/shard_map/ppermute | solution.py:329
  53.5 0.6 collective-permute-done.12.refs_1_
  54.1 1.5 %collective-permute-start.14 = (bf16[2,4,16,128]{3,2,1,0:T(8,128)(2,1)S(1)}, bf16[2,4,16,128]{3,2,1,0:T(8,128)(2,1)S(1)}, u32[]{:S(2)}, u32[]{:S(2)}) collective-permute-start(bf16[2,4,16,128]{3,2,1,0:T(8,128)(2,1)S(1)} %collective-permute-done.12.refs_1_), channel_id=1, source_target_pairs={{0,4},{1,5},{2,6},{3,7},{4,0},{5,1},{6,2},{7,3},{8,12},{9,13},{10,... | collective-permute-start | bytes 98312 | tf_op jit(solution)/shard_map/ppermute | solution.py:329
  55.6 0.0 collective-permute-start.15
  55.6 0.5 collective-permute-start.16
  56.1 0.0 collective-permute-start.17
  56.1 1.9 %collective-permute-done.14.refs_3_ = bf16[2,4,16,128]{3,2,1,0:T(8,128)(2,1)S(1)} collective-permute-done((bf16[2,4,16,128]{3,2,1,0:T(8,128)(2,1)S(1)}, bf16[2,4,16,128]{3,2,1,0:T(8,128)(2,1)S(1)}, u32[]{:S(2)}, u32[]{:S(2)}) %collective-permute-start.14) | collective-permute-done | bytes 32800 | tf_op jit(solution)/shard_map/ppermute | solution.py:329
  58.0 0.0 collective-permute-start.18
  58.0 0.7 %shard_map.105 = (bf16[16,128,128]{2,1,0:T(8,128)(2,1)S(1)}, bf16[16,128,128]{2,1,0:T(8,128)(2,1)S(1)}, bf16[16,128,128]{2,1,0:T(8,128)(2,1)S(1)}, f32[16,128,128]{2,1,0:T(8,128)S(1)}) custom-call(bf16[16,128,128]{2,1,0:T(8,128)(2,1)S(1)} %get-tuple-element.21.norm_ref, bf16[128,512]{1,0:T(8,128)(2,1)S(1)} %copy-done.2), custom_call_target="tpu_custom_call" | custom-call | tf_op jit(solution)/shard_map/pallas_call | solution.py:69
  58.7 0.0 collective-permute-done.15.refs_4_
  58.7 0.0 collective-permute-done.17.refs_6_
  58.8 0.5 collective-permute-done.18.refs_7_
  59.2 5.0 %shard_map.106 = bf16[16,128,128]{2,1,0:T(8,128)(2,1)} custom-call(bf16[2,4,16,128]{3,2,1,0:T(8,128)(2,1)S(1)} %broadcast_select_fusion.refs_0_, bf16[2,4,16,128]{3,2,1,0:T(8,128)(2,1)S(1)} %collective-permute-done.12.refs_1_, bf16[2,4,16,128]{3,2,1,0:T(8,128)(2,1)S(1)} %collective-permute-done.13.refs_2_, ...), custom_call_target="tpu_custom_call" | custom-call | tf_op jit(solution)/shard_map/pallas_call | solution.py:69
  (15 shorter events, 0.1 us)
Async XLA Ops:
  0.0 25.1 %copy-start = (bf16[16,128,128]{2,1,0:T(8,128)(2,1)S(1)}, bf16[16,128,128]{2,1,0:T(8,128)(2,1)}, u32[]{:S(2)}) copy-start(bf16[16,128,128]{2,1,0:T(8,128)(2,1)} %refs_3_.1) | copy-start | bytes 1572868
  2.1 7.3 %collective-permute-start.2 = (bf16[16,16,128]{2,1,0:T(8,128)(2,1)S(1)}, bf16[16,16,128]{2,1,0:T(8,128)(2,1)S(1)}, u32[]{:S(2)}, u32[]{:S(2)}) collective-permute-start(bf16[16,16,128]{2,1,0:T(8,128)(2,1)S(1)} %get-tuple-element.17), channel_id=1, source_target_pairs={{1,16},{3,18},{5,20},{7,22},{9,24},{11,26},{13,28},{15,30},{16,1},... | collective-permute-start | bytes 196616 | tf_op jit(solution)/shard_map/ppermute | solution.py:329
  2.8 9.1 %collective-permute-start.1 = (bf16[16,16,128]{2,1,0:T(8,128)(2,1)S(1)}, bf16[16,16,128]{2,1,0:T(8,128)(2,1)S(1)}, u32[]{:S(2)}, u32[]{:S(2)}) collective-permute-start(bf16[16,16,128]{2,1,0:T(8,128)(2,1)S(1)} %get-tuple-element.17), channel_id=1, source_target_pairs={{0,16},{1,0},{2,18},{3,2},{4,20},{5,4},{6,22},{7,6},{8,24},{9,8},{... | collective-permute-start | bytes 196616 | tf_op jit(solution)/shard_map/ppermute | solution.py:329
  11.9 13.3 %copy-start.1 = (bf16[128,640]{1,0:T(8,128)(2,1)S(1)}, bf16[128,640]{1,0:T(8,128)(2,1)}, u32[]{:S(2)}) copy-start(bf16[128,640]{1,0:T(8,128)(2,1)} %w_ref.4) | copy-start | bytes 491524
  11.9 5.0 %collective-permute-start.3 = (bf16[2,16,16,128]{3,2,1,0:T(8,128)(2,1)S(1)}, bf16[2,16,16,128]{3,2,1,0:T(8,128)(2,1)S(1)}, u32[]{:S(2)}, u32[]{:S(2)}) collective-permute-start(bf16[2,16,16,128]{3,2,1,0:T(8,128)(2,1)S(1)} %maximum_select_fusion.refs_2_), channel_id=1, source_target_pairs={{0,8},{1,9},{2,10},{3,11},{4,12},{5,13},{6,14},{7,15},{8,0},{9,1},... | collective-permute-start | bytes 393224 | tf_op jit(solution)/shard_map/ppermute | solution.py:329
  13.5 6.3 %collective-permute-start.6 = (bf16[2,16,16,128]{3,2,1,0:T(8,128)(2,1)S(1)}, bf16[2,16,16,128]{3,2,1,0:T(8,128)(2,1)S(1)}, u32[]{:S(2)}, u32[]{:S(2)}) collective-permute-start(bf16[2,16,16,128]{3,2,1,0:T(8,128)(2,1)S(1)} %maximum_select_fusion.refs_2_), channel_id=1, source_target_pairs={{0,4},{1,5},{2,6},{3,7},{4,0},{5,1},{6,2},{7,3},{8,12},{9,13},{10,... | collective-permute-start | bytes 393224 | tf_op jit(solution)/shard_map/ppermute | solution.py:329
  16.9 5.0 %collective-permute-start.4 = (bf16[2,16,16,128]{3,2,1,0:T(8,128)(2,1)S(1)}, bf16[2,16,16,128]{3,2,1,0:T(8,128)(2,1)S(1)}, u32[]{:S(2)}, u32[]{:S(2)}) collective-permute-start(bf16[2,16,16,128]{3,2,1,0:T(8,128)(2,1)S(1)} %collective-permute-done.3.refs_4_), channel_id=1, source_target_pairs={{0,4},{1,5},{2,6},{3,7},{4,0},{5,1},{6,2},{7,3},{8,12},{9,13},{10,... | collective-permute-start | bytes 393224 | tf_op jit(solution)/shard_map/ppermute | solution.py:329
  18.4 9.5 %collective-permute-start.8 = (bf16[2,16,16,128]{3,2,1,0:T(8,128)(2,1)S(1)}, bf16[2,16,16,128]{3,2,1,0:T(8,128)(2,1)S(1)}, u32[]{:S(2)}, u32[]{:S(2)}) collective-permute-start(bf16[2,16,16,128]{3,2,1,0:T(8,128)(2,1)S(1)} %maximum_select_fusion.refs_2_), channel_id=1, source_target_pairs={{0,2},{1,3},{2,0},{3,1},{4,6},{5,7},{6,4},{7,5},{8,10},{9,11},{10,... | collective-permute-start | bytes 393224 | tf_op jit(solution)/shard_map/ppermute | solution.py:329
  18.4 9.5 %collective-permute-start.9 = (bf16[2,16,16,128]{3,2,1,0:T(8,128)(2,1)S(1)}, bf16[2,16,16,128]{3,2,1,0:T(8,128)(2,1)S(1)}, u32[]{:S(2)}, u32[]{:S(2)}) collective-permute-start(bf16[2,16,16,128]{3,2,1,0:T(8,128)(2,1)S(1)} %collective-permute-done.3.refs_4_), channel_id=1, source_target_pairs={{0,2},{1,3},{2,0},{3,1},{4,6},{5,7},{6,4},{7,5},{8,10},{9,11},{10,... | collective-permute-start | bytes 393224 | tf_op jit(solution)/shard_map/ppermute | solution.py:329
  19.9 9.3 %collective-permute-start.7 = (bf16[2,16,16,128]{3,2,1,0:T(8,128)(2,1)S(1)}, bf16[2,16,16,128]{3,2,1,0:T(8,128)(2,1)S(1)}, u32[]{:S(2)}, u32[]{:S(2)}) collective-permute-start(bf16[2,16,16,128]{3,2,1,0:T(8,128)(2,1)S(1)} %collective-permute-done.6.refs_2_), channel_id=1, source_target_pairs={{0,2},{1,3},{2,0},{3,1},{4,6},{5,7},{6,4},{7,5},{8,10},{9,11},{10,... | collective-permute-start | bytes 393224 | tf_op jit(solution)/shard_map/ppermute | solution.py:329
  21.9 8.4 %collective-permute-start.5 = (bf16[2,16,16,128]{3,2,1,0:T(8,128)(2,1)S(1)}, bf16[2,16,16,128]{3,2,1,0:T(8,128)(2,1)S(1)}, u32[]{:S(2)}, u32[]{:S(2)}) collective-permute-start(bf16[2,16,16,128]{3,2,1,0:T(8,128)(2,1)S(1)} %collective-permute-done.4.refs_2_), channel_id=1, source_target_pairs={{0,2},{1,3},{2,0},{3,1},{4,6},{5,7},{6,4},{7,5},{8,10},{9,11},{10,... | collective-permute-start | bytes 393224 | tf_op jit(solution)/shard_map/ppermute | solution.py:329
  21.9 6.0 %collective-permute-start = (bf16[16,16,128]{2,1,0:T(8,128)(2,1)S(1)}, bf16[16,16,128]{2,1,0:T(8,128)(2,1)S(1)}, u32[]{:S(2)}, u32[]{:S(2)}) collective-permute-start(bf16[16,16,128]{2,1,0:T(8,128)(2,1)S(1)} %get-tuple-element.16.refs_0_), channel_id=1, source_target_pairs={{0,1},{1,0},{2,3},{3,2},{4,5},{5,4},{6,7},{7,6},{8,9},{9,8},{10,11... | collective-permute-start | bytes 196616 | tf_op jit(solution)/shard_map/ppermute | solution.py:329
  29.9 0.8 %copy-start.3 = (bf16[128,128]{1,0:T(8,128)(2,1)S(1)}, bf16[128,128]{1,0:T(8,128)(2,1)}, u32[]{:S(2)}) copy-start(bf16[128,128]{1,0:T(8,128)(2,1)} %refs_6_.1) | copy-start | bytes 98308
  30.2 0.7 %copy-start.5 = (bf16[128,4]{0,1:T(4,128)(2,1)S(1)}, bf16[128,4]{0,1:T(4,128)(2,1)}, u32[]{:S(2)}) copy-start(bf16[128,4]{0,1:T(4,128)(2,1)} %param.18) | copy-start | bytes 3076
  33.1 24.9 %copy-start.2 = (bf16[128,512]{1,0:T(8,128)(2,1)S(1)}, bf16[128,512]{1,0:T(8,128)(2,1)}, u32[]{:S(2)}) copy-start(bf16[128,512]{1,0:T(8,128)(2,1)} %refs_16_.1) | copy-start | bytes 393220
  33.1 26.1 %collective-permute-start.19 = (bf16[16,128,128]{2,1,0:T(8,128)(2,1)S(1)}, bf16[16,128,128]{2,1,0:T(8,128)(2,1)S(1)}, u32[]{:S(2)}, u32[]{:S(2)}) collective-permute-start(bf16[16,128,128]{2,1,0:T(8,128)(2,1)S(1)} %get-tuple-element.20.refs_13_), channel_id=1, source_target_pairs={{0,1},{1,0},{2,3},{3,2},{4,5},{5,4},{6,7},{7,6},{8,9},{9,8},{10,11... | collective-permute-start | bytes 1572872 | tf_op jit(solution)/shard_map/ppermute | solution.py:329
  34.9 12.4 %collective-permute-start.10 = (bf16[4,16,128]{2,1,0:T(8,128)(2,1)S(1)}, bf16[4,16,128]{2,1,0:T(8,128)(2,1)S(1)}, u32[]{:S(2)}, u32[]{:S(2)}) collective-permute-start(bf16[4,16,128]{2,1,0:T(8,128)(2,1)S(1)} %get-tuple-element.19), channel_id=1, source_target_pairs={{1,0},{3,2},{5,4},{7,6},{9,8},{11,10},{13,12},{15,14},{16,17},{18,... | collective-permute-start | bytes 49160 | tf_op jit(solution)/shard_map/ppermute | solution.py:329
  47.3 2.9 %collective-permute-start.11 = (bf16[2,4,16,128]{3,2,1,0:T(8,128)(2,1)S(1)}, bf16[2,4,16,128]{3,2,1,0:T(8,128)(2,1)S(1)}, u32[]{:S(2)}, u32[]{:S(2)}) collective-permute-start(bf16[2,4,16,128]{3,2,1,0:T(8,128)(2,1)S(1)} %pad_maximum_fusion), channel_id=1, source_target_pairs={{0,16},{2,18},{4,20},{6,22},{8,24},{10,26},{12,28},{14,30},{17,1},... | collective-permute-start | bytes 98312 | tf_op jit(solution)/shard_map/ppermute | solution.py:329
  50.2 3.9 %collective-permute-start.12 = (bf16[2,4,16,128]{3,2,1,0:T(8,128)(2,1)S(1)}, bf16[2,4,16,128]{3,2,1,0:T(8,128)(2,1)S(1)}, u32[]{:S(2)}, u32[]{:S(2)}) collective-permute-start(bf16[2,4,16,128]{3,2,1,0:T(8,128)(2,1)S(1)} %broadcast_select_fusion.refs_0_), channel_id=1, source_target_pairs={{0,8},{1,9},{2,10},{3,11},{4,12},{5,13},{6,14},{7,15},{8,0},{9,1},... | collective-permute-start | bytes 98312 | tf_op jit(solution)/shard_map/ppermute | solution.py:329
  52.0 4.1 %collective-permute-start.13 = (bf16[2,4,16,128]{3,2,1,0:T(8,128)(2,1)S(1)}, bf16[2,4,16,128]{3,2,1,0:T(8,128)(2,1)S(1)}, u32[]{:S(2)}, u32[]{:S(2)}) collective-permute-start(bf16[2,4,16,128]{3,2,1,0:T(8,128)(2,1)S(1)} %broadcast_select_fusion.refs_0_), channel_id=1, source_target_pairs={{0,4},{1,5},{2,6},{3,7},{4,0},{5,1},{6,2},{7,3},{8,12},{9,13},{10,... | collective-permute-start | bytes 98312 | tf_op jit(solution)/shard_map/ppermute | solution.py:329
  54.1 3.9 %collective-permute-start.14 = (bf16[2,4,16,128]{3,2,1,0:T(8,128)(2,1)S(1)}, bf16[2,4,16,128]{3,2,1,0:T(8,128)(2,1)S(1)}, u32[]{:S(2)}, u32[]{:S(2)}) collective-permute-start(bf16[2,4,16,128]{3,2,1,0:T(8,128)(2,1)S(1)} %collective-permute-done.12.refs_1_), channel_id=1, source_target_pairs={{0,4},{1,5},{2,6},{3,7},{4,0},{5,1},{6,2},{7,3},{8,12},{9,13},{10,... | collective-permute-start | bytes 98312 | tf_op jit(solution)/shard_map/ppermute | solution.py:329
  55.6 3.1 %collective-permute-start.15 = (bf16[2,4,16,128]{3,2,1,0:T(8,128)(2,1)S(1)}, bf16[2,4,16,128]{3,2,1,0:T(8,128)(2,1)S(1)}, u32[]{:S(2)}, u32[]{:S(2)}) collective-permute-start(bf16[2,4,16,128]{3,2,1,0:T(8,128)(2,1)S(1)} %broadcast_select_fusion.refs_0_), channel_id=1, source_target_pairs={{0,2},{1,3},{2,0},{3,1},{4,6},{5,7},{6,4},{7,5},{8,10},{9,11},{10,... | collective-permute-start | bytes 98312 | tf_op jit(solution)/shard_map/ppermute | solution.py:329
  55.6 3.2 %collective-permute-start.16 = (bf16[2,4,16,128]{3,2,1,0:T(8,128)(2,1)S(1)}, bf16[2,4,16,128]{3,2,1,0:T(8,128)(2,1)S(1)}, u32[]{:S(2)}, u32[]{:S(2)}) collective-permute-start(bf16[2,4,16,128]{3,2,1,0:T(8,128)(2,1)S(1)} %collective-permute-done.12.refs_1_), channel_id=1, source_target_pairs={{0,2},{1,3},{2,0},{3,1},{4,6},{5,7},{6,4},{7,5},{8,10},{9,11},{10,... | collective-permute-start | bytes 98312 | tf_op jit(solution)/shard_map/ppermute | solution.py:329
  56.1 2.6 %collective-permute-start.17 = (bf16[2,4,16,128]{3,2,1,0:T(8,128)(2,1)S(1)}, bf16[2,4,16,128]{3,2,1,0:T(8,128)(2,1)S(1)}, u32[]{:S(2)}, u32[]{:S(2)}) collective-permute-start(bf16[2,4,16,128]{3,2,1,0:T(8,128)(2,1)S(1)} %collective-permute-done.13.refs_2_), channel_id=1, source_target_pairs={{0,2},{1,3},{2,0},{3,1},{4,6},{5,7},{6,4},{7,5},{8,10},{9,11},{10,... | collective-permute-start | bytes 98312 | tf_op jit(solution)/shard_map/ppermute | solution.py:329
  58.0 1.2 %collective-permute-start.18 = (bf16[2,4,16,128]{3,2,1,0:T(8,128)(2,1)S(1)}, bf16[2,4,16,128]{3,2,1,0:T(8,128)(2,1)S(1)}, u32[]{:S(2)}, u32[]{:S(2)}) collective-permute-start(bf16[2,4,16,128]{3,2,1,0:T(8,128)(2,1)S(1)} %collective-permute-done.14.refs_3_), channel_id=1, source_target_pairs={{0,2},{1,3},{2,0},{3,1},{4,6},{5,7},{6,4},{7,5},{8,10},{9,11},{10,... | collective-permute-start | bytes 98312 | tf_op jit(solution)/shard_map/ppermute | solution.py:329
  58.0 1.2 %copy-start.4 = (bf16[128,128]{1,0:T(8,128)(2,1)S(1)}, bf16[128,128]{1,0:T(8,128)(2,1)}, u32[]{:S(2)}) copy-start(bf16[128,128]{1,0:T(8,128)(2,1)} %refs_17_.1) | copy-start | bytes 98308

commit v4 on v3

--- a/solution.py
+++ b/solution.py
@@ -214,14 +214,38 @@
     lax.fori_loop(0, rows // step, body, 0, unroll=unroll_of(rows // step, cols))
 
 
+def make_spread_kernel(n_col):
+    def kernel(*refs):
+        others = refs[: n_col - 1]
+        k_ref, v_ref, gains_ref, kv_w_ref, keys_ref, values_ref = refs[n_col - 1 :]
+        rows, cols, width = k_ref.shape
+        step = 2
+
+        def spread(t, carry):
+            at = pl.ds(t * step, step)
+            keys_ref[at, 0:cols] = k_ref[at]
+            values_ref[at, 0:cols] = v_ref[at]
+            for d in range(n_col - 1):
+                there = others[d][at].reshape(step * cols, width).astype(F32)
+                normed = layer_norm(there, gains_ref[1:2, :]).astype(BF16)
+                kv = dot(normed, kv_w_ref[:, width : 3 * width]).astype(BF16)
+                low = (d + 1) * cols
+                keys_ref[at, low : low + cols] = kv[:, :width].reshape(step, cols, width)
+                values_ref[at, low : low + cols] = kv[:, width:].reshape(step, cols, width)
+            return carry
+
+        lax.fori_loop(0, rows // step, spread, 0, unroll=unroll_of(rows // step, cols))
+
+    return kernel
+
+
 def make_attend_kernel(n_col, n_blk, place):
     def kernel(*refs):
         biases = refs[:n_blk]
-        others = refs[n_blk : n_blk + n_col - 1]
-        q_ref, k_ref, v_ref, gate_ref, mid_ref, gains_ref, live_ref, kv_w_ref, out_w_ref = refs[
-            n_blk + n_col - 1 : n_blk + n_col + 8
+        q_ref, keys_ref, values_ref, gate_ref, mid_ref, live_ref, out_w_ref = refs[
+            n_blk : n_blk + 7
         ]
-        out_ref, bias_ref, keys_ref, values_ref = refs[n_blk + n_col + 8 :]
+        out_ref, bias_ref = refs[n_blk + 7 :]
         rows, cols, width = q_ref.shape
         blk = biases[0].shape[2]
         for d in range(n_col):
@@ -239,21 +263,6 @@
         ones = jnp.ones((n_col * cols, width), BF16)
 
         step = 2
-
-        def spread(t, carry):
-            at = pl.ds(t * step, step)
-            keys_ref[at, 0:cols] = k_ref[at]
-            values_ref[at, 0:cols] = v_ref[at]
-            for d in range(n_col - 1):
-                there = others[d][at].reshape(step * cols, width).astype(F32)
-                normed = layer_norm(there, gains_ref[1:2, :]).astype(BF16)
-                kv = dot(normed, kv_w_ref[:, width : 3 * width]).astype(BF16)
-                low = (d + 1) * cols
-                keys_ref[at, low : low + cols] = kv[:, :width].reshape(step, cols, width)
-                values_ref[at, low : low + cols] = kv[:, width:].reshape(step, cols, width)
-            return carry
-
-        lax.fori_loop(0, rows // step, spread, 0, unroll=unroll_of(rows // step, cols))
 
         def attend(i, carry):
             key = keys_ref[i]
@@ -368,8 +377,12 @@
         bit = self.n_blk // 2
         while bit:
             moved = []
-            for block in blocks:
-                moved.append(self.flip_row(block, bit))
+            for at, block in enumerate(blocks):
+                far_bits = bit ^ self.offsets[at]
+                if relay and bit > 1:
+                    moved.append(self.flip_row(pair, far_bits))
+                else:
+                    moved.append(self.flip_row(block, bit))
             blocks = blocks + moved
             bit //= 2
         return blocks
@@ -456,31 +469,19 @@
         query, key, value, att_gate = call(
             project_kernel, (wide, wide, wide, jax.ShapeDtypeStruct(whole, F32)), 0, 2, limit
         )(normed, att_in)
+        all_keys = jax.ShapeDtypeStruct((rows, n_col * cols, width), BF16)
+        keys, values = call(
+            make_spread_kernel(n_col), (all_keys, all_keys), 0, n_col + 3, limit
+        )(*others, key, value, gains, att_in)
         return call(
             make_attend_kernel(n_col, n_blk, grid.place),
             wide,
             0,
-            n_blk + n_col - 1 + 9,
+            n_blk + 7,
             limit,
-            [
-                pltpu.VMEM((H * cols, n_col * cols), F32),
-                pltpu.VMEM((rows, n_col * cols, width), BF16),
-                pltpu.VMEM((rows, n_col * cols, width), BF16),
-            ],
+            [pltpu.VMEM((H * cols, n_col * cols), F32)],
             held_out=False,
-        )(
-            *biases,
-            *others,
-            query,
-            key,
-            value,
-            att_gate,
-            mid,
-            gains,
-            live,
-            att_in,
-            att_out,
-        )
+        )(*biases, query, keys, values, att_gate, mid, live, att_out)
 
     return body
 

time: 65.5 us -> 65.6 us (level); the launches traced: 64.3 us -> 65.4 us
  waiting for transfers between devices: 24.8 us -> 25.9 us
    ppermute x20, waiting for transfers between devices: 24.8 us -> 25.9 us  [move(): return lax.ppermute(value, ('row', 'col'), pairs)]
    pallas_call x7 -> x8, Pallas kernels: 11.2 us -> 11.3 us  [apply(): return run(*args[:n_smem], *held)]
  transfers between devices with their start and end apart: 20 -> 20, of which waited for: 10 -> 9; matrix products, arithmetic and copies ran while one was open for 0% -> 0% of each run, Pallas kernels for 6% -> 7%
where the time goes in v4:
time: 65.6 us; the launch traced here: 65.4 us
  waiting for transfers between devices  25.9 us (39%)
  starting transfers between devices  25.2 us (38%)
  Pallas kernels  13.4 us (20%)
  local copies, waits for them, and re-layouts  0.69 us (1%)
    ppermute x20, waiting for transfers between devices, move(): return lax.ppermute(value, ('row', 'col'), pairs)  25.9 us
    ppermute x20, starting transfers between devices, move(): return lax.ppermute(value, ('row', 'col'), pairs)  25.2 us
    pallas_call x8, Pallas kernels, apply(): return run(*args[:n_smem], *held)  11.3 us
    pallas_call x1, Pallas kernels, body(): pl.pallas_call(make_edge_kernel(cols, n_col, grid.col_of), name='edges',...  2.11 us
  transfers between devices with their start and end apart: 20, of which 9 were waited for; matrix products, arithmetic and copies ran while one was open for 0% of the time, Pallas kernels for 7%

profile of v4, /device:TPU:0, one launch (start us, length us, event | category | flops | bytes accessed | tf_op | source)
XLA Modules:
  0.0 65.4 jit_solution(5982925311405605044)
XLA Ops:
  0.0 2.1 %edges.1 = (bf16[16,16,128]{2,1,0:T(8,128)(2,1)S(1)}, bf16[16,16,128]{2,1,0:T(8,128)(2,1)S(1)}, f32[3,128]{1,0:T(4,128)S(1)}, f32[1,256]{1,0:T(1,128)S(1)}) custom-call(s32[4]{0:T(128)} %len_ref.1, bf16[16,128,128]{2,1,0:T(8,128)(2,1)} %refs_3_.1, f32[1,128]{1,0:T(1,128)} %bitcast.17, f32[1,128]{1,0:T(1,128)} %bitcast.18, f32[1,128]{1,0:T(1,128)} %bitcast.19, ...), custom_call_target="tpu_custom_call" | custom-call | tf_op jit(solution)/shard_map/edges/pallas_call | solution.py:407
  2.1 4.1 %collective-permute-start.1 = (bf16[16,16,128]{2,1,0:T(8,128)(2,1)S(1)}, bf16[16,16,128]{2,1,0:T(8,128)(2,1)S(1)}, u32[]{:S(2)}, u32[]{:S(2)}) collective-permute-start(bf16[16,16,128]{2,1,0:T(8,128)(2,1)S(1)} %get-tuple-element.19), channel_id=1, source_target_pairs={{0,16},{1,0},{2,18},{3,2},{4,20},{5,4},{6,22},{7,6},{8,24},{9,8},{... | collective-permute-start | bytes 196616 | tf_op jit(solution)/shard_map/ppermute | solution.py:338
  6.2 0.7 collective-permute-start.2
  6.9 1.2 %collective-permute-done.1 = bf16[16,16,128]{2,1,0:T(8,128)(2,1)S(1)} collective-permute-done((bf16[16,16,128]{2,1,0:T(8,128)(2,1)S(1)}, bf16[16,16,128]{2,1,0:T(8,128)(2,1)S(1)}, u32[]{:S(2)}, u32[]{:S(2)}) %collective-permute-start.1) | collective-permute-done | bytes 65568 | tf_op jit(solution)/shard_map/ppermute | solution.py:338
  8.1 0.0 collective-permute-done.2
  8.2 2.4 %collective-permute-start.3 = (bf16[2,16,16,128]{3,2,1,0:T(8,128)(2,1)S(1)}, bf16[2,16,16,128]{3,2,1,0:T(8,128)(2,1)S(1)}, u32[]{:S(2)}, u32[]{:S(2)}) collective-permute-start(bf16[2,16,16,128]{3,2,1,0:T(8,128)(2,1)S(1)} %maximum_select_fusion.refs_2_), channel_id=1, source_target_pairs={{0,8},{1,9},{2,10},{3,11},{4,12},{5,13},{6,14},{7,15},{8,0},{9,1},... | collective-permute-start | bytes 393224 | tf_op jit(solution)/shard_map/ppermute | solution.py:338
  10.6 1.5 %collective-permute-start.6 = (bf16[2,16,16,128]{3,2,1,0:T(8,128)(2,1)S(1)}, bf16[2,16,16,128]{3,2,1,0:T(8,128)(2,1)S(1)}, u32[]{:S(2)}, u32[]{:S(2)}) collective-permute-start(bf16[2,16,16,128]{3,2,1,0:T(8,128)(2,1)S(1)} %maximum_select_fusion.refs_2_), channel_id=1, source_target_pairs={{0,4},{1,5},{2,6},{3,7},{4,0},{5,1},{6,2},{7,3},{8,12},{9,13},{10,... | collective-permute-start | bytes 393224 | tf_op jit(solution)/shard_map/ppermute | solution.py:338
  12.0 2.4 %collective-permute-done.3.refs_4_ = bf16[2,16,16,128]{3,2,1,0:T(8,128)(2,1)S(1)} collective-permute-done((bf16[2,16,16,128]{3,2,1,0:T(8,128)(2,1)S(1)}, bf16[2,16,16,128]{3,2,1,0:T(8,128)(2,1)S(1)}, u32[]{:S(2)}, u32[]{:S(2)}) %collective-permute-start.3) | collective-permute-done | bytes 131104 | tf_op jit(solution)/shard_map/ppermute | solution.py:338
  14.5 1.5 %collective-permute-start.4 = (bf16[2,16,16,128]{3,2,1,0:T(8,128)(2,1)S(1)}, bf16[2,16,16,128]{3,2,1,0:T(8,128)(2,1)S(1)}, u32[]{:S(2)}, u32[]{:S(2)}) collective-permute-start(bf16[2,16,16,128]{3,2,1,0:T(8,128)(2,1)S(1)} %collective-permute-done.3.refs_4_), channel_id=1, source_target_pairs={{0,4},{1,5},{2,6},{3,7},{4,0},{5,1},{6,2},{7,3},{8,12},{9,13},{10,... | collective-permute-start | bytes 393224 | tf_op jit(solution)/shard_map/ppermute | solution.py:338
  16.0 0.0 collective-permute-start.8
  16.0 0.5 collective-permute-start.9
  16.5 0.0 collective-permute-done.6.refs_2_
  16.5 0.0 collective-permute-start.7
  16.5 3.0 %collective-permute-done.4.refs_2_ = bf16[2,16,16,128]{3,2,1,0:T(8,128)(2,1)S(1)} collective-permute-done((bf16[2,16,16,128]{3,2,1,0:T(8,128)(2,1)S(1)}, bf16[2,16,16,128]{3,2,1,0:T(8,128)(2,1)S(1)}, u32[]{:S(2)}, u32[]{:S(2)}) %collective-permute-start.4) | collective-permute-done | bytes 131104 | tf_op jit(solution)/shard_map/ppermute | solution.py:338
  19.4 0.0 collective-permute-start.5
  19.4 4.6 %collective-permute-start = (bf16[16,16,128]{2,1,0:T(8,128)(2,1)S(1)}, bf16[16,16,128]{2,1,0:T(8,128)(2,1)S(1)}, u32[]{:S(2)}, u32[]{:S(2)}) collective-permute-start(bf16[16,16,128]{2,1,0:T(8,128)(2,1)S(1)} %get-tuple-element.18.refs_0_), channel_id=1, source_target_pairs={{0,1},{1,0},{2,3},{3,2},{4,5},{5,4},{6,7},{7,6},{8,9},{9,8},{10,11... | collective-permute-start | bytes 196616 | tf_op jit(solution)/shard_map/ppermute | solution.py:338
  24.1 0.9 %shard_map.100.refs_4_ = f32[16,128,128]{2,1,0:T(8,128)S(1)} custom-call(bf16[16,128,128]{2,1,0:T(8,128)(2,1)S(1)} %copy-done, f32[3,128]{1,0:T(4,128)S(1)} %get-tuple-element.20.gains_ref.refs_5_.refs_3_, bf16[128,640]{1,0:T(8,128)(2,1)S(1)} %copy-done.1), custom_call_target="tpu_custom_call" | custom-call | tf_op jit(solution)/shard_map/pallas_call | solution.py:69
  25.0 1.8 %collective-permute-done.refs_1_ = bf16[16,16,128]{2,1,0:T(8,128)(2,1)S(1)} collective-permute-done((bf16[16,16,128]{2,1,0:T(8,128)(2,1)S(1)}, bf16[16,16,128]{2,1,0:T(8,128)(2,1)S(1)}, u32[]{:S(2)}, u32[]{:S(2)}) %collective-permute-start) | collective-permute-done | bytes 65568 | tf_op jit(solution)/shard_map/ppermute | solution.py:338
  26.8 0.0 collective-permute-done.9.refs_5_
  26.8 1.3 %shard_map.101.refs_4_ = f32[16,128,128]{2,1,0:T(8,128)S(1)} custom-call(bf16[16,16,128]{2,1,0:T(8,128)(2,1)S(1)} %get-tuple-element.18.refs_0_, bf16[16,16,128]{2,1,0:T(8,128)(2,1)S(1)} %collective-permute-done.refs_1_, bf16[2,16,16,128]{3,2,1,0:T(8,128)(2,1)S(1)} %maximum_select_fusion.refs_2_, ...), custom_call_target="tpu_custom_call" | custom-call | tf_op jit(solution)/shard_map/pallas_call | solution.py:69
  28.2 0.0 collective-permute-done.7.refs_3_
  28.2 0.7 %shard_map.102.refs_3_ = f32[16,128,128]{2,1,0:T(8,128)S(1)} custom-call(bf16[16,16,128]{2,1,0:T(8,128)(2,1)S(1)} %get-tuple-element.18.refs_0_, bf16[16,16,128]{2,1,0:T(8,128)(2,1)S(1)} %collective-permute-done.refs_1_, bf16[2,16,16,128]{3,2,1,0:T(8,128)(2,1)S(1)} %collective-permute-done.6.refs_2_, ...), custom_call_target="tpu_custom_call", output_to_operand_aliasing={{}: (4, {})} | custom-call | tf_op jit(solution)/shard_map/pallas_call | solution.py:69
  28.8 0.3 shard_map.103.refs_8_
  29.2 0.0 copy-start.5
  29.2 0.4 copy-done.3
  29.6 0.3 copy-done.5
  29.9 2.2 %shard_map.104 = (bf16[16,128,128]{2,1,0:T(8,128)(2,1)S(1)}, bf16[16,128,128]{2,1,0:T(8,128)(2,1)S(1)}, bf16[4,16,128]{2,1,0:T(8,128)(2,1)S(1)}, f32[16,128,128]{2,1,0:T(8,128)S(1)}) custom-call(bf16[16,16,128]{2,1,0:T(8,128)(2,1)S(1)} %get-tuple-element.18.refs_0_, ...), custom_call_target="tpu_custom_call", output_to_operand_aliasing={{3}: (8, {})} | custom-call | tf_op jit(solution)/shard_map/pallas_call | solution.py:69
  32.0 0.0 copy-start.2
  32.1 1.8 %collective-permute-start.19 = (bf16[16,128,128]{2,1,0:T(8,128)(2,1)S(1)}, bf16[16,128,128]{2,1,0:T(8,128)(2,1)S(1)}, u32[]{:S(2)}, u32[]{:S(2)}) collective-permute-start(bf16[16,128,128]{2,1,0:T(8,128)(2,1)S(1)} %get-tuple-element.24.refs_12_), channel_id=1, source_target_pairs={{0,1},{1,0},{2,3},{3,2},{4,5},{5,4},{6,7},{7,6},{8,9},{9,8},{10,11... | collective-permute-start | bytes 1572872 | tf_op jit(solution)/shard_map/ppermute | solution.py:338
  33.9 1.3 %collective-permute-start.10 = (bf16[4,16,128]{2,1,0:T(8,128)(2,1)S(1)}, bf16[4,16,128]{2,1,0:T(8,128)(2,1)S(1)}, u32[]{:S(2)}, u32[]{:S(2)}) collective-permute-start(bf16[4,16,128]{2,1,0:T(8,128)(2,1)S(1)} %get-tuple-element.21), channel_id=1, source_target_pairs={{1,0},{3,2},{5,4},{7,6},{9,8},{11,10},{13,12},{15,14},{16,17},{18,... | collective-permute-start | bytes 49160 | tf_op jit(solution)/shard_map/ppermute | solution.py:338
  35.1 11.1 %collective-permute-done.10 = bf16[4,16,128]{2,1,0:T(8,128)(2,1)S(1)} collective-permute-done((bf16[4,16,128]{2,1,0:T(8,128)(2,1)S(1)}, bf16[4,16,128]{2,1,0:T(8,128)(2,1)S(1)}, u32[]{:S(2)}, u32[]{:S(2)}) %collective-permute-start.10) | collective-permute-done | bytes 16416 | tf_op jit(solution)/shard_map/ppermute | solution.py:338
  46.2 3.2 %collective-permute-start.11 = (bf16[2,4,16,128]{3,2,1,0:T(8,128)(2,1)S(1)}, bf16[2,4,16,128]{3,2,1,0:T(8,128)(2,1)S(1)}, u32[]{:S(2)}, u32[]{:S(2)}) collective-permute-start(bf16[2,4,16,128]{3,2,1,0:T(8,128)(2,1)S(1)} %pad_maximum_fusion), channel_id=1, source_target_pairs={{0,16},{2,18},{4,20},{6,22},{8,24},{10,26},{12,28},{14,30},{17,1},... | collective-permute-start | bytes 98312 | tf_op jit(solution)/shard_map/ppermute | solution.py:338
  49.5 1.6 %collective-permute-done.11 = bf16[2,4,16,128]{3,2,1,0:T(8,128)(2,1)S(1)} collective-permute-done((bf16[2,4,16,128]{3,2,1,0:T(8,128)(2,1)S(1)}, bf16[2,4,16,128]{3,2,1,0:T(8,128)(2,1)S(1)}, u32[]{:S(2)}, u32[]{:S(2)}) %collective-permute-start.11) | collective-permute-done | bytes 32800 | tf_op jit(solution)/shard_map/ppermute | solution.py:338
  51.1 2.0 %collective-permute-start.12 = (bf16[2,4,16,128]{3,2,1,0:T(8,128)(2,1)S(1)}, bf16[2,4,16,128]{3,2,1,0:T(8,128)(2,1)S(1)}, u32[]{:S(2)}, u32[]{:S(2)}) collective-permute-start(bf16[2,4,16,128]{3,2,1,0:T(8,128)(2,1)S(1)} %broadcast_select_fusion.refs_0_), channel_id=1, source_target_pairs={{0,8},{1,9},{2,10},{3,11},{4,12},{5,13},{6,14},{7,15},{8,0},{9,1},... | collective-permute-start | bytes 98312 | tf_op jit(solution)/shard_map/ppermute | solution.py:338
  53.1 1.5 %collective-permute-start.13 = (bf16[2,4,16,128]{3,2,1,0:T(8,128)(2,1)S(1)}, bf16[2,4,16,128]{3,2,1,0:T(8,128)(2,1)S(1)}, u32[]{:S(2)}, u32[]{:S(2)}) collective-permute-start(bf16[2,4,16,128]{3,2,1,0:T(8,128)(2,1)S(1)} %broadcast_select_fusion.refs_0_), channel_id=1, source_target_pairs={{0,4},{1,5},{2,6},{3,7},{4,0},{5,1},{6,2},{7,3},{8,12},{9,13},{10,... | collective-permute-start | bytes 98312 | tf_op jit(solution)/shard_map/ppermute | solution.py:338
  54.6 0.0 collective-permute-start.14
  54.6 0.0 collective-permute-start.15
  54.6 0.5 collective-permute-done.12.refs_1_
  55.2 0.0 collective-permute-start.16
  55.2 1.8 %collective-permute-done.13.refs_2_ = bf16[2,4,16,128]{3,2,1,0:T(8,128)(2,1)S(1)} collective-permute-done((bf16[2,4,16,128]{3,2,1,0:T(8,128)(2,1)S(1)}, bf16[2,4,16,128]{3,2,1,0:T(8,128)(2,1)S(1)}, u32[]{:S(2)}, u32[]{:S(2)}) %collective-permute-start.13) | collective-permute-done | bytes 32800 | tf_op jit(solution)/shard_map/ppermute | solution.py:338
  57.0 2.4 %collective-permute-done.14.refs_3_ = bf16[2,4,16,128]{3,2,1,0:T(8,128)(2,1)S(1)} collective-permute-done((bf16[2,4,16,128]{3,2,1,0:T(8,128)(2,1)S(1)}, bf16[2,4,16,128]{3,2,1,0:T(8,128)(2,1)S(1)}, u32[]{:S(2)}, u32[]{:S(2)}) %collective-permute-start.14) | collective-permute-done | bytes 32800 | tf_op jit(solution)/shard_map/ppermute | solution.py:338
  59.4 0.0 collective-permute-start.18
  59.4 0.7 %shard_map.105 = (bf16[16,128,128]{2,1,0:T(8,128)(2,1)S(1)}, bf16[16,128,128]{2,1,0:T(8,128)(2,1)S(1)}, bf16[16,128,128]{2,1,0:T(8,128)(2,1)S(1)}, f32[16,128,128]{2,1,0:T(8,128)S(1)}) custom-call(bf16[16,128,128]{2,1,0:T(8,128)(2,1)S(1)} %get-tuple-element.22.norm_ref, bf16[128,512]{1,0:T(8,128)(2,1)S(1)} %copy-done.2), custom_call_target="tpu_custom_call" | custom-call | tf_op jit(solution)/shard_map/pallas_call | solution.py:69
  60.1 0.0 collective-permute-done.19.refs_0_
  60.1 0.0 copy-start.4
  60.1 0.9 %shard_map.106 = (bf16[16,256,128]{2,1,0:T(8,128)(2,1)S(1)}, bf16[16,256,128]{2,1,0:T(8,128)(2,1)S(1)}) custom-call(bf16[16,128,128]{2,1,0:T(8,128)(2,1)S(1)} %collective-permute-done.19.refs_0_, bf16[16,128,128]{2,1,0:T(8,128)(2,1)S(1)} %get-tuple-element.25.refs_1_, bf16[16,128,128]{2,1,0:T(8,128)(2,1)S(1)} %get-tuple-element.26.refs_2_, ...), custom_call_target="tpu_custom_call" | custom-call | tf_op jit(solution)/shard_map/pallas_call | solution.py:69
  61.1 0.0 collective-permute-done.16.refs_5_
  61.1 4.2 %shard_map.107 = bf16[16,128,128]{2,1,0:T(8,128)(2,1)} custom-call(bf16[2,4,16,128]{3,2,1,0:T(8,128)(2,1)S(1)} %broadcast_select_fusion.refs_0_, bf16[2,4,16,128]{3,2,1,0:T(8,128)(2,1)S(1)} %collective-permute-done.12.refs_1_, bf16[2,4,16,128]{3,2,1,0:T(8,128)(2,1)S(1)} %collective-permute-done.13.refs_2_, ...), custom_call_target="tpu_custom_call" | custom-call | tf_op jit(solution)/shard_map/pallas_call | solution.py:69
  (16 shorter events, 0.1 us)
Async XLA Ops:
  0.0 24.1 %copy-start = (bf16[16,128,128]{2,1,0:T(8,128)(2,1)S(1)}, bf16[16,128,128]{2,1,0:T(8,128)(2,1)}, u32[]{:S(2)}) copy-start(bf16[16,128,128]{2,1,0:T(8,128)(2,1)} %refs_3_.1) | copy-start | bytes 1572868
  2.1 6.0 %collective-permute-start.1 = (bf16[16,16,128]{2,1,0:T(8,128)(2,1)S(1)}, bf16[16,16,128]{2,1,0:T(8,128)(2,1)S(1)}, u32[]{:S(2)}, u32[]{:S(2)}) collective-permute-start(bf16[16,16,128]{2,1,0:T(8,128)(2,1)S(1)} %get-tuple-element.19), channel_id=1, source_target_pairs={{0,16},{1,0},{2,18},{3,2},{4,20},{5,4},{6,22},{7,6},{8,24},{9,8},{... | collective-permute-start | bytes 196616 | tf_op jit(solution)/shard_map/ppermute | solution.py:338
  6.2 1.9 %collective-permute-start.2 = (bf16[16,16,128]{2,1,0:T(8,128)(2,1)S(1)}, bf16[16,16,128]{2,1,0:T(8,128)(2,1)S(1)}, u32[]{:S(2)}, u32[]{:S(2)}) collective-permute-start(bf16[16,16,128]{2,1,0:T(8,128)(2,1)S(1)} %get-tuple-element.19), channel_id=1, source_target_pairs={{1,16},{3,18},{5,20},{7,22},{9,24},{11,26},{13,28},{15,30},{16,1},... | collective-permute-start | bytes 196616 | tf_op jit(solution)/shard_map/ppermute | solution.py:338
  8.1 15.9 %copy-start.1 = (bf16[128,640]{1,0:T(8,128)(2,1)S(1)}, bf16[128,640]{1,0:T(8,128)(2,1)}, u32[]{:S(2)}) copy-start(bf16[128,640]{1,0:T(8,128)(2,1)} %w_ref.4) | copy-start | bytes 491524
  8.2 6.3 %collective-permute-start.3 = (bf16[2,16,16,128]{3,2,1,0:T(8,128)(2,1)S(1)}, bf16[2,16,16,128]{3,2,1,0:T(8,128)(2,1)S(1)}, u32[]{:S(2)}, u32[]{:S(2)}) collective-permute-start(bf16[2,16,16,128]{3,2,1,0:T(8,128)(2,1)S(1)} %maximum_select_fusion.refs_2_), channel_id=1, source_target_pairs={{0,8},{1,9},{2,10},{3,11},{4,12},{5,13},{6,14},{7,15},{8,0},{9,1},... | collective-permute-start | bytes 393224 | tf_op jit(solution)/shard_map/ppermute | solution.py:338
  10.6 5.9 %collective-permute-start.6 = (bf16[2,16,16,128]{3,2,1,0:T(8,128)(2,1)S(1)}, bf16[2,16,16,128]{3,2,1,0:T(8,128)(2,1)S(1)}, u32[]{:S(2)}, u32[]{:S(2)}) collective-permute-start(bf16[2,16,16,128]{3,2,1,0:T(8,128)(2,1)S(1)} %maximum_select_fusion.refs_2_), channel_id=1, source_target_pairs={{0,4},{1,5},{2,6},{3,7},{4,0},{5,1},{6,2},{7,3},{8,12},{9,13},{10,... | collective-permute-start | bytes 393224 | tf_op jit(solution)/shard_map/ppermute | solution.py:338
  14.5 5.0 %collective-permute-start.4 = (bf16[2,16,16,128]{3,2,1,0:T(8,128)(2,1)S(1)}, bf16[2,16,16,128]{3,2,1,0:T(8,128)(2,1)S(1)}, u32[]{:S(2)}, u32[]{:S(2)}) collective-permute-start(bf16[2,16,16,128]{3,2,1,0:T(8,128)(2,1)S(1)} %collective-permute-done.3.refs_4_), channel_id=1, source_target_pairs={{0,4},{1,5},{2,6},{3,7},{4,0},{5,1},{6,2},{7,3},{8,12},{9,13},{10,... | collective-permute-start | bytes 393224 | tf_op jit(solution)/shard_map/ppermute | solution.py:338
  16.0 10.9 %collective-permute-start.8 = (bf16[2,16,16,128]{3,2,1,0:T(8,128)(2,1)S(1)}, bf16[2,16,16,128]{3,2,1,0:T(8,128)(2,1)S(1)}, u32[]{:S(2)}, u32[]{:S(2)}) collective-permute-start(bf16[2,16,16,128]{3,2,1,0:T(8,128)(2,1)S(1)} %maximum_select_fusion.refs_2_), channel_id=1, source_target_pairs={{0,2},{1,3},{2,0},{3,1},{4,6},{5,7},{6,4},{7,5},{8,10},{9,11},{10,... | collective-permute-start | bytes 393224 | tf_op jit(solution)/shard_map/ppermute | solution.py:338
  16.0 10.9 %collective-permute-start.9 = (bf16[2,16,16,128]{3,2,1,0:T(8,128)(2,1)S(1)}, bf16[2,16,16,128]{3,2,1,0:T(8,128)(2,1)S(1)}, u32[]{:S(2)}, u32[]{:S(2)}) collective-permute-start(bf16[2,16,16,128]{3,2,1,0:T(8,128)(2,1)S(1)} %collective-permute-done.3.refs_4_), channel_id=1, source_target_pairs={{0,2},{1,3},{2,0},{3,1},{4,6},{5,7},{6,4},{7,5},{8,10},{9,11},{10,... | collective-permute-start | bytes 393224 | tf_op jit(solution)/shard_map/ppermute | solution.py:338
  16.5 11.7 %collective-permute-start.7 = (bf16[2,16,16,128]{3,2,1,0:T(8,128)(2,1)S(1)}, bf16[2,16,16,128]{3,2,1,0:T(8,128)(2,1)S(1)}, u32[]{:S(2)}, u32[]{:S(2)}) collective-permute-start(bf16[2,16,16,128]{3,2,1,0:T(8,128)(2,1)S(1)} %collective-permute-done.6.refs_2_), channel_id=1, source_target_pairs={{0,2},{1,3},{2,0},{3,1},{4,6},{5,7},{6,4},{7,5},{8,10},{9,11},{10,... | collective-permute-start | bytes 393224 | tf_op jit(solution)/shard_map/ppermute | solution.py:338
  19.4 9.8 %collective-permute-start.5 = (bf16[2,16,16,128]{3,2,1,0:T(8,128)(2,1)S(1)}, bf16[2,16,16,128]{3,2,1,0:T(8,128)(2,1)S(1)}, u32[]{:S(2)}, u32[]{:S(2)}) collective-permute-start(bf16[2,16,16,128]{3,2,1,0:T(8,128)(2,1)S(1)} %collective-permute-done.4.refs_2_), channel_id=1, source_target_pairs={{0,2},{1,3},{2,0},{3,1},{4,6},{5,7},{6,4},{7,5},{8,10},{9,11},{10,... | collective-permute-start | bytes 393224 | tf_op jit(solution)/shard_map/ppermute | solution.py:338
  19.4 7.4 %collective-permute-start = (bf16[16,16,128]{2,1,0:T(8,128)(2,1)S(1)}, bf16[16,16,128]{2,1,0:T(8,128)(2,1)S(1)}, u32[]{:S(2)}, u32[]{:S(2)}) collective-permute-start(bf16[16,16,128]{2,1,0:T(8,128)(2,1)S(1)} %get-tuple-element.18.refs_0_), channel_id=1, source_target_pairs={{0,1},{1,0},{2,3},{3,2},{4,5},{5,4},{6,7},{7,6},{8,9},{9,8},{10,11... | collective-permute-start | bytes 196616 | tf_op jit(solution)/shard_map/ppermute | solution.py:338
  28.8 0.8 %copy-start.3 = (bf16[128,128]{1,0:T(8,128)(2,1)S(1)}, bf16[128,128]{1,0:T(8,128)(2,1)}, u32[]{:S(2)}) copy-start(bf16[128,128]{1,0:T(8,128)(2,1)} %refs_6_.1) | copy-start | bytes 98308
  29.2 0.7 %copy-start.5 = (bf16[128,4]{0,1:T(4,128)(2,1)S(1)}, bf16[128,4]{0,1:T(4,128)(2,1)}, u32[]{:S(2)}) copy-start(bf16[128,4]{0,1:T(4,128)(2,1)} %param.18) | copy-start | bytes 3076
  32.0 27.4 %copy-start.2 = (bf16[128,512]{1,0:T(8,128)(2,1)S(1)}, bf16[128,512]{1,0:T(8,128)(2,1)}, u32[]{:S(2)}) copy-start(bf16[128,512]{1,0:T(8,128)(2,1)} %refs_4_.1) | copy-start | bytes 393220
  32.1 28.1 %collective-permute-start.19 = (bf16[16,128,128]{2,1,0:T(8,128)(2,1)S(1)}, bf16[16,128,128]{2,1,0:T(8,128)(2,1)S(1)}, u32[]{:S(2)}, u32[]{:S(2)}) collective-permute-start(bf16[16,128,128]{2,1,0:T(8,128)(2,1)S(1)} %get-tuple-element.24.refs_12_), channel_id=1, source_target_pairs={{0,1},{1,0},{2,3},{3,2},{4,5},{5,4},{6,7},{7,6},{8,9},{9,8},{10,11... | collective-permute-start | bytes 1572872 | tf_op jit(solution)/shard_map/ppermute | solution.py:338
  33.9 12.4 %collective-permute-start.10 = (bf16[4,16,128]{2,1,0:T(8,128)(2,1)S(1)}, bf16[4,16,128]{2,1,0:T(8,128)(2,1)S(1)}, u32[]{:S(2)}, u32[]{:S(2)}) collective-permute-start(bf16[4,16,128]{2,1,0:T(8,128)(2,1)S(1)} %get-tuple-element.21), channel_id=1, source_target_pairs={{1,0},{3,2},{5,4},{7,6},{9,8},{11,10},{13,12},{15,14},{16,17},{18,... | collective-permute-start | bytes 49160 | tf_op jit(solution)/shard_map/ppermute | solution.py:338
  46.2 4.8 %collective-permute-start.11 = (bf16[2,4,16,128]{3,2,1,0:T(8,128)(2,1)S(1)}, bf16[2,4,16,128]{3,2,1,0:T(8,128)(2,1)S(1)}, u32[]{:S(2)}, u32[]{:S(2)}) collective-permute-start(bf16[2,4,16,128]{3,2,1,0:T(8,128)(2,1)S(1)} %pad_maximum_fusion), channel_id=1, source_target_pairs={{0,16},{2,18},{4,20},{6,22},{8,24},{10,26},{12,28},{14,30},{17,1},... | collective-permute-start | bytes 98312 | tf_op jit(solution)/shard_map/ppermute | solution.py:338
  51.1 4.1 %collective-permute-start.12 = (bf16[2,4,16,128]{3,2,1,0:T(8,128)(2,1)S(1)}, bf16[2,4,16,128]{3,2,1,0:T(8,128)(2,1)S(1)}, u32[]{:S(2)}, u32[]{:S(2)}) collective-permute-start(bf16[2,4,16,128]{3,2,1,0:T(8,128)(2,1)S(1)} %broadcast_select_fusion.refs_0_), channel_id=1, source_target_pairs={{0,8},{1,9},{2,10},{3,11},{4,12},{5,13},{6,14},{7,15},{8,0},{9,1},... | collective-permute-start | bytes 98312 | tf_op jit(solution)/shard_map/ppermute | solution.py:338
  53.1 3.9 %collective-permute-start.13 = (bf16[2,4,16,128]{3,2,1,0:T(8,128)(2,1)S(1)}, bf16[2,4,16,128]{3,2,1,0:T(8,128)(2,1)S(1)}, u32[]{:S(2)}, u32[]{:S(2)}) collective-permute-start(bf16[2,4,16,128]{3,2,1,0:T(8,128)(2,1)S(1)} %broadcast_select_fusion.refs_0_), channel_id=1, source_target_pairs={{0,4},{1,5},{2,6},{3,7},{4,0},{5,1},{6,2},{7,3},{8,12},{9,13},{10,... | collective-permute-start | bytes 98312 | tf_op jit(solution)/shard_map/ppermute | solution.py:338
  54.6 4.8 %collective-permute-start.14 = (bf16[2,4,16,128]{3,2,1,0:T(8,128)(2,1)S(1)}, bf16[2,4,16,128]{3,2,1,0:T(8,128)(2,1)S(1)}, u32[]{:S(2)}, u32[]{:S(2)}) collective-permute-start(bf16[2,4,16,128]{3,2,1,0:T(8,128)(2,1)S(1)} %broadcast_select_fusion.refs_0_), channel_id=1, source_target_pairs={{0,12},{1,13},{2,14},{3,15},{4,8},{5,9},{6,10},{7,11},{8,4},{9,5},... | collective-permute-start | bytes 98312 | tf_op jit(solution)/shard_map/ppermute | solution.py:338
  54.6 6.4 %collective-permute-start.15 = (bf16[2,4,16,128]{3,2,1,0:T(8,128)(2,1)S(1)}, bf16[2,4,16,128]{3,2,1,0:T(8,128)(2,1)S(1)}, u32[]{:S(2)}, u32[]{:S(2)}) collective-permute-start(bf16[2,4,16,128]{3,2,1,0:T(8,128)(2,1)S(1)} %broadcast_select_fusion.refs_0_), channel_id=1, source_target_pairs={{0,2},{1,3},{2,0},{3,1},{4,6},{5,7},{6,4},{7,5},{8,10},{9,11},{10,... | collective-permute-start | bytes 98312 | tf_op jit(solution)/shard_map/ppermute | solution.py:338
  55.2 5.9 %collective-permute-start.16 = (bf16[2,4,16,128]{3,2,1,0:T(8,128)(2,1)S(1)}, bf16[2,4,16,128]{3,2,1,0:T(8,128)(2,1)S(1)}, u32[]{:S(2)}, u32[]{:S(2)}) collective-permute-start(bf16[2,4,16,128]{3,2,1,0:T(8,128)(2,1)S(1)} %collective-permute-done.12.refs_1_), channel_id=1, source_target_pairs={{0,2},{1,3},{2,0},{3,1},{4,6},{5,7},{6,4},{7,5},{8,10},{9,11},{10,... | collective-permute-start | bytes 98312 | tf_op jit(solution)/shard_map/ppermute | solution.py:338
  57.0 4.1 %collective-permute-start.17 = (bf16[2,4,16,128]{3,2,1,0:T(8,128)(2,1)S(1)}, bf16[2,4,16,128]{3,2,1,0:T(8,128)(2,1)S(1)}, u32[]{:S(2)}, u32[]{:S(2)}) collective-permute-start(bf16[2,4,16,128]{3,2,1,0:T(8,128)(2,1)S(1)} %collective-permute-done.13.refs_2_), channel_id=1, source_target_pairs={{0,2},{1,3},{2,0},{3,1},{4,6},{5,7},{6,4},{7,5},{8,10},{9,11},{10,... | collective-permute-start | bytes 98312 | tf_op jit(solution)/shard_map/ppermute | solution.py:338
  59.4 1.7 %collective-permute-start.18 = (bf16[2,4,16,128]{3,2,1,0:T(8,128)(2,1)S(1)}, bf16[2,4,16,128]{3,2,1,0:T(8,128)(2,1)S(1)}, u32[]{:S(2)}, u32[]{:S(2)}) collective-permute-start(bf16[2,4,16,128]{3,2,1,0:T(8,128)(2,1)S(1)} %collective-permute-done.14.refs_3_), channel_id=1, source_target_pairs={{0,2},{1,3},{2,0},{3,1},{4,6},{5,7},{6,4},{7,5},{8,10},{9,11},{10,... | collective-permute-start | bytes 98312 | tf_op jit(solution)/shard_map/ppermute | solution.py:338
  60.1 1.0 %copy-start.4 = (bf16[128,128]{1,0:T(8,128)(2,1)S(1)}, bf16[128,128]{1,0:T(8,128)(2,1)}, u32[]{:S(2)}) copy-start(bf16[128,128]{1,0:T(8,128)(2,1)} %refs_14_.1) | copy-start | bytes 98308

commit v5 on v4

--- a/solution.py
+++ b/solution.py
@@ -162,35 +162,40 @@
     return kernel
 
 
-def make_tri_kernel(n_col, blocks, place):
+def make_tri_kernel(n_col, blocks, place, parts):
     def kernel(*refs):
         lefts = refs[:n_col]
         rights = refs[n_col : n_col + len(blocks)]
         pair_ref, gate_ref, gains_ref, w_ref, bias_w_ref = refs[
             n_col + len(blocks) : n_col + len(blocks) + 5
         ]
-        mid_ref, norm_ref, bias_ref, sum_ref, left_ref, bias_scr = refs[-6:]
+        mid_refs = refs[-5 - parts : -5]
+        norm_ref, bias_ref, sum_ref, left_ref, bias_scr = refs[-5:]
         rows, cols, width = pair_ref.shape
         add_sums(left_ref, lefts, rights, sum_ref, [place(s) for s in blocks])
         step = 2
 
-        def finish(t, carry):
-            at = pl.ds(t * step, step)
-            total = sum_ref[at].reshape(step * cols, width)
-            normed = layer_norm(total, gains_ref[0:1, :]).astype(BF16)
-            update = dot(normed, w_ref[...])
-            pair = pair_ref[at].reshape(step * cols, width).astype(F32)
-            gate = gate_ref[at].reshape(step * cols, width)
-            mid = (pair + gate * update).astype(BF16)
-            mid_ref[at] = mid.reshape(step, cols, width)
-            att = layer_norm(mid.astype(F32), gains_ref[1:2, :]).astype(BF16)
-            norm_ref[at] = att.reshape(step, cols, width)
-            bias = dot_nt(bias_w_ref[...], att)
-            for u in range(step):
-                bias_scr[t * step + u] = bias[:, u * cols : (u + 1) * cols]
-            return carry
-
-        lax.fori_loop(0, rows // step, finish, 0, unroll=unroll_of(rows // step, cols))
+        share = rows // parts // step
+        for part, mid_ref in enumerate(mid_refs):
+
+            def finish(t, carry, part=part, mid_ref=mid_ref):
+                row = part * share * step + t * step
+                at = pl.ds(row, step)
+                total = sum_ref[at].reshape(step * cols, width)
+                normed = layer_norm(total, gains_ref[0:1, :]).astype(BF16)
+                update = dot(normed, w_ref[...])
+                pair = pair_ref[at].reshape(step * cols, width).astype(F32)
+                gate = gate_ref[at].reshape(step * cols, width)
+                mid = (pair + gate * update).astype(BF16)
+                mid_ref[pl.ds(t * step, step)] = mid.reshape(step, cols, width)
+                att = layer_norm(mid.astype(F32), gains_ref[1:2, :]).astype(BF16)
+                norm_ref[at] = att.reshape(step, cols, width)
+                bias = dot_nt(bias_w_ref[...], att)
+                for u in range(step):
+                    bias_scr[row + u] = bias[:, u * cols : (u + 1) * cols]
+                return carry
+
+            lax.fori_loop(0, share, finish, 0, unroll=unroll_of(share, cols))
         for h in range(H):
             bias_ref[h] = bias_scr[:, h, :].astype(BF16)
 
@@ -214,17 +219,19 @@
     lax.fori_loop(0, rows // step, body, 0, unroll=unroll_of(rows // step, cols))
 
 
-def make_spread_kernel(n_col):
+def make_spread_kernel(n_col, base):
     def kernel(*refs):
         others = refs[: n_col - 1]
         k_ref, v_ref, gains_ref, kv_w_ref, keys_ref, values_ref = refs[n_col - 1 :]
-        rows, cols, width = k_ref.shape
+        rows = keys_ref.shape[0]
+        cols, width = k_ref.shape[1:]
         step = 2
 
         def spread(t, carry):
             at = pl.ds(t * step, step)
-            keys_ref[at, 0:cols] = k_ref[at]
-            values_ref[at, 0:cols] = v_ref[at]
+            own = pl.ds(base + t * step, step)
+            keys_ref[at, 0:cols] = k_ref[own]
+            values_ref[at, 0:cols] = v_ref[own]
             for d in range(n_col - 1):
                 there = others[d][at].reshape(step * cols, width).astype(F32)
                 normed = layer_norm(there, gains_ref[1:2, :]).astype(BF16)
@@ -239,14 +246,19 @@
     return kernel
 
 
-def make_attend_kernel(n_col, n_blk, place):
+def make_attend_kernel(n_col, n_blk, place, base, n_done):
     def kernel(*refs):
         biases = refs[:n_blk]
         q_ref, keys_ref, values_ref, gate_ref, mid_ref, live_ref, out_w_ref = refs[
             n_blk : n_blk + 7
         ]
-        out_ref, bias_ref = refs[n_blk + 7 :]
-        rows, cols, width = q_ref.shape
+        done = refs[n_blk + 7 : n_blk + 7 + n_done]
+        whole_ref, bias_ref = refs[n_blk + 7 + n_done :]
+        rows, cols, width = mid_ref.shape
+        first_row = base if n_done else 0
+        out_ref = whole_ref.at[first_row : first_row + rows]
+        for at, done_ref in enumerate(done):
+            whole_ref[at * rows : (at + 1) * rows] = done_ref[...]
         blk = biases[0].shape[2]
         for d in range(n_col):
             live = jnp.broadcast_to(live_ref[:, d * cols : (d + 1) * cols], (blk, cols)) > 0.5
@@ -267,7 +279,7 @@
         def attend(i, carry):
             key = keys_ref[i]
             value = jnp.concatenate([values_ref[i], ones], axis=1)
-            query = q_ref[i]
+            query = q_ref[base + i]
             stack = jnp.concatenate(
                 [jnp.where(head == h, query, jnp.zeros_like(query)) for h in range(H)], axis=0
             )
@@ -282,7 +294,7 @@
                 part = both[h * cols : (h + 1) * cols]
                 summed = jnp.where(mine, part[:, :width], summed)
                 totals = jnp.where(mine, part[:, width:], totals)
-            out_ref[i] = (summed / totals * gate_ref[i]).astype(BF16)
+            out_ref[i] = (summed / totals * gate_ref[base + i]).astype(BF16)
             return carry
 
         lax.fori_loop(0, rows, attend, 0, unroll=max(1, min(rows, 2**18 // (cols * n_col * cols))))
@@ -395,6 +407,7 @@
         rows, cols, width = pair_rep.shape
         n_col, n_blk = grid.n_col, grid.n_blk
         whole = (rows, cols, width)
+        parts = 2 if grid.fast else 1
         limit = min(60 * MIB, 12 * MIB + 24 * H * cols * n_col * cols * 4)
         tri_gain = tri_gain.reshape(1, width)
         sum_gain = sum_gain.reshape(1, width)
@@ -449,10 +462,10 @@
                     aliases={n_col + len(blocks): 0} if sums else {},
                 )(*lefts, *[rights[s] for s in blocks], *sums)
             ]
-        mid, normed, bias, _ = call(
-            make_tri_kernel(n_col, last, grid.place),
+        *mids, normed, bias, _ = call(
+            make_tri_kernel(n_col, last, grid.place, parts),
             (
-                jax.ShapeDtypeStruct(whole, BF16),
+                *[jax.ShapeDtypeStruct((rows // parts, cols, width), BF16)] * parts,
                 jax.ShapeDtypeStruct(whole, BF16),
                 jax.ShapeDtypeStruct((H, rows, cols), BF16),
                 jax.ShapeDtypeStruct(whole, F32),
@@ -461,27 +474,46 @@
             n_col + len(last) + 5 + len(sums),
             limit,
             [left_scr, pltpu.VMEM((rows, H, cols), F32)],
-            aliases={n_col + len(last) + 5: 3} if sums else {},
+            aliases={n_col + len(last) + 5: parts + 2} if sums else {},
         )(*lefts, *[rights[s] for s in last], pair_rep, gate, gains, tri_out, att_bias.T, *sums)
         biases = grid.gather(bias, True)
-        others = [grid.shift_col(mid, d) for d in range(1, n_col)]
+        others = []
+        for mid in mids:
+            others.append([grid.shift_col(mid, d) for d in range(1, n_col)])
         wide = jax.ShapeDtypeStruct(whole, BF16)
         query, key, value, att_gate = call(
             project_kernel, (wide, wide, wide, jax.ShapeDtypeStruct(whole, F32)), 0, 2, limit
         )(normed, att_in)
-        all_keys = jax.ShapeDtypeStruct((rows, n_col * cols, width), BF16)
-        keys, values = call(
-            make_spread_kernel(n_col), (all_keys, all_keys), 0, n_col + 3, limit
-        )(*others, key, value, gains, att_in)
-        return call(
-            make_attend_kernel(n_col, n_blk, grid.place),
-            wide,
-            0,
-            n_blk + 7,
-            limit,
-            [pltpu.VMEM((H * cols, n_col * cols), F32)],
-            held_out=False,
-        )(*biases, query, keys, values, att_gate, mid, live, att_out)
+        share = rows // parts
+        all_keys = jax.ShapeDtypeStruct((share, n_col * cols, width), BF16)
+        done = []
+        for part in range(parts):
+            base = part * share
+            final = part == parts - 1
+            keys, values = call(
+                make_spread_kernel(n_col, base), (all_keys, all_keys), 0, n_col + 3, limit
+            )(*others[part], key, value, gains, att_in)
+            result = call(
+                make_attend_kernel(n_col, n_blk, grid.place, base, len(done) * final),
+                wide if final else jax.ShapeDtypeStruct((share, cols, width), BF16),
+                0,
+                n_blk + 7 + len(done) * final,
+                limit,
+                [pltpu.VMEM((H * cols, n_col * cols), F32)],
+                held_out=not final,
+            )(
+                *biases,
+                query,
+                keys,
+                values,
+                att_gate,
+                mids[part],
+                live,
+                att_out,
+                *(done if final else []),
+            )
+            done.append(result)
+        return result
 
     return body
 

time: 65.6 us -> 59 us (0.90)
  waiting for transfers between devices: 25.9 us -> 17.9 us
  starting transfers between devices: 25.2 us -> 26.4 us
    ppermute x20 -> x21, waiting for transfers between devices: 25.9 us -> 17.9 us  [move(): return lax.ppermute(value, ('row', 'col'), pairs)]
    ppermute x20 -> x21, starting transfers between devices: 25.2 us -> 26.4 us  [move(): return lax.ppermute(value, ('row', 'col'), pairs)]
    pallas_call x8 -> x10, Pallas kernels: 11.3 us -> 11.4 us  [apply(): return run(*args[:n_smem], *held)]
  transfers between devices with their start and end apart: 20 -> 21, of which waited for: 9 -> 9; matrix products, arithmetic and copies ran while one was open for 0% -> 0% of each run, Pallas kernels for 7% -> 9%
where the time goes in v5:
time: 59 us; the launch traced here: 58.7 us
  starting transfers between devices  26.4 us (45%)
  waiting for transfers between devices  17.9 us (30%)
  Pallas kernels  13.5 us (23%)
  local copies, waits for them, and re-layouts  0.69 us (1%)
    ppermute x21, starting transfers between devices, move(): return lax.ppermute(value, ('row', 'col'), pairs)  26.4 us
    ppermute x21, waiting for transfers between devices, move(): return lax.ppermute(value, ('row', 'col'), pairs)  17.9 us
    pallas_call x10, Pallas kernels, apply(): return run(*args[:n_smem], *held)  11.4 us
    pallas_call x1, Pallas kernels, body(): pl.pallas_call(make_edge_kernel(cols, n_col, grid.col_of), name='edges',...  2.11 us
  transfers between devices with their start and end apart: 21, of which 9 were waited for; matrix products, arithmetic and copies ran while one was open for 0% of the time, Pallas kernels for 9%

profile of v5, /device:TPU:0, one launch (start us, length us, event | category | flops | bytes accessed | tf_op | source)
XLA Modules:
  0.0 58.7 jit_solution(16131063246825300185)
XLA Ops:
  0.0 2.1 %edges.1 = (bf16[16,16,128]{2,1,0:T(8,128)(2,1)S(1)}, bf16[16,16,128]{2,1,0:T(8,128)(2,1)S(1)}, f32[3,128]{1,0:T(4,128)S(1)}, f32[1,256]{1,0:T(1,128)S(1)}) custom-call(s32[4]{0:T(128)} %len_ref.1, bf16[16,128,128]{2,1,0:T(8,128)(2,1)} %refs_3_.1, f32[1,128]{1,0:T(1,128)} %bitcast.17, f32[1,128]{1,0:T(1,128)} %bitcast.18, f32[1,128]{1,0:T(1,128)} %bitcast.19, ...), custom_call_target="tpu_custom_call" | custom-call | tf_op jit(solution)/shard_map/edges/pallas_call | solution.py:420
  2.1 4.1 %collective-permute-start.1 = (bf16[16,16,128]{2,1,0:T(8,128)(2,1)S(1)}, bf16[16,16,128]{2,1,0:T(8,128)(2,1)S(1)}, u32[]{:S(2)}, u32[]{:S(2)}) collective-permute-start(bf16[16,16,128]{2,1,0:T(8,128)(2,1)S(1)} %get-tuple-element.22), channel_id=1, source_target_pairs={{0,16},{1,0},{2,18},{3,2},{4,20},{5,4},{6,22},{7,6},{8,24},{9,8},{... | collective-permute-start | bytes 196616 | tf_op jit(solution)/shard_map/ppermute | solution.py:350
  6.2 0.7 %collective-permute-start.2 = (bf16[16,16,128]{2,1,0:T(8,128)(2,1)S(1)}, bf16[16,16,128]{2,1,0:T(8,128)(2,1)S(1)}, u32[]{:S(2)}, u32[]{:S(2)}) collective-permute-start(bf16[16,16,128]{2,1,0:T(8,128)(2,1)S(1)} %get-tuple-element.22), channel_id=1, source_target_pairs={{1,16},{3,18},{5,20},{7,22},{9,24},{11,26},{13,28},{15,30},{16,1},... | collective-permute-start | bytes 196616 | tf_op jit(solution)/shard_map/ppermute | solution.py:350
  6.9 1.2 %collective-permute-done.1 = bf16[16,16,128]{2,1,0:T(8,128)(2,1)S(1)} collective-permute-done((bf16[16,16,128]{2,1,0:T(8,128)(2,1)S(1)}, bf16[16,16,128]{2,1,0:T(8,128)(2,1)S(1)}, u32[]{:S(2)}, u32[]{:S(2)}) %collective-permute-start.1) | collective-permute-done | bytes 65568 | tf_op jit(solution)/shard_map/ppermute | solution.py:350
  8.1 0.0 collective-permute-done.2
  8.2 2.4 %collective-permute-start.3 = (bf16[2,16,16,128]{3,2,1,0:T(8,128)(2,1)S(1)}, bf16[2,16,16,128]{3,2,1,0:T(8,128)(2,1)S(1)}, u32[]{:S(2)}, u32[]{:S(2)}) collective-permute-start(bf16[2,16,16,128]{3,2,1,0:T(8,128)(2,1)S(1)} %maximum_select_fusion.refs_2_), channel_id=1, source_target_pairs={{0,8},{1,9},{2,10},{3,11},{4,12},{5,13},{6,14},{7,15},{8,0},{9,1},... | collective-permute-start | bytes 393224 | tf_op jit(solution)/shard_map/ppermute | solution.py:350
  10.6 1.5 %collective-permute-start.6 = (bf16[2,16,16,128]{3,2,1,0:T(8,128)(2,1)S(1)}, bf16[2,16,16,128]{3,2,1,0:T(8,128)(2,1)S(1)}, u32[]{:S(2)}, u32[]{:S(2)}) collective-permute-start(bf16[2,16,16,128]{3,2,1,0:T(8,128)(2,1)S(1)} %maximum_select_fusion.refs_2_), channel_id=1, source_target_pairs={{0,4},{1,5},{2,6},{3,7},{4,0},{5,1},{6,2},{7,3},{8,12},{9,13},{10,... | collective-permute-start | bytes 393224 | tf_op jit(solution)/shard_map/ppermute | solution.py:350
  12.0 2.4 %collective-permute-done.3.refs_4_ = bf16[2,16,16,128]{3,2,1,0:T(8,128)(2,1)S(1)} collective-permute-done((bf16[2,16,16,128]{3,2,1,0:T(8,128)(2,1)S(1)}, bf16[2,16,16,128]{3,2,1,0:T(8,128)(2,1)S(1)}, u32[]{:S(2)}, u32[]{:S(2)}) %collective-permute-start.3) | collective-permute-done | bytes 131104 | tf_op jit(solution)/shard_map/ppermute | solution.py:350
  14.5 1.5 %collective-permute-start.4 = (bf16[2,16,16,128]{3,2,1,0:T(8,128)(2,1)S(1)}, bf16[2,16,16,128]{3,2,1,0:T(8,128)(2,1)S(1)}, u32[]{:S(2)}, u32[]{:S(2)}) collective-permute-start(bf16[2,16,16,128]{3,2,1,0:T(8,128)(2,1)S(1)} %collective-permute-done.3.refs_4_), channel_id=1, source_target_pairs={{0,4},{1,5},{2,6},{3,7},{4,0},{5,1},{6,2},{7,3},{8,12},{9,13},{10,... | collective-permute-start | bytes 393224 | tf_op jit(solution)/shard_map/ppermute | solution.py:350
  16.0 0.0 collective-permute-start.8
  16.0 0.5 collective-permute-start.9
  16.5 0.0 collective-permute-done.6.refs_2_
  16.5 0.0 collective-permute-start.7
  16.5 3.0 %collective-permute-done.4.refs_2_ = bf16[2,16,16,128]{3,2,1,0:T(8,128)(2,1)S(1)} collective-permute-done((bf16[2,16,16,128]{3,2,1,0:T(8,128)(2,1)S(1)}, bf16[2,16,16,128]{3,2,1,0:T(8,128)(2,1)S(1)}, u32[]{:S(2)}, u32[]{:S(2)}) %collective-permute-start.4) | collective-permute-done | bytes 131104 | tf_op jit(solution)/shard_map/ppermute | solution.py:350
  19.4 0.0 collective-permute-start.5
  19.4 4.6 %collective-permute-start = (bf16[16,16,128]{2,1,0:T(8,128)(2,1)S(1)}, bf16[16,16,128]{2,1,0:T(8,128)(2,1)S(1)}, u32[]{:S(2)}, u32[]{:S(2)}) collective-permute-start(bf16[16,16,128]{2,1,0:T(8,128)(2,1)S(1)} %get-tuple-element.21.refs_0_), channel_id=1, source_target_pairs={{0,1},{1,0},{2,3},{3,2},{4,5},{5,4},{6,7},{7,6},{8,9},{9,8},{10,11... | collective-permute-start | bytes 196616 | tf_op jit(solution)/shard_map/ppermute | solution.py:350
  24.1 0.9 %shard_map.100.refs_4_ = f32[16,128,128]{2,1,0:T(8,128)S(1)} custom-call(bf16[16,128,128]{2,1,0:T(8,128)(2,1)S(1)} %copy-done, f32[3,128]{1,0:T(4,128)S(1)} %get-tuple-element.23.gains_ref.refs_5_.refs_3_, bf16[128,640]{1,0:T(8,128)(2,1)S(1)} %copy-done.2), custom_call_target="tpu_custom_call" | custom-call | tf_op jit(solution)/shard_map/pallas_call | solution.py:69
  25.0 1.8 %collective-permute-done.refs_1_ = bf16[16,16,128]{2,1,0:T(8,128)(2,1)S(1)} collective-permute-done((bf16[16,16,128]{2,1,0:T(8,128)(2,1)S(1)}, bf16[16,16,128]{2,1,0:T(8,128)(2,1)S(1)}, u32[]{:S(2)}, u32[]{:S(2)}) %collective-permute-start) | collective-permute-done | bytes 65568 | tf_op jit(solution)/shard_map/ppermute | solution.py:350
  26.8 0.0 collective-permute-done.9.refs_5_
  26.8 1.3 %shard_map.101.refs_4_ = f32[16,128,128]{2,1,0:T(8,128)S(1)} custom-call(bf16[16,16,128]{2,1,0:T(8,128)(2,1)S(1)} %get-tuple-element.21.refs_0_, bf16[16,16,128]{2,1,0:T(8,128)(2,1)S(1)} %collective-permute-done.refs_1_, bf16[2,16,16,128]{3,2,1,0:T(8,128)(2,1)S(1)} %maximum_select_fusion.refs_2_, ...), custom_call_target="tpu_custom_call" | custom-call | tf_op jit(solution)/shard_map/pallas_call | solution.py:69
  28.2 0.0 collective-permute-done.7.refs_3_
  28.2 0.7 %shard_map.102.refs_3_ = f32[16,128,128]{2,1,0:T(8,128)S(1)} custom-call(bf16[16,16,128]{2,1,0:T(8,128)(2,1)S(1)} %get-tuple-element.21.refs_0_, bf16[16,16,128]{2,1,0:T(8,128)(2,1)S(1)} %collective-permute-done.refs_1_, bf16[2,16,16,128]{3,2,1,0:T(8,128)(2,1)S(1)} %collective-permute-done.6.refs_2_, ...), custom_call_target="tpu_custom_call", output_to_operand_aliasing={{}: (4, {})} | custom-call | tf_op jit(solution)/shard_map/pallas_call | solution.py:69
  28.8 0.3 shard_map.103.refs_8_
  29.2 0.0 copy-start.5
  29.2 0.4 copy-done.4
  29.6 0.3 copy-done.5
  29.9 2.2 %shard_map.104 = (bf16[8,128,128]{2,1,0:T(8,128)(2,1)S(1)}, bf16[8,128,128]{2,1,0:T(8,128)(2,1)S(1)}, bf16[16,128,128]{2,1,0:T(8,128)(2,1)S(1)}, bf16[4,16,128]{2,1,0:T(8,128)(2,1)S(1)}, f32[16,128,128]{2,1,0:T(8,128)S(1)}) custom-call(bf16[16,16,128]{2,1,0:T(8,128)(2,1)S(1)} %get-tuple-element.21.refs_0_, ...), custom_call_target="tpu_custom_call", output_to_operand_aliasing={{4}: (8, {})} | custom-call | tf_op jit(solution)/shard_map/pallas_call | solution.py:69
  32.0 0.0 copy-start.1
  32.1 1.4 %collective-permute-start.10 = (bf16[4,16,128]{2,1,0:T(8,128)(2,1)S(1)}, bf16[4,16,128]{2,1,0:T(8,128)(2,1)S(1)}, u32[]{:S(2)}, u32[]{:S(2)}) collective-permute-start(bf16[4,16,128]{2,1,0:T(8,128)(2,1)S(1)} %get-tuple-element.24), channel_id=1, source_target_pairs={{1,0},{3,2},{5,4},{7,6},{9,8},{11,10},{13,12},{15,14},{16,17},{18,... | collective-permute-start | bytes 49160 | tf_op jit(solution)/shard_map/ppermute | solution.py:350
  33.5 4.3 %collective-permute-done.10 = bf16[4,16,128]{2,1,0:T(8,128)(2,1)S(1)} collective-permute-done((bf16[4,16,128]{2,1,0:T(8,128)(2,1)S(1)}, bf16[4,16,128]{2,1,0:T(8,128)(2,1)S(1)}, u32[]{:S(2)}, u32[]{:S(2)}) %collective-permute-start.10) | collective-permute-done | bytes 16416 | tf_op jit(solution)/shard_map/ppermute | solution.py:350
  37.8 3.4 %collective-permute-start.11 = (bf16[2,4,16,128]{3,2,1,0:T(8,128)(2,1)S(1)}, bf16[2,4,16,128]{3,2,1,0:T(8,128)(2,1)S(1)}, u32[]{:S(2)}, u32[]{:S(2)}) collective-permute-start(bf16[2,4,16,128]{3,2,1,0:T(8,128)(2,1)S(1)} %pad_maximum_fusion), channel_id=1, source_target_pairs={{0,16},{2,18},{4,20},{6,22},{8,24},{10,26},{12,28},{14,30},{17,1},... | collective-permute-start | bytes 98312 | tf_op jit(solution)/shard_map/ppermute | solution.py:350
  41.3 0.1 collective-permute-start.20
  41.3 2.0 %collective-permute-start.19 = (bf16[8,128,128]{2,1,0:T(8,128)(2,1)S(1)}, bf16[8,128,128]{2,1,0:T(8,128)(2,1)S(1)}, u32[]{:S(2)}, u32[]{:S(2)}) collective-permute-start(bf16[8,128,128]{2,1,0:T(8,128)(2,1)S(1)} %get-tuple-element.27.refs_12_), channel_id=1, source_target_pairs={{0,1},{1,0},{2,3},{3,2},{4,5},{5,4},{6,7},{7,6},{8,9},{9,8},{10,11... | collective-permute-start | bytes 786440 | tf_op jit(solution)/shard_map/ppermute | solution.py:350
  43.3 0.0 collective-permute-done.11
  43.4 2.1 %collective-permute-start.12 = (bf16[2,4,16,128]{3,2,1,0:T(8,128)(2,1)S(1)}, bf16[2,4,16,128]{3,2,1,0:T(8,128)(2,1)S(1)}, u32[]{:S(2)}, u32[]{:S(2)}) collective-permute-start(bf16[2,4,16,128]{3,2,1,0:T(8,128)(2,1)S(1)} %broadcast_select_fusion.refs_0_), channel_id=1, source_target_pairs={{0,8},{1,9},{2,10},{3,11},{4,12},{5,13},{6,14},{7,15},{8,0},{9,1},... | collective-permute-start | bytes 98312 | tf_op jit(solution)/shard_map/ppermute | solution.py:350
  45.4 1.5 %collective-permute-start.13 = (bf16[2,4,16,128]{3,2,1,0:T(8,128)(2,1)S(1)}, bf16[2,4,16,128]{3,2,1,0:T(8,128)(2,1)S(1)}, u32[]{:S(2)}, u32[]{:S(2)}) collective-permute-start(bf16[2,4,16,128]{3,2,1,0:T(8,128)(2,1)S(1)} %broadcast_select_fusion.refs_0_), channel_id=1, source_target_pairs={{0,4},{1,5},{2,6},{3,7},{4,0},{5,1},{6,2},{7,3},{8,12},{9,13},{10,... | collective-permute-start | bytes 98312 | tf_op jit(solution)/shard_map/ppermute | solution.py:350
  46.9 0.1 collective-permute-start.14
  47.0 0.5 collective-permute-done.12.refs_1_
  47.5 1.9 %collective-permute-done.13.refs_2_ = bf16[2,4,16,128]{3,2,1,0:T(8,128)(2,1)S(1)} collective-permute-done((bf16[2,4,16,128]{3,2,1,0:T(8,128)(2,1)S(1)}, bf16[2,4,16,128]{3,2,1,0:T(8,128)(2,1)S(1)}, u32[]{:S(2)}, u32[]{:S(2)}) %collective-permute-start.13) | collective-permute-done | bytes 32800 | tf_op jit(solution)/shard_map/ppermute | solution.py:350
  49.4 2.4 %collective-permute-done.14.refs_3_ = bf16[2,4,16,128]{3,2,1,0:T(8,128)(2,1)S(1)} collective-permute-done((bf16[2,4,16,128]{3,2,1,0:T(8,128)(2,1)S(1)}, bf16[2,4,16,128]{3,2,1,0:T(8,128)(2,1)S(1)}, u32[]{:S(2)}, u32[]{:S(2)}) %collective-permute-start.14) | collective-permute-done | bytes 32800 | tf_op jit(solution)/shard_map/ppermute | solution.py:350
  51.8 0.5 collective-permute-start.18
  52.3 0.7 %shard_map.105 = (bf16[16,128,128]{2,1,0:T(8,128)(2,1)S(1)}, bf16[16,128,128]{2,1,0:T(8,128)(2,1)S(1)}, bf16[16,128,128]{2,1,0:T(8,128)(2,1)S(1)}, f32[16,128,128]{2,1,0:T(8,128)S(1)}) custom-call(bf16[16,128,128]{2,1,0:T(8,128)(2,1)S(1)} %get-tuple-element.25.norm_ref, bf16[128,512]{1,0:T(8,128)(2,1)S(1)} %copy-done.1), custom_call_target="tpu_custom_call" | custom-call | tf_op jit(solution)/shard_map/pallas_call | solution.py:69
  53.0 0.6 shard_map.107
  53.6 0.0 copy-start.3
  53.6 0.4 collective-permute-done.19.refs_0_
  53.9 0.6 shard_map.106
  54.6 1.7 %shard_map.108.refs_15_ = bf16[8,128,128]{2,1,0:T(8,128)(2,1)S(1)} custom-call(bf16[2,4,16,128]{3,2,1,0:T(8,128)(2,1)S(1)} %broadcast_select_fusion.refs_0_, bf16[2,4,16,128]{3,2,1,0:T(8,128)(2,1)S(1)} %collective-permute-done.12.refs_1_, bf16[2,4,16,128]{3,2,1,0:T(8,128)(2,1)S(1)} %collective-permute-done.13.refs_2_, ...), custom_call_target="tpu_custom_call" | custom-call | tf_op jit(solution)/shard_map/pallas_call | solution.py:69
  56.3 2.5 %shard_map.109 = bf16[16,128,128]{2,1,0:T(8,128)(2,1)} custom-call(bf16[2,4,16,128]{3,2,1,0:T(8,128)(2,1)S(1)} %broadcast_select_fusion.refs_0_, bf16[2,4,16,128]{3,2,1,0:T(8,128)(2,1)S(1)} %collective-permute-done.12.refs_1_, bf16[2,4,16,128]{3,2,1,0:T(8,128)(2,1)S(1)} %collective-permute-done.13.refs_2_, ...), custom_call_target="tpu_custom_call" | custom-call | tf_op jit(solution)/shard_map/pallas_call | solution.py:69
  (20 shorter events, 0.1 us)
Async XLA Ops:
  0.0 24.1 %copy-start = (bf16[16,128,128]{2,1,0:T(8,128)(2,1)S(1)}, bf16[16,128,128]{2,1,0:T(8,128)(2,1)}, u32[]{:S(2)}) copy-start(bf16[16,128,128]{2,1,0:T(8,128)(2,1)} %refs_3_.1) | copy-start | bytes 1572868
  2.1 6.0 %collective-permute-start.1 = (bf16[16,16,128]{2,1,0:T(8,128)(2,1)S(1)}, bf16[16,16,128]{2,1,0:T(8,128)(2,1)S(1)}, u32[]{:S(2)}, u32[]{:S(2)}) collective-permute-start(bf16[16,16,128]{2,1,0:T(8,128)(2,1)S(1)} %get-tuple-element.22), channel_id=1, source_target_pairs={{0,16},{1,0},{2,18},{3,2},{4,20},{5,4},{6,22},{7,6},{8,24},{9,8},{... | collective-permute-start | bytes 196616 | tf_op jit(solution)/shard_map/ppermute | solution.py:350
  6.2 1.9 %collective-permute-start.2 = (bf16[16,16,128]{2,1,0:T(8,128)(2,1)S(1)}, bf16[16,16,128]{2,1,0:T(8,128)(2,1)S(1)}, u32[]{:S(2)}, u32[]{:S(2)}) collective-permute-start(bf16[16,16,128]{2,1,0:T(8,128)(2,1)S(1)} %get-tuple-element.22), channel_id=1, source_target_pairs={{1,16},{3,18},{5,20},{7,22},{9,24},{11,26},{13,28},{15,30},{16,1},... | collective-permute-start | bytes 196616 | tf_op jit(solution)/shard_map/ppermute | solution.py:350
  8.1 15.9 %copy-start.2 = (bf16[128,640]{1,0:T(8,128)(2,1)S(1)}, bf16[128,640]{1,0:T(8,128)(2,1)}, u32[]{:S(2)}) copy-start(bf16[128,640]{1,0:T(8,128)(2,1)} %w_ref.4) | copy-start | bytes 491524
  8.2 6.3 %collective-permute-start.3 = (bf16[2,16,16,128]{3,2,1,0:T(8,128)(2,1)S(1)}, bf16[2,16,16,128]{3,2,1,0:T(8,128)(2,1)S(1)}, u32[]{:S(2)}, u32[]{:S(2)}) collective-permute-start(bf16[2,16,16,128]{3,2,1,0:T(8,128)(2,1)S(1)} %maximum_select_fusion.refs_2_), channel_id=1, source_target_pairs={{0,8},{1,9},{2,10},{3,11},{4,12},{5,13},{6,14},{7,15},{8,0},{9,1},... | collective-permute-start | bytes 393224 | tf_op jit(solution)/shard_map/ppermute | solution.py:350
  10.6 5.9 %collective-permute-start.6 = (bf16[2,16,16,128]{3,2,1,0:T(8,128)(2,1)S(1)}, bf16[2,16,16,128]{3,2,1,0:T(8,128)(2,1)S(1)}, u32[]{:S(2)}, u32[]{:S(2)}) collective-permute-start(bf16[2,16,16,128]{3,2,1,0:T(8,128)(2,1)S(1)} %maximum_select_fusion.refs_2_), channel_id=1, source_target_pairs={{0,4},{1,5},{2,6},{3,7},{4,0},{5,1},{6,2},{7,3},{8,12},{9,13},{10,... | collective-permute-start | bytes 393224 | tf_op jit(solution)/shard_map/ppermute | solution.py:350
  14.5 5.0 %collective-permute-start.4 = (bf16[2,16,16,128]{3,2,1,0:T(8,128)(2,1)S(1)}, bf16[2,16,16,128]{3,2,1,0:T(8,128)(2,1)S(1)}, u32[]{:S(2)}, u32[]{:S(2)}) collective-permute-start(bf16[2,16,16,128]{3,2,1,0:T(8,128)(2,1)S(1)} %collective-permute-done.3.refs_4_), channel_id=1, source_target_pairs={{0,4},{1,5},{2,6},{3,7},{4,0},{5,1},{6,2},{7,3},{8,12},{9,13},{10,... | collective-permute-start | bytes 393224 | tf_op jit(solution)/shard_map/ppermute | solution.py:350
  16.0 10.9 %collective-permute-start.8 = (bf16[2,16,16,128]{3,2,1,0:T(8,128)(2,1)S(1)}, bf16[2,16,16,128]{3,2,1,0:T(8,128)(2,1)S(1)}, u32[]{:S(2)}, u32[]{:S(2)}) collective-permute-start(bf16[2,16,16,128]{3,2,1,0:T(8,128)(2,1)S(1)} %maximum_select_fusion.refs_2_), channel_id=1, source_target_pairs={{0,2},{1,3},{2,0},{3,1},{4,6},{5,7},{6,4},{7,5},{8,10},{9,11},{10,... | collective-permute-start | bytes 393224 | tf_op jit(solution)/shard_map/ppermute | solution.py:350
  16.0 10.9 %collective-permute-start.9 = (bf16[2,16,16,128]{3,2,1,0:T(8,128)(2,1)S(1)}, bf16[2,16,16,128]{3,2,1,0:T(8,128)(2,1)S(1)}, u32[]{:S(2)}, u32[]{:S(2)}) collective-permute-start(bf16[2,16,16,128]{3,2,1,0:T(8,128)(2,1)S(1)} %collective-permute-done.3.refs_4_), channel_id=1, source_target_pairs={{0,2},{1,3},{2,0},{3,1},{4,6},{5,7},{6,4},{7,5},{8,10},{9,11},{10,... | collective-permute-start | bytes 393224 | tf_op jit(solution)/shard_map/ppermute | solution.py:350
  16.5 11.7 %collective-permute-start.7 = (bf16[2,16,16,128]{3,2,1,0:T(8,128)(2,1)S(1)}, bf16[2,16,16,128]{3,2,1,0:T(8,128)(2,1)S(1)}, u32[]{:S(2)}, u32[]{:S(2)}) collective-permute-start(bf16[2,16,16,128]{3,2,1,0:T(8,128)(2,1)S(1)} %collective-permute-done.6.refs_2_), channel_id=1, source_target_pairs={{0,2},{1,3},{2,0},{3,1},{4,6},{5,7},{6,4},{7,5},{8,10},{9,11},{10,... | collective-permute-start | bytes 393224 | tf_op jit(solution)/shard_map/ppermute | solution.py:350
  19.4 9.8 %collective-permute-start.5 = (bf16[2,16,16,128]{3,2,1,0:T(8,128)(2,1)S(1)}, bf16[2,16,16,128]{3,2,1,0:T(8,128)(2,1)S(1)}, u32[]{:S(2)}, u32[]{:S(2)}) collective-permute-start(bf16[2,16,16,128]{3,2,1,0:T(8,128)(2,1)S(1)} %collective-permute-done.4.refs_2_), channel_id=1, source_target_pairs={{0,2},{1,3},{2,0},{3,1},{4,6},{5,7},{6,4},{7,5},{8,10},{9,11},{10,... | collective-permute-start | bytes 393224 | tf_op jit(solution)/shard_map/ppermute | solution.py:350
  19.4 7.4 %collective-permute-start = (bf16[16,16,128]{2,1,0:T(8,128)(2,1)S(1)}, bf16[16,16,128]{2,1,0:T(8,128)(2,1)S(1)}, u32[]{:S(2)}, u32[]{:S(2)}) collective-permute-start(bf16[16,16,128]{2,1,0:T(8,128)(2,1)S(1)} %get-tuple-element.21.refs_0_), channel_id=1, source_target_pairs={{0,1},{1,0},{2,3},{3,2},{4,5},{5,4},{6,7},{7,6},{8,9},{9,8},{10,11... | collective-permute-start | bytes 196616 | tf_op jit(solution)/shard_map/ppermute | solution.py:350
  28.8 0.8 %copy-start.4 = (bf16[128,128]{1,0:T(8,128)(2,1)S(1)}, bf16[128,128]{1,0:T(8,128)(2,1)}, u32[]{:S(2)}) copy-start(bf16[128,128]{1,0:T(8,128)(2,1)} %refs_6_.1) | copy-start | bytes 98308
  29.2 0.7 %copy-start.5 = (bf16[128,4]{0,1:T(4,128)(2,1)S(1)}, bf16[128,4]{0,1:T(4,128)(2,1)}, u32[]{:S(2)}) copy-start(bf16[128,4]{0,1:T(4,128)(2,1)} %param.18) | copy-start | bytes 3076
  32.0 20.2 %copy-start.1 = (bf16[128,512]{1,0:T(8,128)(2,1)S(1)}, bf16[128,512]{1,0:T(8,128)(2,1)}, u32[]{:S(2)}) copy-start(bf16[128,512]{1,0:T(8,128)(2,1)} %refs_4_.3) | copy-start | bytes 393220
  32.1 5.8 %collective-permute-start.10 = (bf16[4,16,128]{2,1,0:T(8,128)(2,1)S(1)}, bf16[4,16,128]{2,1,0:T(8,128)(2,1)S(1)}, u32[]{:S(2)}, u32[]{:S(2)}) collective-permute-start(bf16[4,16,128]{2,1,0:T(8,128)(2,1)S(1)} %get-tuple-element.24), channel_id=1, source_target_pairs={{1,0},{3,2},{5,4},{7,6},{9,8},{11,10},{13,12},{15,14},{16,17},{18,... | collective-permute-start | bytes 49160 | tf_op jit(solution)/shard_map/ppermute | solution.py:350
  37.8 5.5 %collective-permute-start.11 = (bf16[2,4,16,128]{3,2,1,0:T(8,128)(2,1)S(1)}, bf16[2,4,16,128]{3,2,1,0:T(8,128)(2,1)S(1)}, u32[]{:S(2)}, u32[]{:S(2)}) collective-permute-start(bf16[2,4,16,128]{3,2,1,0:T(8,128)(2,1)S(1)} %pad_maximum_fusion), channel_id=1, source_target_pairs={{0,16},{2,18},{4,20},{6,22},{8,24},{10,26},{12,28},{14,30},{17,1},... | collective-permute-start | bytes 98312 | tf_op jit(solution)/shard_map/ppermute | solution.py:350
  41.3 10.5 %collective-permute-start.20 = (bf16[8,128,128]{2,1,0:T(8,128)(2,1)S(1)}, bf16[8,128,128]{2,1,0:T(8,128)(2,1)S(1)}, u32[]{:S(2)}, u32[]{:S(2)}) collective-permute-start(bf16[8,128,128]{2,1,0:T(8,128)(2,1)S(1)} %get-tuple-element.34.refs_12_), channel_id=1, source_target_pairs={{0,1},{1,0},{2,3},{3,2},{4,5},{5,4},{6,7},{7,6},{8,9},{9,8},{10,11... | collective-permute-start | bytes 786440 | tf_op jit(solution)/shard_map/ppermute | solution.py:350
  41.3 12.6 %collective-permute-start.19 = (bf16[8,128,128]{2,1,0:T(8,128)(2,1)S(1)}, bf16[8,128,128]{2,1,0:T(8,128)(2,1)S(1)}, u32[]{:S(2)}, u32[]{:S(2)}) collective-permute-start(bf16[8,128,128]{2,1,0:T(8,128)(2,1)S(1)} %get-tuple-element.27.refs_12_), channel_id=1, source_target_pairs={{0,1},{1,0},{2,3},{3,2},{4,5},{5,4},{6,7},{7,6},{8,9},{9,8},{10,11... | collective-permute-start | bytes 786440 | tf_op jit(solution)/shard_map/ppermute | solution.py:350
  43.4 4.1 %collective-permute-start.12 = (bf16[2,4,16,128]{3,2,1,0:T(8,128)(2,1)S(1)}, bf16[2,4,16,128]{3,2,1,0:T(8,128)(2,1)S(1)}, u32[]{:S(2)}, u32[]{:S(2)}) collective-permute-start(bf16[2,4,16,128]{3,2,1,0:T(8,128)(2,1)S(1)} %broadcast_select_fusion.refs_0_), channel_id=1, source_target_pairs={{0,8},{1,9},{2,10},{3,11},{4,12},{5,13},{6,14},{7,15},{8,0},{9,1},... | collective-permute-start | bytes 98312 | tf_op jit(solution)/shard_map/ppermute | solution.py:350
  45.4 3.9 %collective-permute-start.13 = (bf16[2,4,16,128]{3,2,1,0:T(8,128)(2,1)S(1)}, bf16[2,4,16,128]{3,2,1,0:T(8,128)(2,1)S(1)}, u32[]{:S(2)}, u32[]{:S(2)}) collective-permute-start(bf16[2,4,16,128]{3,2,1,0:T(8,128)(2,1)S(1)} %broadcast_select_fusion.refs_0_), channel_id=1, source_target_pairs={{0,4},{1,5},{2,6},{3,7},{4,0},{5,1},{6,2},{7,3},{8,12},{9,13},{10,... | collective-permute-start | bytes 98312 | tf_op jit(solution)/shard_map/ppermute | solution.py:350
  46.9 4.8 %collective-permute-start.14 = (bf16[2,4,16,128]{3,2,1,0:T(8,128)(2,1)S(1)}, bf16[2,4,16,128]{3,2,1,0:T(8,128)(2,1)S(1)}, u32[]{:S(2)}, u32[]{:S(2)}) collective-permute-start(bf16[2,4,16,128]{3,2,1,0:T(8,128)(2,1)S(1)} %broadcast_select_fusion.refs_0_), channel_id=1, source_target_pairs={{0,12},{1,13},{2,14},{3,15},{4,8},{5,9},{6,10},{7,11},{8,4},{9,5},... | collective-permute-start | bytes 98312 | tf_op jit(solution)/shard_map/ppermute | solution.py:350
  47.5 7.0 %collective-permute-start.15 = (bf16[2,4,16,128]{3,2,1,0:T(8,128)(2,1)S(1)}, bf16[2,4,16,128]{3,2,1,0:T(8,128)(2,1)S(1)}, u32[]{:S(2)}, u32[]{:S(2)}) collective-permute-start(bf16[2,4,16,128]{3,2,1,0:T(8,128)(2,1)S(1)} %broadcast_select_fusion.refs_0_), channel_id=1, source_target_pairs={{0,2},{1,3},{2,0},{3,1},{4,6},{5,7},{6,4},{7,5},{8,10},{9,11},{10,... | collective-permute-start | bytes 98312 | tf_op jit(solution)/shard_map/ppermute | solution.py:350
  49.4 5.2 %collective-permute-start.16 = (bf16[2,4,16,128]{3,2,1,0:T(8,128)(2,1)S(1)}, bf16[2,4,16,128]{3,2,1,0:T(8,128)(2,1)S(1)}, u32[]{:S(2)}, u32[]{:S(2)}) collective-permute-start(bf16[2,4,16,128]{3,2,1,0:T(8,128)(2,1)S(1)} %collective-permute-done.12.refs_1_), channel_id=1, source_target_pairs={{0,2},{1,3},{2,0},{3,1},{4,6},{5,7},{6,4},{7,5},{8,10},{9,11},{10,... | collective-permute-start | bytes 98312 | tf_op jit(solution)/shard_map/ppermute | solution.py:350
  51.8 2.8 %collective-permute-start.17 = (bf16[2,4,16,128]{3,2,1,0:T(8,128)(2,1)S(1)}, bf16[2,4,16,128]{3,2,1,0:T(8,128)(2,1)S(1)}, u32[]{:S(2)}, u32[]{:S(2)}) collective-permute-start(bf16[2,4,16,128]{3,2,1,0:T(8,128)(2,1)S(1)} %collective-permute-done.13.refs_2_), channel_id=1, source_target_pairs={{0,2},{1,3},{2,0},{3,1},{4,6},{5,7},{6,4},{7,5},{8,10},{9,11},{10,... | collective-permute-start | bytes 98312 | tf_op jit(solution)/shard_map/ppermute | solution.py:350
  51.8 2.8 %collective-permute-start.18 = (bf16[2,4,16,128]{3,2,1,0:T(8,128)(2,1)S(1)}, bf16[2,4,16,128]{3,2,1,0:T(8,128)(2,1)S(1)}, u32[]{:S(2)}, u32[]{:S(2)}) collective-permute-start(bf16[2,4,16,128]{3,2,1,0:T(8,128)(2,1)S(1)} %collective-permute-done.14.refs_3_), channel_id=1, source_target_pairs={{0,2},{1,3},{2,0},{3,1},{4,6},{5,7},{6,4},{7,5},{8,10},{9,11},{10,... | collective-permute-start | bytes 98312 | tf_op jit(solution)/shard_map/ppermute | solution.py:350
  53.6 1.0 %copy-start.3 = (bf16[128,128]{1,0:T(8,128)(2,1)S(1)}, bf16[128,128]{1,0:T(8,128)(2,1)}, u32[]{:S(2)}) copy-start(bf16[128,128]{1,0:T(8,128)(2,1)} %refs_14_.3) | copy-start | bytes 98308

commit v6 on v5

--- a/solution.py
+++ b/solution.py
@@ -328,7 +328,7 @@
         if not self.fast or self.n_blk < 8:
             return [], list(range(self.n_blk))
         half = self.n_blk // 2
-        parts = [range(half // 2), range(half // 2, half - 1), range(half - 1, half)]
+        parts = [range(half // 2), range(half // 2 + 1, half), range(half // 2, half // 2 + 1)]
         groups = [[t for s in part for t in (s, s + half)] for part in parts]
         return groups[:-1] + [groups[-1][:1]], groups[-1][1:]
 
@@ -355,7 +355,7 @@
     def flip_row(self, value, bit):
         return self.move(value, lambda r, c: (r ^ bit, c))
 
-    def gather(self, own, relay):
+    def gather(self, own):
         if not self.fast:
             stacked = lax.all_gather(own, "row", axis=0)
             stacked = lax.all_to_all(stacked, "col", split_axis=0, concat_axis=0, tiled=True)
@@ -369,29 +369,22 @@
         def inside(r, c):
             return r // half == c
 
-        if relay:
-            near = self.move(own, lambda r, c: None if inside(r, c) else (r, 1 - c))
-            both = jnp.stack([own, near])
-            far = self.move(both, lambda r, c: (r ^ half, c) if inside(r, c) else None)
-            pair = jnp.where(same, both, far)
-        else:
-
-            def first(r, c):
-                return (r ^ half, c) if inside(r, c) else (r, 1 - c)
-
-            def second(r, c):
-                return None if inside(r, c) else (r ^ half, 1 - c)
-
-            near = self.move(own, first)
-            far = self.move(own, second)
-            pair = jnp.where(same, jnp.stack([own, near]), jnp.stack([near, far]))
+        def first(r, c):
+            return (r ^ half, c) if inside(r, c) else (r, 1 - c)
+
+        def second(r, c):
+            return None if inside(r, c) else (r ^ half, 1 - c)
+
+        near = self.move(own, first)
+        far = self.move(own, second)
+        pair = jnp.where(same, jnp.stack([own, near]), jnp.stack([near, far]))
         blocks = [pair]
         bit = self.n_blk // 2
         while bit:
             moved = []
             for at, block in enumerate(blocks):
                 far_bits = bit ^ self.offsets[at]
-                if relay and bit > 1:
+                if bit > 1:
                     moved.append(self.flip_row(pair, far_bits))
                 else:
                     moved.append(self.flip_row(block, bit))
@@ -442,7 +435,7 @@
                 pltpu.SemaphoreType.DMA((2,)),
             ],
         )(chain_len, pair_rep, tri_gain, sum_gain, att_gain, tri_in)
-        rights = grid.gather(right, False)
+        rights = grid.gather(right)
         lefts = [left] + [grid.shift_col(left, d) for d in range(1, n_col)]
         gate = call(gate_kernel, jax.ShapeDtypeStruct(whole, F32), 0, 3, limit)(
             pair_rep, gains, tri_in
@@ -476,7 +469,7 @@
             [left_scr, pltpu.VMEM((rows, H, cols), F32)],
             aliases={n_col + len(last) + 5: parts + 2} if sums else {},
         )(*lefts, *[rights[s] for s in last], pair_rep, gate, gains, tri_out, att_bias.T, *sums)
-        biases = grid.gather(bias, True)
+        biases = grid.gather(bias)
         others = []
         for mid in mids:
             others.append([grid.shift_col(mid, d) for d in range(1, n_col)])

time: 59 us -> 59 us (level)
  starting transfers between devices: 26.4 us -> 23.5 us
  waiting for transfers between devices: 17.9 us -> 20.6 us
    ppermute x21, starting transfers between devices: 26.4 us -> 23.5 us  [move(): return lax.ppermute(value, ('row', 'col'), pairs)]
    ppermute x21, waiting for transfers between devices: 17.9 us -> 20.6 us  [move(): return lax.ppermute(value, ('row', 'col'), pairs)]
where the time goes in v6:
time: 59 us; the launch traced here: 58.7 us
  starting transfers between devices  23.5 us (40%)
  waiting for transfers between devices  20.6 us (35%)
  Pallas kernels  13.5 us (23%)
  local copies, waits for them, and re-layouts  0.81 us (1%)
    ppermute x21, starting transfers between devices, move(): return lax.ppermute(value, ('row', 'col'), pairs)  23.5 us
    ppermute x21, waiting for transfers between devices, move(): return lax.ppermute(value, ('row', 'col'), pairs)  20.6 us
    pallas_call x10, Pallas kernels, apply(): return run(*args[:n_smem], *held)  11.4 us
    pallas_call x1, Pallas kernels, body(): pl.pallas_call(make_edge_kernel(cols, n_col, grid.col_of), name='edges',...  2.11 us
  transfers between devices with their start and end apart: 21, of which 9 were waited for; matrix products, arithmetic and copies ran while one was open for 0% of the time, Pallas kernels for 9%

profile of v6, /device:TPU:0, one launch (start us, length us, event | category | flops | bytes accessed | tf_op | source)
XLA Modules:
  0.0 58.7 jit_solution(13303986743558440321)
XLA Ops:
  0.0 2.1 %edges.1 = (bf16[16,16,128]{2,1,0:T(8,128)(2,1)S(1)}, bf16[16,16,128]{2,1,0:T(8,128)(2,1)S(1)}, f32[3,128]{1,0:T(4,128)S(1)}, f32[1,256]{1,0:T(1,128)S(1)}) custom-call(s32[4]{0:T(128)} %len_ref.1, bf16[16,128,128]{2,1,0:T(8,128)(2,1)} %refs_3_.1, f32[1,128]{1,0:T(1,128)} %bitcast.17, f32[1,128]{1,0:T(1,128)} %bitcast.18, f32[1,128]{1,0:T(1,128)} %bitcast.19, ...), custom_call_target="tpu_custom_call" | custom-call | tf_op jit(solution)/shard_map/edges/pallas_call | solution.py:413
  2.1 4.1 %collective-permute-start.1 = (bf16[16,16,128]{2,1,0:T(8,128)(2,1)S(1)}, bf16[16,16,128]{2,1,0:T(8,128)(2,1)S(1)}, u32[]{:S(2)}, u32[]{:S(2)}) collective-permute-start(bf16[16,16,128]{2,1,0:T(8,128)(2,1)S(1)} %get-tuple-element.22), channel_id=1, source_target_pairs={{0,16},{1,0},{2,18},{3,2},{4,20},{5,4},{6,22},{7,6},{8,24},{9,8},{... | collective-permute-start | bytes 196616 | tf_op jit(solution)/shard_map/ppermute | solution.py:350
  6.2 0.7 %collective-permute-start.2 = (bf16[16,16,128]{2,1,0:T(8,128)(2,1)S(1)}, bf16[16,16,128]{2,1,0:T(8,128)(2,1)S(1)}, u32[]{:S(2)}, u32[]{:S(2)}) collective-permute-start(bf16[16,16,128]{2,1,0:T(8,128)(2,1)S(1)} %get-tuple-element.22), channel_id=1, source_target_pairs={{1,16},{3,18},{5,20},{7,22},{9,24},{11,26},{13,28},{15,30},{16,1},... | collective-permute-start | bytes 196616 | tf_op jit(solution)/shard_map/ppermute | solution.py:350
  6.9 1.2 %collective-permute-done.1 = bf16[16,16,128]{2,1,0:T(8,128)(2,1)S(1)} collective-permute-done((bf16[16,16,128]{2,1,0:T(8,128)(2,1)S(1)}, bf16[16,16,128]{2,1,0:T(8,128)(2,1)S(1)}, u32[]{:S(2)}, u32[]{:S(2)}) %collective-permute-start.1) | collective-permute-done | bytes 65568 | tf_op jit(solution)/shard_map/ppermute | solution.py:350
  8.1 0.0 collective-permute-done.2
  8.2 2.4 %collective-permute-start.8 = (bf16[2,16,16,128]{3,2,1,0:T(8,128)(2,1)S(1)}, bf16[2,16,16,128]{3,2,1,0:T(8,128)(2,1)S(1)}, u32[]{:S(2)}, u32[]{:S(2)}) collective-permute-start(bf16[2,16,16,128]{3,2,1,0:T(8,128)(2,1)S(1)} %maximum_select_fusion.refs_2_), channel_id=1, source_target_pairs={{0,8},{1,9},{2,10},{3,11},{4,12},{5,13},{6,14},{7,15},{8,0},{9,1},... | collective-permute-start | bytes 393224 | tf_op jit(solution)/shard_map/ppermute | solution.py:350
  10.6 1.0 %collective-permute-start.5 = (bf16[2,16,16,128]{3,2,1,0:T(8,128)(2,1)S(1)}, bf16[2,16,16,128]{3,2,1,0:T(8,128)(2,1)S(1)}, u32[]{:S(2)}, u32[]{:S(2)}) collective-permute-start(bf16[2,16,16,128]{3,2,1,0:T(8,128)(2,1)S(1)} %maximum_select_fusion.refs_2_), channel_id=1, source_target_pairs={{0,12},{1,13},{2,14},{3,15},{4,8},{5,9},{6,10},{7,11},{8,4},{9,5},... | collective-permute-start | bytes 393224 | tf_op jit(solution)/shard_map/ppermute | solution.py:350
  11.6 0.5 collective-permute-start.3
  12.1 0.0 collective-permute-start.7
  12.1 3.3 %collective-permute-done.8.refs_4_ = bf16[2,16,16,128]{3,2,1,0:T(8,128)(2,1)S(1)} collective-permute-done((bf16[2,16,16,128]{3,2,1,0:T(8,128)(2,1)S(1)}, bf16[2,16,16,128]{3,2,1,0:T(8,128)(2,1)S(1)}, u32[]{:S(2)}, u32[]{:S(2)}) %collective-permute-start.8) | collective-permute-done | bytes 131104 | tf_op jit(solution)/shard_map/ppermute | solution.py:350
  15.4 2.9 %collective-permute-done.5.refs_2_ = bf16[2,16,16,128]{3,2,1,0:T(8,128)(2,1)S(1)} collective-permute-done((bf16[2,16,16,128]{3,2,1,0:T(8,128)(2,1)S(1)}, bf16[2,16,16,128]{3,2,1,0:T(8,128)(2,1)S(1)}, u32[]{:S(2)}, u32[]{:S(2)}) %collective-permute-start.5) | collective-permute-done | bytes 131104 | tf_op jit(solution)/shard_map/ppermute | solution.py:350
  18.3 0.0 collective-permute-start.6
  18.3 0.7 %collective-permute-done.3.refs_2_ = bf16[2,16,16,128]{3,2,1,0:T(8,128)(2,1)S(1)} collective-permute-done((bf16[2,16,16,128]{3,2,1,0:T(8,128)(2,1)S(1)}, bf16[2,16,16,128]{3,2,1,0:T(8,128)(2,1)S(1)}, u32[]{:S(2)}, u32[]{:S(2)}) %collective-permute-start.3) | collective-permute-done | bytes 131104 | tf_op jit(solution)/shard_map/ppermute | solution.py:350
  19.0 0.0 collective-permute-start.4
  19.0 3.8 %collective-permute-start = (bf16[16,16,128]{2,1,0:T(8,128)(2,1)S(1)}, bf16[16,16,128]{2,1,0:T(8,128)(2,1)S(1)}, u32[]{:S(2)}, u32[]{:S(2)}) collective-permute-start(bf16[16,16,128]{2,1,0:T(8,128)(2,1)S(1)} %get-tuple-element.21.refs_0_), channel_id=1, source_target_pairs={{0,1},{1,0},{2,3},{3,2},{4,5},{5,4},{6,7},{7,6},{8,9},{9,8},{10,11... | collective-permute-start | bytes 196616 | tf_op jit(solution)/shard_map/ppermute | solution.py:350
  22.8 0.9 %shard_map.100.refs_4_ = f32[16,128,128]{2,1,0:T(8,128)S(1)} custom-call(bf16[16,128,128]{2,1,0:T(8,128)(2,1)S(1)} %copy-done, f32[3,128]{1,0:T(4,128)S(1)} %get-tuple-element.23.gains_ref.refs_5_.refs_3_, bf16[128,640]{1,0:T(8,128)(2,1)S(1)} %copy-done.2), custom_call_target="tpu_custom_call" | custom-call | tf_op jit(solution)/shard_map/pallas_call | solution.py:69
  23.8 1.8 %collective-permute-done.refs_1_ = bf16[16,16,128]{2,1,0:T(8,128)(2,1)S(1)} collective-permute-done((bf16[16,16,128]{2,1,0:T(8,128)(2,1)S(1)}, bf16[16,16,128]{2,1,0:T(8,128)(2,1)S(1)}, u32[]{:S(2)}, u32[]{:S(2)}) %collective-permute-start) | collective-permute-done | bytes 65568 | tf_op jit(solution)/shard_map/ppermute | solution.py:350
  25.6 1.3 %shard_map.101.refs_4_ = f32[16,128,128]{2,1,0:T(8,128)S(1)} custom-call(bf16[16,16,128]{2,1,0:T(8,128)(2,1)S(1)} %get-tuple-element.21.refs_0_, bf16[16,16,128]{2,1,0:T(8,128)(2,1)S(1)} %collective-permute-done.refs_1_, bf16[2,16,16,128]{3,2,1,0:T(8,128)(2,1)S(1)} %maximum_select_fusion.refs_2_, ...), custom_call_target="tpu_custom_call" | custom-call | tf_op jit(solution)/shard_map/pallas_call | solution.py:69
  26.9 0.0 collective-permute-done.6.refs_3_
  26.9 0.7 %shard_map.102.refs_3_ = f32[16,128,128]{2,1,0:T(8,128)S(1)} custom-call(bf16[16,16,128]{2,1,0:T(8,128)(2,1)S(1)} %get-tuple-element.21.refs_0_, bf16[16,16,128]{2,1,0:T(8,128)(2,1)S(1)} %collective-permute-done.refs_1_, bf16[2,16,16,128]{3,2,1,0:T(8,128)(2,1)S(1)} %collective-permute-done.5.refs_2_, ...), custom_call_target="tpu_custom_call", output_to_operand_aliasing={{}: (4, {})} | custom-call | tf_op jit(solution)/shard_map/pallas_call | solution.py:69
  27.6 0.3 shard_map.103.refs_8_
  28.0 0.0 copy-start.5
  28.0 0.4 copy-done.4
  28.4 0.3 copy-done.5
  28.7 2.2 %shard_map.104 = (bf16[8,128,128]{2,1,0:T(8,128)(2,1)S(1)}, bf16[8,128,128]{2,1,0:T(8,128)(2,1)S(1)}, bf16[16,128,128]{2,1,0:T(8,128)(2,1)S(1)}, bf16[4,16,128]{2,1,0:T(8,128)(2,1)S(1)}, f32[16,128,128]{2,1,0:T(8,128)S(1)}) custom-call(bf16[16,16,128]{2,1,0:T(8,128)(2,1)S(1)} %get-tuple-element.21.refs_0_, ...), custom_call_target="tpu_custom_call", output_to_operand_aliasing={{4}: (8, {})} | custom-call | tf_op jit(solution)/shard_map/pallas_call | solution.py:69
  30.8 1.8 %collective-permute-start.20 = (bf16[8,128,128]{2,1,0:T(8,128)(2,1)S(1)}, bf16[8,128,128]{2,1,0:T(8,128)(2,1)S(1)}, u32[]{:S(2)}, u32[]{:S(2)}) collective-permute-start(bf16[8,128,128]{2,1,0:T(8,128)(2,1)S(1)} %get-tuple-element.34.refs_12_), channel_id=1, source_target_pairs={{0,1},{1,0},{2,3},{3,2},{4,5},{5,4},{6,7},{7,6},{8,9},{9,8},{10,11... | collective-permute-start | bytes 786440 | tf_op jit(solution)/shard_map/ppermute | solution.py:350
  32.6 0.3 collective-permute-start.19
  32.9 4.2 %collective-permute-start.10 = (bf16[4,16,128]{2,1,0:T(8,128)(2,1)S(1)}, bf16[4,16,128]{2,1,0:T(8,128)(2,1)S(1)}, u32[]{:S(2)}, u32[]{:S(2)}) collective-permute-start(bf16[4,16,128]{2,1,0:T(8,128)(2,1)S(1)} %get-tuple-element.24), channel_id=1, source_target_pairs={{0,16},{1,0},{2,18},{3,2},{4,20},{5,4},{6,22},{7,6},{8,24},{9,8},{... | collective-permute-start | bytes 49160 | tf_op jit(solution)/shard_map/ppermute | solution.py:350
  37.1 0.7 %collective-permute-start.11 = (bf16[4,16,128]{2,1,0:T(8,128)(2,1)S(1)}, bf16[4,16,128]{2,1,0:T(8,128)(2,1)S(1)}, u32[]{:S(2)}, u32[]{:S(2)}) collective-permute-start(bf16[4,16,128]{2,1,0:T(8,128)(2,1)S(1)} %get-tuple-element.24), channel_id=1, source_target_pairs={{1,16},{3,18},{5,20},{7,22},{9,24},{11,26},{13,28},{15,30},{16,1},... | collective-permute-start | bytes 49160 | tf_op jit(solution)/shard_map/ppermute | solution.py:350
  37.8 7.2 %collective-permute-done.10 = bf16[4,16,128]{2,1,0:T(8,128)(2,1)S(1)} collective-permute-done((bf16[4,16,128]{2,1,0:T(8,128)(2,1)S(1)}, bf16[4,16,128]{2,1,0:T(8,128)(2,1)S(1)}, u32[]{:S(2)}, u32[]{:S(2)}) %collective-permute-start.10) | collective-permute-done | bytes 16416 | tf_op jit(solution)/shard_map/ppermute | solution.py:350
  45.0 1.6 %collective-permute-start.12 = (bf16[2,4,16,128]{3,2,1,0:T(8,128)(2,1)S(1)}, bf16[2,4,16,128]{3,2,1,0:T(8,128)(2,1)S(1)}, u32[]{:S(2)}, u32[]{:S(2)}) collective-permute-start(bf16[2,4,16,128]{3,2,1,0:T(8,128)(2,1)S(1)} %maximum_select_fusion.1.refs_0_), channel_id=1, source_target_pairs={{0,8},{1,9},{2,10},{3,11},{4,12},{5,13},{6,14},{7,15},{8,0},{9,1},... | collective-permute-start | bytes 98312 | tf_op jit(solution)/shard_map/ppermute | solution.py:350
  46.6 0.5 collective-permute-start.13
  47.2 1.4 %collective-permute-start.14 = (bf16[2,4,16,128]{3,2,1,0:T(8,128)(2,1)S(1)}, bf16[2,4,16,128]{3,2,1,0:T(8,128)(2,1)S(1)}, u32[]{:S(2)}, u32[]{:S(2)}) collective-permute-start(bf16[2,4,16,128]{3,2,1,0:T(8,128)(2,1)S(1)} %maximum_select_fusion.1.refs_0_), channel_id=1, source_target_pairs={{0,12},{1,13},{2,14},{3,15},{4,8},{5,9},{6,10},{7,11},{8,4},{9,5},... | collective-permute-start | bytes 98312 | tf_op jit(solution)/shard_map/ppermute | solution.py:350
  48.5 0.4 collective-permute-done.12.refs_1_
  49.0 1.5 %collective-permute-done.13.refs_2_ = bf16[2,4,16,128]{3,2,1,0:T(8,128)(2,1)S(1)} collective-permute-done((bf16[2,4,16,128]{3,2,1,0:T(8,128)(2,1)S(1)}, bf16[2,4,16,128]{3,2,1,0:T(8,128)(2,1)S(1)}, u32[]{:S(2)}, u32[]{:S(2)}) %collective-permute-start.13) | collective-permute-done | bytes 32800 | tf_op jit(solution)/shard_map/ppermute | solution.py:350
  50.5 0.0 collective-permute-start.16
  50.5 1.4 %collective-permute-done.14.refs_3_ = bf16[2,4,16,128]{3,2,1,0:T(8,128)(2,1)S(1)} collective-permute-done((bf16[2,4,16,128]{3,2,1,0:T(8,128)(2,1)S(1)}, bf16[2,4,16,128]{3,2,1,0:T(8,128)(2,1)S(1)}, u32[]{:S(2)}, u32[]{:S(2)}) %collective-permute-start.14) | collective-permute-done | bytes 32800 | tf_op jit(solution)/shard_map/ppermute | solution.py:350
  52.0 0.0 collective-permute-done.20.refs_0_
  52.0 0.5 collective-permute-start.18
  52.5 0.7 %shard_map.105 = (bf16[16,128,128]{2,1,0:T(8,128)(2,1)S(1)}, bf16[16,128,128]{2,1,0:T(8,128)(2,1)S(1)}, bf16[16,128,128]{2,1,0:T(8,128)(2,1)S(1)}, f32[16,128,128]{2,1,0:T(8,128)S(1)}) custom-call(bf16[16,128,128]{2,1,0:T(8,128)(2,1)S(1)} %get-tuple-element.25.norm_ref, bf16[128,512]{1,0:T(8,128)(2,1)S(1)} %copy-done.1), custom_call_target="tpu_custom_call" | custom-call | tf_op jit(solution)/shard_map/pallas_call | solution.py:69
  53.2 0.6 shard_map.107
  53.8 0.0 copy-start.3
  53.8 0.0 collective-permute-done.19.refs_0_
  53.8 0.6 shard_map.106
  54.4 0.0 collective-permute-done.15.refs_4_
  54.4 0.1 copy-done.3
  54.5 1.7 %shard_map.108.refs_15_ = bf16[8,128,128]{2,1,0:T(8,128)(2,1)S(1)} custom-call(bf16[2,4,16,128]{3,2,1,0:T(8,128)(2,1)S(1)} %maximum_select_fusion.1.refs_0_, bf16[2,4,16,128]{3,2,1,0:T(8,128)(2,1)S(1)} %collective-permute-done.12.refs_1_, bf16[2,4,16,128]{3,2,1,0:T(8,128)(2,1)S(1)} %collective-permute-done.13.refs_2_, ...), custom_call_target="tpu_custom_call" | custom-call | tf_op jit(solution)/shard_map/pallas_call | solution.py:69
  56.2 2.5 %shard_map.109 = bf16[16,128,128]{2,1,0:T(8,128)(2,1)} custom-call(bf16[2,4,16,128]{3,2,1,0:T(8,128)(2,1)S(1)} %maximum_select_fusion.1.refs_0_, bf16[2,4,16,128]{3,2,1,0:T(8,128)(2,1)S(1)} %collective-permute-done.12.refs_1_, bf16[2,4,16,128]{3,2,1,0:T(8,128)(2,1)S(1)} %collective-permute-done.13.refs_2_, ...), custom_call_target="tpu_custom_call" | custom-call | tf_op jit(solution)/shard_map/pallas_call | solution.py:69
  (19 shorter events, 0.1 us)
Async XLA Ops:
  0.0 22.8 %copy-start = (bf16[16,128,128]{2,1,0:T(8,128)(2,1)S(1)}, bf16[16,128,128]{2,1,0:T(8,128)(2,1)}, u32[]{:S(2)}) copy-start(bf16[16,128,128]{2,1,0:T(8,128)(2,1)} %refs_3_.1) | copy-start | bytes 1572868
  2.1 6.0 %collective-permute-start.1 = (bf16[16,16,128]{2,1,0:T(8,128)(2,1)S(1)}, bf16[16,16,128]{2,1,0:T(8,128)(2,1)S(1)}, u32[]{:S(2)}, u32[]{:S(2)}) collective-permute-start(bf16[16,16,128]{2,1,0:T(8,128)(2,1)S(1)} %get-tuple-element.22), channel_id=1, source_target_pairs={{0,16},{1,0},{2,18},{3,2},{4,20},{5,4},{6,22},{7,6},{8,24},{9,8},{... | collective-permute-start | bytes 196616 | tf_op jit(solution)/shard_map/ppermute | solution.py:350
  6.2 1.9 %collective-permute-start.2 = (bf16[16,16,128]{2,1,0:T(8,128)(2,1)S(1)}, bf16[16,16,128]{2,1,0:T(8,128)(2,1)S(1)}, u32[]{:S(2)}, u32[]{:S(2)}) collective-permute-start(bf16[16,16,128]{2,1,0:T(8,128)(2,1)S(1)} %get-tuple-element.22), channel_id=1, source_target_pairs={{1,16},{3,18},{5,20},{7,22},{9,24},{11,26},{13,28},{15,30},{16,1},... | collective-permute-start | bytes 196616 | tf_op jit(solution)/shard_map/ppermute | solution.py:350
  8.1 14.7 %copy-start.2 = (bf16[128,640]{1,0:T(8,128)(2,1)S(1)}, bf16[128,640]{1,0:T(8,128)(2,1)}, u32[]{:S(2)}) copy-start(bf16[128,640]{1,0:T(8,128)(2,1)} %w_ref.4) | copy-start | bytes 491524
  8.2 7.2 %collective-permute-start.8 = (bf16[2,16,16,128]{3,2,1,0:T(8,128)(2,1)S(1)}, bf16[2,16,16,128]{3,2,1,0:T(8,128)(2,1)S(1)}, u32[]{:S(2)}, u32[]{:S(2)}) collective-permute-start(bf16[2,16,16,128]{3,2,1,0:T(8,128)(2,1)S(1)} %maximum_select_fusion.refs_2_), channel_id=1, source_target_pairs={{0,8},{1,9},{2,10},{3,11},{4,12},{5,13},{6,14},{7,15},{8,0},{9,1},... | collective-permute-start | bytes 393224 | tf_op jit(solution)/shard_map/ppermute | solution.py:350
  10.6 7.7 %collective-permute-start.5 = (bf16[2,16,16,128]{3,2,1,0:T(8,128)(2,1)S(1)}, bf16[2,16,16,128]{3,2,1,0:T(8,128)(2,1)S(1)}, u32[]{:S(2)}, u32[]{:S(2)}) collective-permute-start(bf16[2,16,16,128]{3,2,1,0:T(8,128)(2,1)S(1)} %maximum_select_fusion.refs_2_), channel_id=1, source_target_pairs={{0,12},{1,13},{2,14},{3,15},{4,8},{5,9},{6,10},{7,11},{8,4},{9,5},... | collective-permute-start | bytes 393224 | tf_op jit(solution)/shard_map/ppermute | solution.py:350
  11.6 7.5 %collective-permute-start.3 = (bf16[2,16,16,128]{3,2,1,0:T(8,128)(2,1)S(1)}, bf16[2,16,16,128]{3,2,1,0:T(8,128)(2,1)S(1)}, u32[]{:S(2)}, u32[]{:S(2)}) collective-permute-start(bf16[2,16,16,128]{3,2,1,0:T(8,128)(2,1)S(1)} %maximum_select_fusion.refs_2_), channel_id=1, source_target_pairs={{0,4},{1,5},{2,6},{3,7},{4,0},{5,1},{6,2},{7,3},{8,12},{9,13},{10,... | collective-permute-start | bytes 393224 | tf_op jit(solution)/shard_map/ppermute | solution.py:350
  12.1 13.5 %collective-permute-start.7 = (bf16[2,16,16,128]{3,2,1,0:T(8,128)(2,1)S(1)}, bf16[2,16,16,128]{3,2,1,0:T(8,128)(2,1)S(1)}, u32[]{:S(2)}, u32[]{:S(2)}) collective-permute-start(bf16[2,16,16,128]{3,2,1,0:T(8,128)(2,1)S(1)} %maximum_select_fusion.refs_2_), channel_id=1, source_target_pairs={{0,2},{1,3},{2,0},{3,1},{4,6},{5,7},{6,4},{7,5},{8,10},{9,11},{10,... | collective-permute-start | bytes 393224 | tf_op jit(solution)/shard_map/ppermute | solution.py:350
  15.4 10.2 %collective-permute-start.9 = (bf16[2,16,16,128]{3,2,1,0:T(8,128)(2,1)S(1)}, bf16[2,16,16,128]{3,2,1,0:T(8,128)(2,1)S(1)}, u32[]{:S(2)}, u32[]{:S(2)}) collective-permute-start(bf16[2,16,16,128]{3,2,1,0:T(8,128)(2,1)S(1)} %collective-permute-done.8.refs_4_), channel_id=1, source_target_pairs={{0,2},{1,3},{2,0},{3,1},{4,6},{5,7},{6,4},{7,5},{8,10},{9,11},{10,... | collective-permute-start | bytes 393224 | tf_op jit(solution)/shard_map/ppermute | solution.py:350
  18.3 8.6 %collective-permute-start.6 = (bf16[2,16,16,128]{3,2,1,0:T(8,128)(2,1)S(1)}, bf16[2,16,16,128]{3,2,1,0:T(8,128)(2,1)S(1)}, u32[]{:S(2)}, u32[]{:S(2)}) collective-permute-start(bf16[2,16,16,128]{3,2,1,0:T(8,128)(2,1)S(1)} %collective-permute-done.5.refs_2_), channel_id=1, source_target_pairs={{0,2},{1,3},{2,0},{3,1},{4,6},{5,7},{6,4},{7,5},{8,10},{9,11},{10,... | collective-permute-start | bytes 393224 | tf_op jit(solution)/shard_map/ppermute | solution.py:350
  19.0 8.9 %collective-permute-start.4 = (bf16[2,16,16,128]{3,2,1,0:T(8,128)(2,1)S(1)}, bf16[2,16,16,128]{3,2,1,0:T(8,128)(2,1)S(1)}, u32[]{:S(2)}, u32[]{:S(2)}) collective-permute-start(bf16[2,16,16,128]{3,2,1,0:T(8,128)(2,1)S(1)} %collective-permute-done.3.refs_2_), channel_id=1, source_target_pairs={{0,2},{1,3},{2,0},{3,1},{4,6},{5,7},{6,4},{7,5},{8,10},{9,11},{10,... | collective-permute-start | bytes 393224 | tf_op jit(solution)/shard_map/ppermute | solution.py:350
  19.0 6.6 %collective-permute-start = (bf16[16,16,128]{2,1,0:T(8,128)(2,1)S(1)}, bf16[16,16,128]{2,1,0:T(8,128)(2,1)S(1)}, u32[]{:S(2)}, u32[]{:S(2)}) collective-permute-start(bf16[16,16,128]{2,1,0:T(8,128)(2,1)S(1)} %get-tuple-element.21.refs_0_), channel_id=1, source_target_pairs={{0,1},{1,0},{2,3},{3,2},{4,5},{5,4},{6,7},{7,6},{8,9},{9,8},{10,11... | collective-permute-start | bytes 196616 | tf_op jit(solution)/shard_map/ppermute | solution.py:350
  27.6 0.8 %copy-start.4 = (bf16[128,128]{1,0:T(8,128)(2,1)S(1)}, bf16[128,128]{1,0:T(8,128)(2,1)}, u32[]{:S(2)}) copy-start(bf16[128,128]{1,0:T(8,128)(2,1)} %refs_6_.1) | copy-start | bytes 98308
  28.0 0.7 %copy-start.5 = (bf16[128,4]{0,1:T(4,128)(2,1)S(1)}, bf16[128,4]{0,1:T(4,128)(2,1)}, u32[]{:S(2)}) copy-start(bf16[128,4]{0,1:T(4,128)(2,1)} %param.18) | copy-start | bytes 3076
  28.6 23.8 %copy-start.1 = (bf16[128,512]{1,0:T(8,128)(2,1)S(1)}, bf16[128,512]{1,0:T(8,128)(2,1)}, u32[]{:S(2)}) copy-start(bf16[128,512]{1,0:T(8,128)(2,1)} %refs_4_.3) | copy-start | bytes 393220
  30.8 21.2 %collective-permute-start.20 = (bf16[8,128,128]{2,1,0:T(8,128)(2,1)S(1)}, bf16[8,128,128]{2,1,0:T(8,128)(2,1)S(1)}, u32[]{:S(2)}, u32[]{:S(2)}) collective-permute-start(bf16[8,128,128]{2,1,0:T(8,128)(2,1)S(1)} %get-tuple-element.34.refs_12_), channel_id=1, source_target_pairs={{0,1},{1,0},{2,3},{3,2},{4,5},{5,4},{6,7},{7,6},{8,9},{9,8},{10,11... | collective-permute-start | bytes 786440 | tf_op jit(solution)/shard_map/ppermute | solution.py:350
  32.6 21.2 %collective-permute-start.19 = (bf16[8,128,128]{2,1,0:T(8,128)(2,1)S(1)}, bf16[8,128,128]{2,1,0:T(8,128)(2,1)S(1)}, u32[]{:S(2)}, u32[]{:S(2)}) collective-permute-start(bf16[8,128,128]{2,1,0:T(8,128)(2,1)S(1)} %get-tuple-element.27.refs_12_), channel_id=1, source_target_pairs={{0,1},{1,0},{2,3},{3,2},{4,5},{5,4},{6,7},{7,6},{8,9},{9,8},{10,11... | collective-permute-start | bytes 786440 | tf_op jit(solution)/shard_map/ppermute | solution.py:350
  32.9 12.1 %collective-permute-start.10 = (bf16[4,16,128]{2,1,0:T(8,128)(2,1)S(1)}, bf16[4,16,128]{2,1,0:T(8,128)(2,1)S(1)}, u32[]{:S(2)}, u32[]{:S(2)}) collective-permute-start(bf16[4,16,128]{2,1,0:T(8,128)(2,1)S(1)} %get-tuple-element.24), channel_id=1, source_target_pairs={{0,16},{1,0},{2,18},{3,2},{4,20},{5,4},{6,22},{7,6},{8,24},{9,8},{... | collective-permute-start | bytes 49160 | tf_op jit(solution)/shard_map/ppermute | solution.py:350
  37.1 7.9 %collective-permute-start.11 = (bf16[4,16,128]{2,1,0:T(8,128)(2,1)S(1)}, bf16[4,16,128]{2,1,0:T(8,128)(2,1)S(1)}, u32[]{:S(2)}, u32[]{:S(2)}) collective-permute-start(bf16[4,16,128]{2,1,0:T(8,128)(2,1)S(1)} %get-tuple-element.24), channel_id=1, source_target_pairs={{1,16},{3,18},{5,20},{7,22},{9,24},{11,26},{13,28},{15,30},{16,1},... | collective-permute-start | bytes 49160 | tf_op jit(solution)/shard_map/ppermute | solution.py:350
  45.0 4.0 %collective-permute-start.12 = (bf16[2,4,16,128]{3,2,1,0:T(8,128)(2,1)S(1)}, bf16[2,4,16,128]{3,2,1,0:T(8,128)(2,1)S(1)}, u32[]{:S(2)}, u32[]{:S(2)}) collective-permute-start(bf16[2,4,16,128]{3,2,1,0:T(8,128)(2,1)S(1)} %maximum_select_fusion.1.refs_0_), channel_id=1, source_target_pairs={{0,8},{1,9},{2,10},{3,11},{4,12},{5,13},{6,14},{7,15},{8,0},{9,1},... | collective-permute-start | bytes 98312 | tf_op jit(solution)/shard_map/ppermute | solution.py:350
  46.6 3.9 %collective-permute-start.13 = (bf16[2,4,16,128]{3,2,1,0:T(8,128)(2,1)S(1)}, bf16[2,4,16,128]{3,2,1,0:T(8,128)(2,1)S(1)}, u32[]{:S(2)}, u32[]{:S(2)}) collective-permute-start(bf16[2,4,16,128]{3,2,1,0:T(8,128)(2,1)S(1)} %maximum_select_fusion.1.refs_0_), channel_id=1, source_target_pairs={{0,4},{1,5},{2,6},{3,7},{4,0},{5,1},{6,2},{7,3},{8,12},{9,13},{10,... | collective-permute-start | bytes 98312 | tf_op jit(solution)/shard_map/ppermute | solution.py:350
  47.2 4.8 %collective-permute-start.14 = (bf16[2,4,16,128]{3,2,1,0:T(8,128)(2,1)S(1)}, bf16[2,4,16,128]{3,2,1,0:T(8,128)(2,1)S(1)}, u32[]{:S(2)}, u32[]{:S(2)}) collective-permute-start(bf16[2,4,16,128]{3,2,1,0:T(8,128)(2,1)S(1)} %maximum_select_fusion.1.refs_0_), channel_id=1, source_target_pairs={{0,12},{1,13},{2,14},{3,15},{4,8},{5,9},{6,10},{7,11},{8,4},{9,5},... | collective-permute-start | bytes 98312 | tf_op jit(solution)/shard_map/ppermute | solution.py:350
  49.0 5.4 %collective-permute-start.15 = (bf16[2,4,16,128]{3,2,1,0:T(8,128)(2,1)S(1)}, bf16[2,4,16,128]{3,2,1,0:T(8,128)(2,1)S(1)}, u32[]{:S(2)}, u32[]{:S(2)}) collective-permute-start(bf16[2,4,16,128]{3,2,1,0:T(8,128)(2,1)S(1)} %maximum_select_fusion.1.refs_0_), channel_id=1, source_target_pairs={{0,2},{1,3},{2,0},{3,1},{4,6},{5,7},{6,4},{7,5},{8,10},{9,11},{10,... | collective-permute-start | bytes 98312 | tf_op jit(solution)/shard_map/ppermute | solution.py:350
  50.5 3.9 %collective-permute-start.16 = (bf16[2,4,16,128]{3,2,1,0:T(8,128)(2,1)S(1)}, bf16[2,4,16,128]{3,2,1,0:T(8,128)(2,1)S(1)}, u32[]{:S(2)}, u32[]{:S(2)}) collective-permute-start(bf16[2,4,16,128]{3,2,1,0:T(8,128)(2,1)S(1)} %collective-permute-done.12.refs_1_), channel_id=1, source_target_pairs={{0,2},{1,3},{2,0},{3,1},{4,6},{5,7},{6,4},{7,5},{8,10},{9,11},{10,... | collective-permute-start | bytes 98312 | tf_op jit(solution)/shard_map/ppermute | solution.py:350
  52.0 2.4 %collective-permute-start.17 = (bf16[2,4,16,128]{3,2,1,0:T(8,128)(2,1)S(1)}, bf16[2,4,16,128]{3,2,1,0:T(8,128)(2,1)S(1)}, u32[]{:S(2)}, u32[]{:S(2)}) collective-permute-start(bf16[2,4,16,128]{3,2,1,0:T(8,128)(2,1)S(1)} %collective-permute-done.13.refs_2_), channel_id=1, source_target_pairs={{0,2},{1,3},{2,0},{3,1},{4,6},{5,7},{6,4},{7,5},{8,10},{9,11},{10,... | collective-permute-start | bytes 98312 | tf_op jit(solution)/shard_map/ppermute | solution.py:350
  52.0 2.4 %collective-permute-start.18 = (bf16[2,4,16,128]{3,2,1,0:T(8,128)(2,1)S(1)}, bf16[2,4,16,128]{3,2,1,0:T(8,128)(2,1)S(1)}, u32[]{:S(2)}, u32[]{:S(2)}) collective-permute-start(bf16[2,4,16,128]{3,2,1,0:T(8,128)(2,1)S(1)} %collective-permute-done.14.refs_3_), channel_id=1, source_target_pairs={{0,2},{1,3},{2,0},{3,1},{4,6},{5,7},{6,4},{7,5},{8,10},{9,11},{10,... | collective-permute-start | bytes 98312 | tf_op jit(solution)/shard_map/ppermute | solution.py:350
  53.8 0.8 %copy-start.3 = (bf16[128,128]{1,0:T(8,128)(2,1)S(1)}, bf16[128,128]{1,0:T(8,128)(2,1)}, u32[]{:S(2)}) copy-start(bf16[128,128]{1,0:T(8,128)(2,1)} %refs_14_.3) | copy-start | bytes 98308

commit v7 on v6

--- a/solution.py
+++ b/solution.py
@@ -328,7 +328,7 @@
         if not self.fast or self.n_blk < 8:
             return [], list(range(self.n_blk))
         half = self.n_blk // 2
-        parts = [range(half // 2), range(half // 2 + 1, half), range(half // 2, half // 2 + 1)]
+        parts = [range(half // 2), range(half // 2, half - 1), range(half - 1, half)]
         groups = [[t for s in part for t in (s, s + half)] for part in parts]
         return groups[:-1] + [groups[-1][:1]], groups[-1][1:]
 
@@ -355,7 +355,7 @@
     def flip_row(self, value, bit):
         return self.move(value, lambda r, c: (r ^ bit, c))
 
-    def gather(self, own):
+    def gather(self, own, direct):
         if not self.fast:
             stacked = lax.all_gather(own, "row", axis=0)
             stacked = lax.all_to_all(stacked, "col", split_axis=0, concat_axis=0, tiled=True)
@@ -384,7 +384,7 @@
             moved = []
             for at, block in enumerate(blocks):
                 far_bits = bit ^ self.offsets[at]
-                if bit > 1:
+                if direct and bit > 1:
                     moved.append(self.flip_row(pair, far_bits))
                 else:
                     moved.append(self.flip_row(block, bit))
@@ -435,7 +435,7 @@
                 pltpu.SemaphoreType.DMA((2,)),
             ],
         )(chain_len, pair_rep, tri_gain, sum_gain, att_gain, tri_in)
-        rights = grid.gather(right)
+        rights = grid.gather(right, False)
         lefts = [left] + [grid.shift_col(left, d) for d in range(1, n_col)]
         gate = call(gate_kernel, jax.ShapeDtypeStruct(whole, F32), 0, 3, limit)(
             pair_rep, gains, tri_in
@@ -469,7 +469,7 @@
             [left_scr, pltpu.VMEM((rows, H, cols), F32)],
             aliases={n_col + len(last) + 5: parts + 2} if sums else {},
         )(*lefts, *[rights[s] for s in last], pair_rep, gate, gains, tri_out, att_bias.T, *sums)
-        biases = grid.gather(bias)
+        biases = grid.gather(bias, True)
         others = []
         for mid in mids:
             others.append([grid.shift_col(mid, d) for d in range(1, n_col)])

time: 59 us -> 60.8 us (1.031)
  starting transfers between devices: 23.5 us -> 25.6 us
    ppermute x21, starting transfers between devices: 23.5 us -> 25.6 us  [move(): return lax.ppermute(value, ('row', 'col'), pairs)]
  transfers between devices with their start and end apart: 21 -> 21, of which waited for: 9 -> 8; matrix products, arithmetic and copies ran while one was open for 0% -> 0% of each run, Pallas kernels for 9% -> 8%
where the time goes in v7:
time: 60.8 us; the launch traced here: 60.5 us
  starting transfers between devices  25.6 us (42%)
  waiting for transfers between devices  20.3 us (33%)
  Pallas kernels  13.5 us (22%)
  local copies, waits for them, and re-layouts  0.81 us (1%)
    ppermute x21, starting transfers between devices, move(): return lax.ppermute(value, ('row', 'col'), pairs)  25.6 us
    ppermute x21, waiting for transfers between devices, move(): return lax.ppermute(value, ('row', 'col'), pairs)  20.3 us
    pallas_call x10, Pallas kernels, apply(): return run(*args[:n_smem], *held)  11.4 us
    pallas_call x1, Pallas kernels, body(): pl.pallas_call(make_edge_kernel(cols, n_col, grid.col_of), name='edges',...  2.11 us
  transfers between devices with their start and end apart: 21, of which 8 were waited for; matrix products, arithmetic and copies ran while one was open for 0% of the time, Pallas kernels for 8%

profile of v7, /device:TPU:0, one launch (start us, length us, event | category | flops | bytes accessed | tf_op | source)
XLA Modules:
  0.0 60.5 jit_solution(11844746416139782603)
XLA Ops:
  0.0 2.1 %edges.1 = (bf16[16,16,128]{2,1,0:T(8,128)(2,1)S(1)}, bf16[16,16,128]{2,1,0:T(8,128)(2,1)S(1)}, f32[3,128]{1,0:T(4,128)S(1)}, f32[1,256]{1,0:T(1,128)S(1)}) custom-call(s32[4]{0:T(128)} %len_ref.1, bf16[16,128,128]{2,1,0:T(8,128)(2,1)} %refs_3_.1, f32[1,128]{1,0:T(1,128)} %bitcast.17, f32[1,128]{1,0:T(1,128)} %bitcast.18, f32[1,128]{1,0:T(1,128)} %bitcast.19, ...), custom_call_target="tpu_custom_call" | custom-call | tf_op jit(solution)/shard_map/edges/pallas_call | solution.py:413
  2.1 4.1 %collective-permute-start.1 = (bf16[16,16,128]{2,1,0:T(8,128)(2,1)S(1)}, bf16[16,16,128]{2,1,0:T(8,128)(2,1)S(1)}, u32[]{:S(2)}, u32[]{:S(2)}) collective-permute-start(bf16[16,16,128]{2,1,0:T(8,128)(2,1)S(1)} %get-tuple-element.22), channel_id=1, source_target_pairs={{0,16},{1,0},{2,18},{3,2},{4,20},{5,4},{6,22},{7,6},{8,24},{9,8},{... | collective-permute-start | bytes 196616 | tf_op jit(solution)/shard_map/ppermute | solution.py:350
  6.2 0.7 %collective-permute-start.2 = (bf16[16,16,128]{2,1,0:T(8,128)(2,1)S(1)}, bf16[16,16,128]{2,1,0:T(8,128)(2,1)S(1)}, u32[]{:S(2)}, u32[]{:S(2)}) collective-permute-start(bf16[16,16,128]{2,1,0:T(8,128)(2,1)S(1)} %get-tuple-element.22), channel_id=1, source_target_pairs={{1,16},{3,18},{5,20},{7,22},{9,24},{11,26},{13,28},{15,30},{16,1},... | collective-permute-start | bytes 196616 | tf_op jit(solution)/shard_map/ppermute | solution.py:350
  6.9 1.2 %collective-permute-done.1 = bf16[16,16,128]{2,1,0:T(8,128)(2,1)S(1)} collective-permute-done((bf16[16,16,128]{2,1,0:T(8,128)(2,1)S(1)}, bf16[16,16,128]{2,1,0:T(8,128)(2,1)S(1)}, u32[]{:S(2)}, u32[]{:S(2)}) %collective-permute-start.1) | collective-permute-done | bytes 65568 | tf_op jit(solution)/shard_map/ppermute | solution.py:350
  8.1 0.0 collective-permute-done.2
  8.2 2.4 %collective-permute-start.3 = (bf16[2,16,16,128]{3,2,1,0:T(8,128)(2,1)S(1)}, bf16[2,16,16,128]{3,2,1,0:T(8,128)(2,1)S(1)}, u32[]{:S(2)}, u32[]{:S(2)}) collective-permute-start(bf16[2,16,16,128]{3,2,1,0:T(8,128)(2,1)S(1)} %maximum_select_fusion.refs_2_), channel_id=1, source_target_pairs={{0,8},{1,9},{2,10},{3,11},{4,12},{5,13},{6,14},{7,15},{8,0},{9,1},... | collective-permute-start | bytes 393224 | tf_op jit(solution)/shard_map/ppermute | solution.py:350
  10.6 1.5 %collective-permute-start.6 = (bf16[2,16,16,128]{3,2,1,0:T(8,128)(2,1)S(1)}, bf16[2,16,16,128]{3,2,1,0:T(8,128)(2,1)S(1)}, u32[]{:S(2)}, u32[]{:S(2)}) collective-permute-start(bf16[2,16,16,128]{3,2,1,0:T(8,128)(2,1)S(1)} %maximum_select_fusion.refs_2_), channel_id=1, source_target_pairs={{0,4},{1,5},{2,6},{3,7},{4,0},{5,1},{6,2},{7,3},{8,12},{9,13},{10,... | collective-permute-start | bytes 393224 | tf_op jit(solution)/shard_map/ppermute | solution.py:350
  12.0 2.4 %collective-permute-done.3.refs_4_ = bf16[2,16,16,128]{3,2,1,0:T(8,128)(2,1)S(1)} collective-permute-done((bf16[2,16,16,128]{3,2,1,0:T(8,128)(2,1)S(1)}, bf16[2,16,16,128]{3,2,1,0:T(8,128)(2,1)S(1)}, u32[]{:S(2)}, u32[]{:S(2)}) %collective-permute-start.3) | collective-permute-done | bytes 131104 | tf_op jit(solution)/shard_map/ppermute | solution.py:350
  14.5 1.5 %collective-permute-start.4 = (bf16[2,16,16,128]{3,2,1,0:T(8,128)(2,1)S(1)}, bf16[2,16,16,128]{3,2,1,0:T(8,128)(2,1)S(1)}, u32[]{:S(2)}, u32[]{:S(2)}) collective-permute-start(bf16[2,16,16,128]{3,2,1,0:T(8,128)(2,1)S(1)} %collective-permute-done.3.refs_4_), channel_id=1, source_target_pairs={{0,4},{1,5},{2,6},{3,7},{4,0},{5,1},{6,2},{7,3},{8,12},{9,13},{10,... | collective-permute-start | bytes 393224 | tf_op jit(solution)/shard_map/ppermute | solution.py:350
  16.0 0.0 collective-permute-start.8
  16.0 0.5 collective-permute-start.9
  16.5 0.0 collective-permute-done.6.refs_2_
  16.5 0.0 collective-permute-start.7
  16.5 3.0 %collective-permute-done.4.refs_2_ = bf16[2,16,16,128]{3,2,1,0:T(8,128)(2,1)S(1)} collective-permute-done((bf16[2,16,16,128]{3,2,1,0:T(8,128)(2,1)S(1)}, bf16[2,16,16,128]{3,2,1,0:T(8,128)(2,1)S(1)}, u32[]{:S(2)}, u32[]{:S(2)}) %collective-permute-start.4) | collective-permute-done | bytes 131104 | tf_op jit(solution)/shard_map/ppermute | solution.py:350
  19.4 0.0 collective-permute-start.5
  19.4 4.6 %collective-permute-start = (bf16[16,16,128]{2,1,0:T(8,128)(2,1)S(1)}, bf16[16,16,128]{2,1,0:T(8,128)(2,1)S(1)}, u32[]{:S(2)}, u32[]{:S(2)}) collective-permute-start(bf16[16,16,128]{2,1,0:T(8,128)(2,1)S(1)} %get-tuple-element.21.refs_0_), channel_id=1, source_target_pairs={{0,1},{1,0},{2,3},{3,2},{4,5},{5,4},{6,7},{7,6},{8,9},{9,8},{10,11... | collective-permute-start | bytes 196616 | tf_op jit(solution)/shard_map/ppermute | solution.py:350
  24.1 0.9 %shard_map.100.refs_4_ = f32[16,128,128]{2,1,0:T(8,128)S(1)} custom-call(bf16[16,128,128]{2,1,0:T(8,128)(2,1)S(1)} %copy-done, f32[3,128]{1,0:T(4,128)S(1)} %get-tuple-element.23.gains_ref.refs_5_.refs_3_, bf16[128,640]{1,0:T(8,128)(2,1)S(1)} %copy-done.2), custom_call_target="tpu_custom_call" | custom-call | tf_op jit(solution)/shard_map/pallas_call | solution.py:69
  25.0 1.8 %collective-permute-done.refs_1_ = bf16[16,16,128]{2,1,0:T(8,128)(2,1)S(1)} collective-permute-done((bf16[16,16,128]{2,1,0:T(8,128)(2,1)S(1)}, bf16[16,16,128]{2,1,0:T(8,128)(2,1)S(1)}, u32[]{:S(2)}, u32[]{:S(2)}) %collective-permute-start) | collective-permute-done | bytes 65568 | tf_op jit(solution)/shard_map/ppermute | solution.py:350
  26.8 0.0 collective-permute-done.9.refs_5_
  26.8 1.3 %shard_map.101.refs_4_ = f32[16,128,128]{2,1,0:T(8,128)S(1)} custom-call(bf16[16,16,128]{2,1,0:T(8,128)(2,1)S(1)} %get-tuple-element.21.refs_0_, bf16[16,16,128]{2,1,0:T(8,128)(2,1)S(1)} %collective-permute-done.refs_1_, bf16[2,16,16,128]{3,2,1,0:T(8,128)(2,1)S(1)} %maximum_select_fusion.refs_2_, ...), custom_call_target="tpu_custom_call" | custom-call | tf_op jit(solution)/shard_map/pallas_call | solution.py:69
  28.2 0.0 collective-permute-done.7.refs_3_
  28.2 0.7 %shard_map.102.refs_3_ = f32[16,128,128]{2,1,0:T(8,128)S(1)} custom-call(bf16[16,16,128]{2,1,0:T(8,128)(2,1)S(1)} %get-tuple-element.21.refs_0_, bf16[16,16,128]{2,1,0:T(8,128)(2,1)S(1)} %collective-permute-done.refs_1_, bf16[2,16,16,128]{3,2,1,0:T(8,128)(2,1)S(1)} %collective-permute-done.6.refs_2_, ...), custom_call_target="tpu_custom_call", output_to_operand_aliasing={{}: (4, {})} | custom-call | tf_op jit(solution)/shard_map/pallas_call | solution.py:69
  28.8 0.3 shard_map.103.refs_8_
  29.2 0.0 copy-start.5
  29.2 0.4 copy-done.4
  29.6 0.3 copy-done.5
  29.9 2.2 %shard_map.104 = (bf16[8,128,128]{2,1,0:T(8,128)(2,1)S(1)}, bf16[8,128,128]{2,1,0:T(8,128)(2,1)S(1)}, bf16[16,128,128]{2,1,0:T(8,128)(2,1)S(1)}, bf16[4,16,128]{2,1,0:T(8,128)(2,1)S(1)}, f32[16,128,128]{2,1,0:T(8,128)S(1)}) custom-call(bf16[16,16,128]{2,1,0:T(8,128)(2,1)S(1)} %get-tuple-element.21.refs_0_, ...), custom_call_target="tpu_custom_call", output_to_operand_aliasing={{4}: (8, {})} | custom-call | tf_op jit(solution)/shard_map/pallas_call | solution.py:69
  32.0 1.8 %collective-permute-start.20 = (bf16[8,128,128]{2,1,0:T(8,128)(2,1)S(1)}, bf16[8,128,128]{2,1,0:T(8,128)(2,1)S(1)}, u32[]{:S(2)}, u32[]{:S(2)}) collective-permute-start(bf16[8,128,128]{2,1,0:T(8,128)(2,1)S(1)} %get-tuple-element.34.refs_12_), channel_id=1, source_target_pairs={{0,1},{1,0},{2,3},{3,2},{4,5},{5,4},{6,7},{7,6},{8,9},{9,8},{10,11... | collective-permute-start | bytes 786440 | tf_op jit(solution)/shard_map/ppermute | solution.py:350
  33.8 0.3 collective-permute-start.19
  34.1 3.5 %collective-permute-start.10 = (bf16[4,16,128]{2,1,0:T(8,128)(2,1)S(1)}, bf16[4,16,128]{2,1,0:T(8,128)(2,1)S(1)}, u32[]{:S(2)}, u32[]{:S(2)}) collective-permute-start(bf16[4,16,128]{2,1,0:T(8,128)(2,1)S(1)} %get-tuple-element.24), channel_id=1, source_target_pairs={{0,16},{1,0},{2,18},{3,2},{4,20},{5,4},{6,22},{7,6},{8,24},{9,8},{... | collective-permute-start | bytes 49160 | tf_op jit(solution)/shard_map/ppermute | solution.py:350
  37.7 0.7 %collective-permute-start.11 = (bf16[4,16,128]{2,1,0:T(8,128)(2,1)S(1)}, bf16[4,16,128]{2,1,0:T(8,128)(2,1)S(1)}, u32[]{:S(2)}, u32[]{:S(2)}) collective-permute-start(bf16[4,16,128]{2,1,0:T(8,128)(2,1)S(1)} %get-tuple-element.24), channel_id=1, source_target_pairs={{1,16},{3,18},{5,20},{7,22},{9,24},{11,26},{13,28},{15,30},{16,1},... | collective-permute-start | bytes 49160 | tf_op jit(solution)/shard_map/ppermute | solution.py:350
  38.3 7.9 %collective-permute-done.10 = bf16[4,16,128]{2,1,0:T(8,128)(2,1)S(1)} collective-permute-done((bf16[4,16,128]{2,1,0:T(8,128)(2,1)S(1)}, bf16[4,16,128]{2,1,0:T(8,128)(2,1)S(1)}, u32[]{:S(2)}, u32[]{:S(2)}) %collective-permute-start.10) | collective-permute-done | bytes 16416 | tf_op jit(solution)/shard_map/ppermute | solution.py:350
  46.2 0.0 collective-permute-done.11
  46.2 1.2 %collective-permute-start.12 = (bf16[2,4,16,128]{3,2,1,0:T(8,128)(2,1)S(1)}, bf16[2,4,16,128]{3,2,1,0:T(8,128)(2,1)S(1)}, u32[]{:S(2)}, u32[]{:S(2)}) collective-permute-start(bf16[2,4,16,128]{3,2,1,0:T(8,128)(2,1)S(1)} %maximum_select_fusion.1.refs_0_), channel_id=1, source_target_pairs={{0,8},{1,9},{2,10},{3,11},{4,12},{5,13},{6,14},{7,15},{8,0},{9,1},... | collective-permute-start | bytes 98312 | tf_op jit(solution)/shard_map/ppermute | solution.py:350
  47.5 1.5 %collective-permute-start.13 = (bf16[2,4,16,128]{3,2,1,0:T(8,128)(2,1)S(1)}, bf16[2,4,16,128]{3,2,1,0:T(8,128)(2,1)S(1)}, u32[]{:S(2)}, u32[]{:S(2)}) collective-permute-start(bf16[2,4,16,128]{3,2,1,0:T(8,128)(2,1)S(1)} %maximum_select_fusion.1.refs_0_), channel_id=1, source_target_pairs={{0,4},{1,5},{2,6},{3,7},{4,0},{5,1},{6,2},{7,3},{8,12},{9,13},{10,... | collective-permute-start | bytes 98312 | tf_op jit(solution)/shard_map/ppermute | solution.py:350
  48.9 0.8 %collective-permute-start.14 = (bf16[2,4,16,128]{3,2,1,0:T(8,128)(2,1)S(1)}, bf16[2,4,16,128]{3,2,1,0:T(8,128)(2,1)S(1)}, u32[]{:S(2)}, u32[]{:S(2)}) collective-permute-start(bf16[2,4,16,128]{3,2,1,0:T(8,128)(2,1)S(1)} %maximum_select_fusion.1.refs_0_), channel_id=1, source_target_pairs={{0,12},{1,13},{2,14},{3,15},{4,8},{5,9},{6,10},{7,11},{8,4},{9,5},... | collective-permute-start | bytes 98312 | tf_op jit(solution)/shard_map/ppermute | solution.py:350
  49.8 0.6 %collective-permute-done.12.refs_1_ = bf16[2,4,16,128]{3,2,1,0:T(8,128)(2,1)S(1)} collective-permute-done((bf16[2,4,16,128]{3,2,1,0:T(8,128)(2,1)S(1)}, bf16[2,4,16,128]{3,2,1,0:T(8,128)(2,1)S(1)}, u32[]{:S(2)}, u32[]{:S(2)}) %collective-permute-start.12) | collective-permute-done | bytes 32800 | tf_op jit(solution)/shard_map/ppermute | solution.py:350
  50.4 1.3 %collective-permute-done.13.refs_2_ = bf16[2,4,16,128]{3,2,1,0:T(8,128)(2,1)S(1)} collective-permute-done((bf16[2,4,16,128]{3,2,1,0:T(8,128)(2,1)S(1)}, bf16[2,4,16,128]{3,2,1,0:T(8,128)(2,1)S(1)}, u32[]{:S(2)}, u32[]{:S(2)}) %collective-permute-start.13) | collective-permute-done | bytes 32800 | tf_op jit(solution)/shard_map/ppermute | solution.py:350
  51.7 2.1 %collective-permute-done.14.refs_3_ = bf16[2,4,16,128]{3,2,1,0:T(8,128)(2,1)S(1)} collective-permute-done((bf16[2,4,16,128]{3,2,1,0:T(8,128)(2,1)S(1)}, bf16[2,4,16,128]{3,2,1,0:T(8,128)(2,1)S(1)}, u32[]{:S(2)}, u32[]{:S(2)}) %collective-permute-start.14) | collective-permute-done | bytes 32800 | tf_op jit(solution)/shard_map/ppermute | solution.py:350
  53.8 0.5 collective-permute-start.18
  54.3 0.7 %shard_map.105 = (bf16[16,128,128]{2,1,0:T(8,128)(2,1)S(1)}, bf16[16,128,128]{2,1,0:T(8,128)(2,1)S(1)}, bf16[16,128,128]{2,1,0:T(8,128)(2,1)S(1)}, f32[16,128,128]{2,1,0:T(8,128)S(1)}) custom-call(bf16[16,128,128]{2,1,0:T(8,128)(2,1)S(1)} %get-tuple-element.25.norm_ref, bf16[128,512]{1,0:T(8,128)(2,1)S(1)} %copy-done.1), custom_call_target="tpu_custom_call" | custom-call | tf_op jit(solution)/shard_map/pallas_call | solution.py:69
  55.0 0.6 shard_map.107
  55.6 0.0 copy-start.3
  55.6 0.0 collective-permute-done.19.refs_0_
  55.6 0.6 shard_map.106
  56.2 0.1 copy-done.3
  56.3 1.7 %shard_map.108.refs_15_ = bf16[8,128,128]{2,1,0:T(8,128)(2,1)S(1)} custom-call(bf16[2,4,16,128]{3,2,1,0:T(8,128)(2,1)S(1)} %maximum_select_fusion.1.refs_0_, bf16[2,4,16,128]{3,2,1,0:T(8,128)(2,1)S(1)} %collective-permute-done.12.refs_1_, bf16[2,4,16,128]{3,2,1,0:T(8,128)(2,1)S(1)} %collective-permute-done.13.refs_2_, ...), custom_call_target="tpu_custom_call" | custom-call | tf_op jit(solution)/shard_map/pallas_call | solution.py:69
  58.0 2.5 %shard_map.109 = bf16[16,128,128]{2,1,0:T(8,128)(2,1)} custom-call(bf16[2,4,16,128]{3,2,1,0:T(8,128)(2,1)S(1)} %maximum_select_fusion.1.refs_0_, bf16[2,4,16,128]{3,2,1,0:T(8,128)(2,1)S(1)} %collective-permute-done.12.refs_1_, bf16[2,4,16,128]{3,2,1,0:T(8,128)(2,1)S(1)} %collective-permute-done.13.refs_2_, ...), custom_call_target="tpu_custom_call" | custom-call | tf_op jit(solution)/shard_map/pallas_call | solution.py:69
  (19 shorter events, 0.1 us)
Async XLA Ops:
  0.0 24.1 %copy-start = (bf16[16,128,128]{2,1,0:T(8,128)(2,1)S(1)}, bf16[16,128,128]{2,1,0:T(8,128)(2,1)}, u32[]{:S(2)}) copy-start(bf16[16,128,128]{2,1,0:T(8,128)(2,1)} %refs_3_.1) | copy-start | bytes 1572868
  2.1 6.0 %collective-permute-start.1 = (bf16[16,16,128]{2,1,0:T(8,128)(2,1)S(1)}, bf16[16,16,128]{2,1,0:T(8,128)(2,1)S(1)}, u32[]{:S(2)}, u32[]{:S(2)}) collective-permute-start(bf16[16,16,128]{2,1,0:T(8,128)(2,1)S(1)} %get-tuple-element.22), channel_id=1, source_target_pairs={{0,16},{1,0},{2,18},{3,2},{4,20},{5,4},{6,22},{7,6},{8,24},{9,8},{... | collective-permute-start | bytes 196616 | tf_op jit(solution)/shard_map/ppermute | solution.py:350
  6.2 1.9 %collective-permute-start.2 = (bf16[16,16,128]{2,1,0:T(8,128)(2,1)S(1)}, bf16[16,16,128]{2,1,0:T(8,128)(2,1)S(1)}, u32[]{:S(2)}, u32[]{:S(2)}) collective-permute-start(bf16[16,16,128]{2,1,0:T(8,128)(2,1)S(1)} %get-tuple-element.22), channel_id=1, source_target_pairs={{1,16},{3,18},{5,20},{7,22},{9,24},{11,26},{13,28},{15,30},{16,1},... | collective-permute-start | bytes 196616 | tf_op jit(solution)/shard_map/ppermute | solution.py:350
  8.1 15.9 %copy-start.2 = (bf16[128,640]{1,0:T(8,128)(2,1)S(1)}, bf16[128,640]{1,0:T(8,128)(2,1)}, u32[]{:S(2)}) copy-start(bf16[128,640]{1,0:T(8,128)(2,1)} %w_ref.4) | copy-start | bytes 491524
  8.2 6.3 %collective-permute-start.3 = (bf16[2,16,16,128]{3,2,1,0:T(8,128)(2,1)S(1)}, bf16[2,16,16,128]{3,2,1,0:T(8,128)(2,1)S(1)}, u32[]{:S(2)}, u32[]{:S(2)}) collective-permute-start(bf16[2,16,16,128]{3,2,1,0:T(8,128)(2,1)S(1)} %maximum_select_fusion.refs_2_), channel_id=1, source_target_pairs={{0,8},{1,9},{2,10},{3,11},{4,12},{5,13},{6,14},{7,15},{8,0},{9,1},... | collective-permute-start | bytes 393224 | tf_op jit(solution)/shard_map/ppermute | solution.py:350
  10.6 5.9 %collective-permute-start.6 = (bf16[2,16,16,128]{3,2,1,0:T(8,128)(2,1)S(1)}, bf16[2,16,16,128]{3,2,1,0:T(8,128)(2,1)S(1)}, u32[]{:S(2)}, u32[]{:S(2)}) collective-permute-start(bf16[2,16,16,128]{3,2,1,0:T(8,128)(2,1)S(1)} %maximum_select_fusion.refs_2_), channel_id=1, source_target_pairs={{0,4},{1,5},{2,6},{3,7},{4,0},{5,1},{6,2},{7,3},{8,12},{9,13},{10,... | collective-permute-start | bytes 393224 | tf_op jit(solution)/shard_map/ppermute | solution.py:350
  14.5 5.0 %collective-permute-start.4 = (bf16[2,16,16,128]{3,2,1,0:T(8,128)(2,1)S(1)}, bf16[2,16,16,128]{3,2,1,0:T(8,128)(2,1)S(1)}, u32[]{:S(2)}, u32[]{:S(2)}) collective-permute-start(bf16[2,16,16,128]{3,2,1,0:T(8,128)(2,1)S(1)} %collective-permute-done.3.refs_4_), channel_id=1, source_target_pairs={{0,4},{1,5},{2,6},{3,7},{4,0},{5,1},{6,2},{7,3},{8,12},{9,13},{10,... | collective-permute-start | bytes 393224 | tf_op jit(solution)/shard_map/ppermute | solution.py:350
  16.0 10.9 %collective-permute-start.8 = (bf16[2,16,16,128]{3,2,1,0:T(8,128)(2,1)S(1)}, bf16[2,16,16,128]{3,2,1,0:T(8,128)(2,1)S(1)}, u32[]{:S(2)}, u32[]{:S(2)}) collective-permute-start(bf16[2,16,16,128]{3,2,1,0:T(8,128)(2,1)S(1)} %maximum_select_fusion.refs_2_), channel_id=1, source_target_pairs={{0,2},{1,3},{2,0},{3,1},{4,6},{5,7},{6,4},{7,5},{8,10},{9,11},{10,... | collective-permute-start | bytes 393224 | tf_op jit(solution)/shard_map/ppermute | solution.py:350
  16.0 10.9 %collective-permute-start.9 = (bf16[2,16,16,128]{3,2,1,0:T(8,128)(2,1)S(1)}, bf16[2,16,16,128]{3,2,1,0:T(8,128)(2,1)S(1)}, u32[]{:S(2)}, u32[]{:S(2)}) collective-permute-start(bf16[2,16,16,128]{3,2,1,0:T(8,128)(2,1)S(1)} %collective-permute-done.3.refs_4_), channel_id=1, source_target_pairs={{0,2},{1,3},{2,0},{3,1},{4,6},{5,7},{6,4},{7,5},{8,10},{9,11},{10,... | collective-permute-start | bytes 393224 | tf_op jit(solution)/shard_map/ppermute | solution.py:350
  16.5 11.7 %collective-permute-start.7 = (bf16[2,16,16,128]{3,2,1,0:T(8,128)(2,1)S(1)}, bf16[2,16,16,128]{3,2,1,0:T(8,128)(2,1)S(1)}, u32[]{:S(2)}, u32[]{:S(2)}) collective-permute-start(bf16[2,16,16,128]{3,2,1,0:T(8,128)(2,1)S(1)} %collective-permute-done.6.refs_2_), channel_id=1, source_target_pairs={{0,2},{1,3},{2,0},{3,1},{4,6},{5,7},{6,4},{7,5},{8,10},{9,11},{10,... | collective-permute-start | bytes 393224 | tf_op jit(solution)/shard_map/ppermute | solution.py:350
  19.4 9.8 %collective-permute-start.5 = (bf16[2,16,16,128]{3,2,1,0:T(8,128)(2,1)S(1)}, bf16[2,16,16,128]{3,2,1,0:T(8,128)(2,1)S(1)}, u32[]{:S(2)}, u32[]{:S(2)}) collective-permute-start(bf16[2,16,16,128]{3,2,1,0:T(8,128)(2,1)S(1)} %collective-permute-done.4.refs_2_), channel_id=1, source_target_pairs={{0,2},{1,3},{2,0},{3,1},{4,6},{5,7},{6,4},{7,5},{8,10},{9,11},{10,... | collective-permute-start | bytes 393224 | tf_op jit(solution)/shard_map/ppermute | solution.py:350
  19.4 7.4 %collective-permute-start = (bf16[16,16,128]{2,1,0:T(8,128)(2,1)S(1)}, bf16[16,16,128]{2,1,0:T(8,128)(2,1)S(1)}, u32[]{:S(2)}, u32[]{:S(2)}) collective-permute-start(bf16[16,16,128]{2,1,0:T(8,128)(2,1)S(1)} %get-tuple-element.21.refs_0_), channel_id=1, source_target_pairs={{0,1},{1,0},{2,3},{3,2},{4,5},{5,4},{6,7},{7,6},{8,9},{9,8},{10,11... | collective-permute-start | bytes 196616 | tf_op jit(solution)/shard_map/ppermute | solution.py:350
  28.8 0.8 %copy-start.4 = (bf16[128,128]{1,0:T(8,128)(2,1)S(1)}, bf16[128,128]{1,0:T(8,128)(2,1)}, u32[]{:S(2)}) copy-start(bf16[128,128]{1,0:T(8,128)(2,1)} %refs_6_.1) | copy-start | bytes 98308
  29.2 0.7 %copy-start.5 = (bf16[128,4]{0,1:T(4,128)(2,1)S(1)}, bf16[128,4]{0,1:T(4,128)(2,1)}, u32[]{:S(2)}) copy-start(bf16[128,4]{0,1:T(4,128)(2,1)} %param.18) | copy-start | bytes 3076
  29.9 24.4 %copy-start.1 = (bf16[128,512]{1,0:T(8,128)(2,1)S(1)}, bf16[128,512]{1,0:T(8,128)(2,1)}, u32[]{:S(2)}) copy-start(bf16[128,512]{1,0:T(8,128)(2,1)} %refs_4_.3) | copy-start | bytes 393220
  32.0 21.7 %collective-permute-start.20 = (bf16[8,128,128]{2,1,0:T(8,128)(2,1)S(1)}, bf16[8,128,128]{2,1,0:T(8,128)(2,1)S(1)}, u32[]{:S(2)}, u32[]{:S(2)}) collective-permute-start(bf16[8,128,128]{2,1,0:T(8,128)(2,1)S(1)} %get-tuple-element.34.refs_12_), channel_id=1, source_target_pairs={{0,1},{1,0},{2,3},{3,2},{4,5},{5,4},{6,7},{7,6},{8,9},{9,8},{10,11... | collective-permute-start | bytes 786440 | tf_op jit(solution)/shard_map/ppermute | solution.py:350
  33.8 21.7 %collective-permute-start.19 = (bf16[8,128,128]{2,1,0:T(8,128)(2,1)S(1)}, bf16[8,128,128]{2,1,0:T(8,128)(2,1)S(1)}, u32[]{:S(2)}, u32[]{:S(2)}) collective-permute-start(bf16[8,128,128]{2,1,0:T(8,128)(2,1)S(1)} %get-tuple-element.27.refs_12_), channel_id=1, source_target_pairs={{0,1},{1,0},{2,3},{3,2},{4,5},{5,4},{6,7},{7,6},{8,9},{9,8},{10,11... | collective-permute-start | bytes 786440 | tf_op jit(solution)/shard_map/ppermute | solution.py:350
  34.1 12.1 %collective-permute-start.10 = (bf16[4,16,128]{2,1,0:T(8,128)(2,1)S(1)}, bf16[4,16,128]{2,1,0:T(8,128)(2,1)S(1)}, u32[]{:S(2)}, u32[]{:S(2)}) collective-permute-start(bf16[4,16,128]{2,1,0:T(8,128)(2,1)S(1)} %get-tuple-element.24), channel_id=1, source_target_pairs={{0,16},{1,0},{2,18},{3,2},{4,20},{5,4},{6,22},{7,6},{8,24},{9,8},{... | collective-permute-start | bytes 49160 | tf_op jit(solution)/shard_map/ppermute | solution.py:350
  37.7 8.5 %collective-permute-start.11 = (bf16[4,16,128]{2,1,0:T(8,128)(2,1)S(1)}, bf16[4,16,128]{2,1,0:T(8,128)(2,1)S(1)}, u32[]{:S(2)}, u32[]{:S(2)}) collective-permute-start(bf16[4,16,128]{2,1,0:T(8,128)(2,1)S(1)} %get-tuple-element.24), channel_id=1, source_target_pairs={{1,16},{3,18},{5,20},{7,22},{9,24},{11,26},{13,28},{15,30},{16,1},... | collective-permute-start | bytes 49160 | tf_op jit(solution)/shard_map/ppermute | solution.py:350
  46.2 4.2 %collective-permute-start.12 = (bf16[2,4,16,128]{3,2,1,0:T(8,128)(2,1)S(1)}, bf16[2,4,16,128]{3,2,1,0:T(8,128)(2,1)S(1)}, u32[]{:S(2)}, u32[]{:S(2)}) collective-permute-start(bf16[2,4,16,128]{3,2,1,0:T(8,128)(2,1)S(1)} %maximum_select_fusion.1.refs_0_), channel_id=1, source_target_pairs={{0,8},{1,9},{2,10},{3,11},{4,12},{5,13},{6,14},{7,15},{8,0},{9,1},... | collective-permute-start | bytes 98312 | tf_op jit(solution)/shard_map/ppermute | solution.py:350
  47.5 4.2 %collective-permute-start.13 = (bf16[2,4,16,128]{3,2,1,0:T(8,128)(2,1)S(1)}, bf16[2,4,16,128]{3,2,1,0:T(8,128)(2,1)S(1)}, u32[]{:S(2)}, u32[]{:S(2)}) collective-permute-start(bf16[2,4,16,128]{3,2,1,0:T(8,128)(2,1)S(1)} %maximum_select_fusion.1.refs_0_), channel_id=1, source_target_pairs={{0,4},{1,5},{2,6},{3,7},{4,0},{5,1},{6,2},{7,3},{8,12},{9,13},{10,... | collective-permute-start | bytes 98312 | tf_op jit(solution)/shard_map/ppermute | solution.py:350
  48.9 4.8 %collective-permute-start.14 = (bf16[2,4,16,128]{3,2,1,0:T(8,128)(2,1)S(1)}, bf16[2,4,16,128]{3,2,1,0:T(8,128)(2,1)S(1)}, u32[]{:S(2)}, u32[]{:S(2)}) collective-permute-start(bf16[2,4,16,128]{3,2,1,0:T(8,128)(2,1)S(1)} %maximum_select_fusion.1.refs_0_), channel_id=1, source_target_pairs={{0,12},{1,13},{2,14},{3,15},{4,8},{5,9},{6,10},{7,11},{8,4},{9,5},... | collective-permute-start | bytes 98312 | tf_op jit(solution)/shard_map/ppermute | solution.py:350
  50.4 5.8 %collective-permute-start.15 = (bf16[2,4,16,128]{3,2,1,0:T(8,128)(2,1)S(1)}, bf16[2,4,16,128]{3,2,1,0:T(8,128)(2,1)S(1)}, u32[]{:S(2)}, u32[]{:S(2)}) collective-permute-start(bf16[2,4,16,128]{3,2,1,0:T(8,128)(2,1)S(1)} %maximum_select_fusion.1.refs_0_), channel_id=1, source_target_pairs={{0,2},{1,3},{2,0},{3,1},{4,6},{5,7},{6,4},{7,5},{8,10},{9,11},{10,... | collective-permute-start | bytes 98312 | tf_op jit(solution)/shard_map/ppermute | solution.py:350
  51.7 4.5 %collective-permute-start.16 = (bf16[2,4,16,128]{3,2,1,0:T(8,128)(2,1)S(1)}, bf16[2,4,16,128]{3,2,1,0:T(8,128)(2,1)S(1)}, u32[]{:S(2)}, u32[]{:S(2)}) collective-permute-start(bf16[2,4,16,128]{3,2,1,0:T(8,128)(2,1)S(1)} %collective-permute-done.12.refs_1_), channel_id=1, source_target_pairs={{0,2},{1,3},{2,0},{3,1},{4,6},{5,7},{6,4},{7,5},{8,10},{9,11},{10,... | collective-permute-start | bytes 98312 | tf_op jit(solution)/shard_map/ppermute | solution.py:350
  53.8 2.4 %collective-permute-start.17 = (bf16[2,4,16,128]{3,2,1,0:T(8,128)(2,1)S(1)}, bf16[2,4,16,128]{3,2,1,0:T(8,128)(2,1)S(1)}, u32[]{:S(2)}, u32[]{:S(2)}) collective-permute-start(bf16[2,4,16,128]{3,2,1,0:T(8,128)(2,1)S(1)} %collective-permute-done.13.refs_2_), channel_id=1, source_target_pairs={{0,2},{1,3},{2,0},{3,1},{4,6},{5,7},{6,4},{7,5},{8,10},{9,11},{10,... | collective-permute-start | bytes 98312 | tf_op jit(solution)/shard_map/ppermute | solution.py:350
  53.8 2.4 %collective-permute-start.18 = (bf16[2,4,16,128]{3,2,1,0:T(8,128)(2,1)S(1)}, bf16[2,4,16,128]{3,2,1,0:T(8,128)(2,1)S(1)}, u32[]{:S(2)}, u32[]{:S(2)}) collective-permute-start(bf16[2,4,16,128]{3,2,1,0:T(8,128)(2,1)S(1)} %collective-permute-done.14.refs_3_), channel_id=1, source_target_pairs={{0,2},{1,3},{2,0},{3,1},{4,6},{5,7},{6,4},{7,5},{8,10},{9,11},{10,... | collective-permute-start | bytes 98312 | tf_op jit(solution)/shard_map/ppermute | solution.py:350
  55.6 0.8 %copy-start.3 = (bf16[128,128]{1,0:T(8,128)(2,1)S(1)}, bf16[128,128]{1,0:T(8,128)(2,1)}, u32[]{:S(2)}) copy-start(bf16[128,128]{1,0:T(8,128)(2,1)} %refs_14_.3) | copy-start | bytes 98308

commit v8 on v7

--- a/solution.py
+++ b/solution.py
@@ -45,10 +45,11 @@
     return lax.dot_general(a, b, (((1,), (1,)), ((), ())), preferred_element_type=F32)
 
 
-def call(kernel, out_shape, n_smem, n_in, limit, scratch=(), held_out=True, aliases=None):
+def call(kernel, out_shape, n_smem, n_in, limit, scratch=(), held_out=True, aliases=None, streamed=False):
     smem = pl.BlockSpec(memory_space=pltpu.SMEM)
     vmem = pl.BlockSpec(memory_space=pltpu.VMEM)
-    outs = jax.tree.map(lambda _: vmem, out_shape)
+    place = pl.BlockSpec(memory_space=pl.ANY) if streamed else vmem
+    outs = jax.tree.map(lambda _: place, out_shape)
     resident = limit < RESIDENT_LIMIT
     if resident and held_out:
         out_shape = jax.tree.map(lambda o: pltpu.VMEM(o.shape, o.dtype), out_shape)
@@ -246,21 +247,28 @@
     return kernel
 
 
-def make_attend_kernel(n_col, n_blk, place, base, n_done):
+def make_attend_kernel(n_col, n_blk, place, base, n_done, stream):
     def kernel(*refs):
         biases = refs[:n_blk]
         q_ref, keys_ref, values_ref, gate_ref, mid_ref, live_ref, out_w_ref = refs[
             n_blk : n_blk + 7
         ]
         done = refs[n_blk + 7 : n_blk + 7 + n_done]
-        whole_ref, bias_ref = refs[n_blk + 7 + n_done :]
         rows, cols, width = mid_ref.shape
-        first_row = base if n_done else 0
-        out_ref = whole_ref.at[first_row : first_row + rows]
+        if stream:
+            bias_ref, whole_ref, out_ref, sems = refs[n_blk + 7 + n_done :]
+        else:
+            out_ref, bias_ref = refs[n_blk + 7 + n_done :]
+        copies = []
         for at, done_ref in enumerate(done):
-            whole_ref[at * rows : (at + 1) * rows] = done_ref[...]
-        blk = biases[0].shape[2]
-        for d in range(n_col):
+            copies.append(
+                pltpu.make_async_copy(
+                    done_ref, whole_ref.at[at * rows : (at + 1) * rows], sems.at[at]
+                )
+            )
+            copies[-1].start()
+        for d in range(n_col if n_blk else 0):
+            blk = biases[0].shape[2]
             live = jnp.broadcast_to(live_ref[:, d * cols : (d + 1) * cols], (blk, cols)) > 0.5
             for s in range(n_blk):
                 first = place(s) * blk
@@ -299,14 +307,33 @@
 
         lax.fori_loop(0, rows, attend, 0, unroll=max(1, min(rows, 2**18 // (cols * n_col * cols))))
 
-        def finish(t, carry):
+        def finish(t):
             at = pl.ds(t * step, step)
             attended = out_ref[at].reshape(step * cols, width)
             new = mid_ref[at].reshape(step * cols, width).astype(F32) + dot(attended, out_w_ref[...])
             out_ref[at] = new.astype(BF16).reshape(step, cols, width)
-            return carry
-
-        lax.fori_loop(0, rows // step, finish, 0, unroll=unroll_of(rows // step, cols))
+
+        if not stream:
+            lax.fori_loop(
+                0,
+                rows // step,
+                lambda t, carry: (finish(t), carry)[1],
+                0,
+                unroll=unroll_of(rows // step, cols),
+            )
+            return
+        for t in range(rows // step):
+            finish(t)
+            copies.append(
+                pltpu.make_async_copy(
+                    out_ref.at[t * step : (t + 1) * step],
+                    whole_ref.at[base + t * step : base + (t + 1) * step],
+                    sems.at[n_done + t],
+                )
+            )
+            copies[-1].start()
+        for copy in copies:
+            copy.wait()
 
     return kernel
 
@@ -398,7 +425,7 @@
         pair_rep, chain_len, tri_gain, tri_in, sum_gain, tri_out, att_gain, att_in, att_bias, att_out
     ):
         rows, cols, width = pair_rep.shape
-        n_col, n_blk = grid.n_col, grid.n_blk
+        n_col = grid.n_col
         whole = (rows, cols, width)
         parts = 2 if grid.fast else 1
         limit = min(60 * MIB, 12 * MIB + 24 * H * cols * n_col * cols * 4)
@@ -486,25 +513,32 @@
             keys, values = call(
                 make_spread_kernel(n_col, base), (all_keys, all_keys), 0, n_col + 3, limit
             )(*others[part], key, value, gains, att_in)
+            stream = part > 0
+            blocks = [] if stream else biases
+            part_shape = jax.ShapeDtypeStruct((share, cols, width), BF16)
+            bias_shape = jax.ShapeDtypeStruct((H * cols, n_col * cols), F32)
+            operands = [*blocks, query, keys, values, att_gate, mids[part], live, att_out]
+            if stream:
+                operands += [*done, bias_all]
             result = call(
-                make_attend_kernel(n_col, n_blk, grid.place, base, len(done) * final),
-                wide if final else jax.ShapeDtypeStruct((share, cols, width), BF16),
+                make_attend_kernel(
+                    n_col, len(blocks), grid.place, base, len(done), stream
+                ),
+                wide if stream else (part_shape, bias_shape),
                 0,
-                n_blk + 7 + len(done) * final,
+                len(operands),
                 limit,
-                [pltpu.VMEM((H * cols, n_col * cols), F32)],
+                [
+                    pltpu.VMEM((share, cols, width), BF16),
+                    pltpu.SemaphoreType.DMA((len(done) + share // 2,)),
+                ]
+                if stream
+                else [],
                 held_out=not final,
-            )(
-                *biases,
-                query,
-                keys,
-                values,
-                att_gate,
-                mids[part],
-                live,
-                att_out,
-                *(done if final else []),
-            )
+                streamed=stream,
+            )(*operands)
+            if not stream:
+                result, bias_all = result
             done.append(result)
         return result
 

time: 60.8 us -> 60.7 us (level)
  no operation moved by 1% of the time
where the time goes in v8:
time: 60.7 us; the launch traced here: 60.4 us
  starting transfers between devices  25.6 us (42%)
  waiting for transfers between devices  20.3 us (33%)
  Pallas kernels  13.5 us (22%)
  local copies, waits for them, and re-layouts  0.81 us (1%)
    ppermute x21, starting transfers between devices, move(): return lax.ppermute(value, ('row', 'col'), pairs)  25.6 us
    ppermute x21, waiting for transfers between devices, move(): return lax.ppermute(value, ('row', 'col'), pairs)  20.3 us
    pallas_call x10, Pallas kernels, apply(): return run(*args[:n_smem], *held)  11.4 us
    pallas_call x1, Pallas kernels, body(): pl.pallas_call(make_edge_kernel(cols, n_col, grid.col_of), name='edges',...  2.11 us
  transfers between devices with their start and end apart: 21, of which 8 were waited for; matrix products, arithmetic and copies ran while one was open for 0% of the time, Pallas kernels for 8%

profile of v8, /device:TPU:0, one launch (start us, length us, event | category | flops | bytes accessed | tf_op | source)
XLA Modules:
  0.0 60.4 jit_solution(1559883479471646218)
XLA Ops:
  0.0 2.1 %edges.1 = (bf16[16,16,128]{2,1,0:T(8,128)(2,1)S(1)}, bf16[16,16,128]{2,1,0:T(8,128)(2,1)S(1)}, f32[3,128]{1,0:T(4,128)S(1)}, f32[1,256]{1,0:T(1,128)S(1)}) custom-call(s32[4]{0:T(128)} %len_ref.1, bf16[16,128,128]{2,1,0:T(8,128)(2,1)} %refs_3_.1, f32[1,128]{1,0:T(1,128)} %bitcast.17, f32[1,128]{1,0:T(1,128)} %bitcast.18, f32[1,128]{1,0:T(1,128)} %bitcast.19, ...), custom_call_target="tpu_custom_call" | custom-call | tf_op jit(solution)/shard_map/edges/pallas_call | solution.py:440
  2.1 4.1 %collective-permute-start.1 = (bf16[16,16,128]{2,1,0:T(8,128)(2,1)S(1)}, bf16[16,16,128]{2,1,0:T(8,128)(2,1)S(1)}, u32[]{:S(2)}, u32[]{:S(2)}) collective-permute-start(bf16[16,16,128]{2,1,0:T(8,128)(2,1)S(1)} %get-tuple-element.24), channel_id=1, source_target_pairs={{0,16},{1,0},{2,18},{3,2},{4,20},{5,4},{6,22},{7,6},{8,24},{9,8},{... | collective-permute-start | bytes 196616 | tf_op jit(solution)/shard_map/ppermute | solution.py:377
  6.2 0.7 %collective-permute-start.2 = (bf16[16,16,128]{2,1,0:T(8,128)(2,1)S(1)}, bf16[16,16,128]{2,1,0:T(8,128)(2,1)S(1)}, u32[]{:S(2)}, u32[]{:S(2)}) collective-permute-start(bf16[16,16,128]{2,1,0:T(8,128)(2,1)S(1)} %get-tuple-element.24), channel_id=1, source_target_pairs={{1,16},{3,18},{5,20},{7,22},{9,24},{11,26},{13,28},{15,30},{16,1},... | collective-permute-start | bytes 196616 | tf_op jit(solution)/shard_map/ppermute | solution.py:377
  6.9 1.2 %collective-permute-done.1 = bf16[16,16,128]{2,1,0:T(8,128)(2,1)S(1)} collective-permute-done((bf16[16,16,128]{2,1,0:T(8,128)(2,1)S(1)}, bf16[16,16,128]{2,1,0:T(8,128)(2,1)S(1)}, u32[]{:S(2)}, u32[]{:S(2)}) %collective-permute-start.1) | collective-permute-done | bytes 65568 | tf_op jit(solution)/shard_map/ppermute | solution.py:377
  8.1 0.0 collective-permute-done.2
  8.2 2.4 %collective-permute-start.3 = (bf16[2,16,16,128]{3,2,1,0:T(8,128)(2,1)S(1)}, bf16[2,16,16,128]{3,2,1,0:T(8,128)(2,1)S(1)}, u32[]{:S(2)}, u32[]{:S(2)}) collective-permute-start(bf16[2,16,16,128]{3,2,1,0:T(8,128)(2,1)S(1)} %maximum_select_fusion.refs_2_), channel_id=1, source_target_pairs={{0,8},{1,9},{2,10},{3,11},{4,12},{5,13},{6,14},{7,15},{8,0},{9,1},... | collective-permute-start | bytes 393224 | tf_op jit(solution)/shard_map/ppermute | solution.py:377
  10.6 1.5 %collective-permute-start.6 = (bf16[2,16,16,128]{3,2,1,0:T(8,128)(2,1)S(1)}, bf16[2,16,16,128]{3,2,1,0:T(8,128)(2,1)S(1)}, u32[]{:S(2)}, u32[]{:S(2)}) collective-permute-start(bf16[2,16,16,128]{3,2,1,0:T(8,128)(2,1)S(1)} %maximum_select_fusion.refs_2_), channel_id=1, source_target_pairs={{0,4},{1,5},{2,6},{3,7},{4,0},{5,1},{6,2},{7,3},{8,12},{9,13},{10,... | collective-permute-start | bytes 393224 | tf_op jit(solution)/shard_map/ppermute | solution.py:377
  12.0 2.4 %collective-permute-done.3.refs_4_ = bf16[2,16,16,128]{3,2,1,0:T(8,128)(2,1)S(1)} collective-permute-done((bf16[2,16,16,128]{3,2,1,0:T(8,128)(2,1)S(1)}, bf16[2,16,16,128]{3,2,1,0:T(8,128)(2,1)S(1)}, u32[]{:S(2)}, u32[]{:S(2)}) %collective-permute-start.3) | collective-permute-done | bytes 131104 | tf_op jit(solution)/shard_map/ppermute | solution.py:377
  14.5 1.5 %collective-permute-start.4 = (bf16[2,16,16,128]{3,2,1,0:T(8,128)(2,1)S(1)}, bf16[2,16,16,128]{3,2,1,0:T(8,128)(2,1)S(1)}, u32[]{:S(2)}, u32[]{:S(2)}) collective-permute-start(bf16[2,16,16,128]{3,2,1,0:T(8,128)(2,1)S(1)} %collective-permute-done.3.refs_4_), channel_id=1, source_target_pairs={{0,4},{1,5},{2,6},{3,7},{4,0},{5,1},{6,2},{7,3},{8,12},{9,13},{10,... | collective-permute-start | bytes 393224 | tf_op jit(solution)/shard_map/ppermute | solution.py:377
  16.0 0.0 collective-permute-start.8
  16.0 0.5 collective-permute-start.9
  16.5 0.0 collective-permute-done.6.refs_2_
  16.5 0.0 collective-permute-start.7
  16.5 3.0 %collective-permute-done.4.refs_2_ = bf16[2,16,16,128]{3,2,1,0:T(8,128)(2,1)S(1)} collective-permute-done((bf16[2,16,16,128]{3,2,1,0:T(8,128)(2,1)S(1)}, bf16[2,16,16,128]{3,2,1,0:T(8,128)(2,1)S(1)}, u32[]{:S(2)}, u32[]{:S(2)}) %collective-permute-start.4) | collective-permute-done | bytes 131104 | tf_op jit(solution)/shard_map/ppermute | solution.py:377
  19.4 0.0 collective-permute-start.5
  19.4 4.6 %collective-permute-start = (bf16[16,16,128]{2,1,0:T(8,128)(2,1)S(1)}, bf16[16,16,128]{2,1,0:T(8,128)(2,1)S(1)}, u32[]{:S(2)}, u32[]{:S(2)}) collective-permute-start(bf16[16,16,128]{2,1,0:T(8,128)(2,1)S(1)} %get-tuple-element.23.refs_0_), channel_id=1, source_target_pairs={{0,1},{1,0},{2,3},{3,2},{4,5},{5,4},{6,7},{7,6},{8,9},{9,8},{10,11... | collective-permute-start | bytes 196616 | tf_op jit(solution)/shard_map/ppermute | solution.py:377
  24.1 0.9 %shard_map.100.refs_4_ = f32[16,128,128]{2,1,0:T(8,128)S(1)} custom-call(bf16[16,128,128]{2,1,0:T(8,128)(2,1)S(1)} %copy-done, f32[3,128]{1,0:T(4,128)S(1)} %get-tuple-element.25.gains_ref.refs_5_.refs_3_, bf16[128,640]{1,0:T(8,128)(2,1)S(1)} %copy-done.2), custom_call_target="tpu_custom_call" | custom-call | tf_op jit(solution)/shard_map/pallas_call | solution.py:70
  25.0 1.8 %collective-permute-done.refs_1_ = bf16[16,16,128]{2,1,0:T(8,128)(2,1)S(1)} collective-permute-done((bf16[16,16,128]{2,1,0:T(8,128)(2,1)S(1)}, bf16[16,16,128]{2,1,0:T(8,128)(2,1)S(1)}, u32[]{:S(2)}, u32[]{:S(2)}) %collective-permute-start) | collective-permute-done | bytes 65568 | tf_op jit(solution)/shard_map/ppermute | solution.py:377
  26.8 0.0 collective-permute-done.9.refs_5_
  26.8 1.3 %shard_map.101.refs_4_ = f32[16,128,128]{2,1,0:T(8,128)S(1)} custom-call(bf16[16,16,128]{2,1,0:T(8,128)(2,1)S(1)} %get-tuple-element.23.refs_0_, bf16[16,16,128]{2,1,0:T(8,128)(2,1)S(1)} %collective-permute-done.refs_1_, bf16[2,16,16,128]{3,2,1,0:T(8,128)(2,1)S(1)} %maximum_select_fusion.refs_2_, ...), custom_call_target="tpu_custom_call" | custom-call | tf_op jit(solution)/shard_map/pallas_call | solution.py:70
  28.2 0.0 collective-permute-done.7.refs_3_
  28.2 0.7 %shard_map.102.refs_3_ = f32[16,128,128]{2,1,0:T(8,128)S(1)} custom-call(bf16[16,16,128]{2,1,0:T(8,128)(2,1)S(1)} %get-tuple-element.23.refs_0_, bf16[16,16,128]{2,1,0:T(8,128)(2,1)S(1)} %collective-permute-done.refs_1_, bf16[2,16,16,128]{3,2,1,0:T(8,128)(2,1)S(1)} %collective-permute-done.6.refs_2_, ...), custom_call_target="tpu_custom_call", output_to_operand_aliasing={{}: (4, {})} | custom-call | tf_op jit(solution)/shard_map/pallas_call | solution.py:70
  28.8 0.3 shard_map.103.refs_8_
  29.2 0.0 copy-start.5
  29.2 0.4 copy-done.4
  29.6 0.3 copy-done.5
  29.9 2.2 %shard_map.104 = (bf16[8,128,128]{2,1,0:T(8,128)(2,1)S(1)}, bf16[8,128,128]{2,1,0:T(8,128)(2,1)S(1)}, bf16[16,128,128]{2,1,0:T(8,128)(2,1)S(1)}, bf16[4,16,128]{2,1,0:T(8,128)(2,1)S(1)}, f32[16,128,128]{2,1,0:T(8,128)S(1)}) custom-call(bf16[16,16,128]{2,1,0:T(8,128)(2,1)S(1)} %get-tuple-element.23.refs_0_, ...), custom_call_target="tpu_custom_call", output_to_operand_aliasing={{4}: (8, {})} | custom-call | tf_op jit(solution)/shard_map/pallas_call | solution.py:70
  32.0 1.8 %collective-permute-start.20 = (bf16[8,128,128]{2,1,0:T(8,128)(2,1)S(1)}, bf16[8,128,128]{2,1,0:T(8,128)(2,1)S(1)}, u32[]{:S(2)}, u32[]{:S(2)}) collective-permute-start(bf16[8,128,128]{2,1,0:T(8,128)(2,1)S(1)} %get-tuple-element.36.refs_12_), channel_id=1, source_target_pairs={{0,1},{1,0},{2,3},{3,2},{4,5},{5,4},{6,7},{7,6},{8,9},{9,8},{10,11... | collective-permute-start | bytes 786440 | tf_op jit(solution)/shard_map/ppermute | solution.py:377
  33.8 0.3 collective-permute-start.10
  34.1 3.5 %collective-permute-start.11 = (bf16[4,16,128]{2,1,0:T(8,128)(2,1)S(1)}, bf16[4,16,128]{2,1,0:T(8,128)(2,1)S(1)}, u32[]{:S(2)}, u32[]{:S(2)}) collective-permute-start(bf16[4,16,128]{2,1,0:T(8,128)(2,1)S(1)} %get-tuple-element.35), channel_id=1, source_target_pairs={{0,16},{1,0},{2,18},{3,2},{4,20},{5,4},{6,22},{7,6},{8,24},{9,8},{... | collective-permute-start | bytes 49160 | tf_op jit(solution)/shard_map/ppermute | solution.py:377
  37.7 0.7 %collective-permute-start.12 = (bf16[4,16,128]{2,1,0:T(8,128)(2,1)S(1)}, bf16[4,16,128]{2,1,0:T(8,128)(2,1)S(1)}, u32[]{:S(2)}, u32[]{:S(2)}) collective-permute-start(bf16[4,16,128]{2,1,0:T(8,128)(2,1)S(1)} %get-tuple-element.35), channel_id=1, source_target_pairs={{1,16},{3,18},{5,20},{7,22},{9,24},{11,26},{13,28},{15,30},{16,1},... | collective-permute-start | bytes 49160 | tf_op jit(solution)/shard_map/ppermute | solution.py:377
  38.3 7.9 %collective-permute-done.11 = bf16[4,16,128]{2,1,0:T(8,128)(2,1)S(1)} collective-permute-done((bf16[4,16,128]{2,1,0:T(8,128)(2,1)S(1)}, bf16[4,16,128]{2,1,0:T(8,128)(2,1)S(1)}, u32[]{:S(2)}, u32[]{:S(2)}) %collective-permute-start.11) | collective-permute-done | bytes 16416 | tf_op jit(solution)/shard_map/ppermute | solution.py:377
  46.2 0.0 collective-permute-done.12
  46.2 1.2 %collective-permute-start.13 = (bf16[2,4,16,128]{3,2,1,0:T(8,128)(2,1)S(1)}, bf16[2,4,16,128]{3,2,1,0:T(8,128)(2,1)S(1)}, u32[]{:S(2)}, u32[]{:S(2)}) collective-permute-start(bf16[2,4,16,128]{3,2,1,0:T(8,128)(2,1)S(1)} %maximum_select_fusion.1.refs_0_), channel_id=1, source_target_pairs={{0,8},{1,9},{2,10},{3,11},{4,12},{5,13},{6,14},{7,15},{8,0},{9,1},... | collective-permute-start | bytes 98312 | tf_op jit(solution)/shard_map/ppermute | solution.py:377
  47.5 1.5 %collective-permute-start.14 = (bf16[2,4,16,128]{3,2,1,0:T(8,128)(2,1)S(1)}, bf16[2,4,16,128]{3,2,1,0:T(8,128)(2,1)S(1)}, u32[]{:S(2)}, u32[]{:S(2)}) collective-permute-start(bf16[2,4,16,128]{3,2,1,0:T(8,128)(2,1)S(1)} %maximum_select_fusion.1.refs_0_), channel_id=1, source_target_pairs={{0,4},{1,5},{2,6},{3,7},{4,0},{5,1},{6,2},{7,3},{8,12},{9,13},{10,... | collective-permute-start | bytes 98312 | tf_op jit(solution)/shard_map/ppermute | solution.py:377
  48.9 0.8 %collective-permute-start.15 = (bf16[2,4,16,128]{3,2,1,0:T(8,128)(2,1)S(1)}, bf16[2,4,16,128]{3,2,1,0:T(8,128)(2,1)S(1)}, u32[]{:S(2)}, u32[]{:S(2)}) collective-permute-start(bf16[2,4,16,128]{3,2,1,0:T(8,128)(2,1)S(1)} %maximum_select_fusion.1.refs_0_), channel_id=1, source_target_pairs={{0,12},{1,13},{2,14},{3,15},{4,8},{5,9},{6,10},{7,11},{8,4},{9,5},... | collective-permute-start | bytes 98312 | tf_op jit(solution)/shard_map/ppermute | solution.py:377
  49.8 0.6 %collective-permute-done.13.refs_1_ = bf16[2,4,16,128]{3,2,1,0:T(8,128)(2,1)S(1)} collective-permute-done((bf16[2,4,16,128]{3,2,1,0:T(8,128)(2,1)S(1)}, bf16[2,4,16,128]{3,2,1,0:T(8,128)(2,1)S(1)}, u32[]{:S(2)}, u32[]{:S(2)}) %collective-permute-start.13) | collective-permute-done | bytes 32800 | tf_op jit(solution)/shard_map/ppermute | solution.py:377
  50.4 1.3 %collective-permute-done.14.refs_2_ = bf16[2,4,16,128]{3,2,1,0:T(8,128)(2,1)S(1)} collective-permute-done((bf16[2,4,16,128]{3,2,1,0:T(8,128)(2,1)S(1)}, bf16[2,4,16,128]{3,2,1,0:T(8,128)(2,1)S(1)}, u32[]{:S(2)}, u32[]{:S(2)}) %collective-permute-start.14) | collective-permute-done | bytes 32800 | tf_op jit(solution)/shard_map/ppermute | solution.py:377
  51.7 0.0 collective-permute-start.17
  51.7 2.1 %collective-permute-done.15.refs_3_ = bf16[2,4,16,128]{3,2,1,0:T(8,128)(2,1)S(1)} collective-permute-done((bf16[2,4,16,128]{3,2,1,0:T(8,128)(2,1)S(1)}, bf16[2,4,16,128]{3,2,1,0:T(8,128)(2,1)S(1)}, u32[]{:S(2)}, u32[]{:S(2)}) %collective-permute-start.15) | collective-permute-done | bytes 32800 | tf_op jit(solution)/shard_map/ppermute | solution.py:377
  53.8 0.5 collective-permute-start.19
  54.3 0.7 %shard_map.105 = (bf16[16,128,128]{2,1,0:T(8,128)(2,1)S(1)}, bf16[16,128,128]{2,1,0:T(8,128)(2,1)S(1)}, bf16[16,128,128]{2,1,0:T(8,128)(2,1)S(1)}, f32[16,128,128]{2,1,0:T(8,128)S(1)}) custom-call(bf16[16,128,128]{2,1,0:T(8,128)(2,1)S(1)} %get-tuple-element.26.norm_ref, bf16[128,512]{1,0:T(8,128)(2,1)S(1)} %copy-done.1), custom_call_target="tpu_custom_call" | custom-call | tf_op jit(solution)/shard_map/pallas_call | solution.py:70
  55.0 0.6 shard_map.107
  55.6 0.0 copy-start.3
  55.6 0.6 shard_map.106
  56.2 0.1 copy-done.3
  56.3 1.7 %shard_map.108 = (bf16[8,128,128]{2,1,0:T(8,128)(2,1)S(1)}, f32[512,256]{1,0:T(8,128)S(1)}) custom-call(bf16[2,4,16,128]{3,2,1,0:T(8,128)(2,1)S(1)} %maximum_select_fusion.1.refs_0_, bf16[2,4,16,128]{3,2,1,0:T(8,128)(2,1)S(1)} %collective-permute-done.13.refs_1_, bf16[2,4,16,128]{3,2,1,0:T(8,128)(2,1)S(1)} %collective-permute-done.14.refs_2_, ...), custom_call_target="tpu_custom_call" | custom-call | tf_op jit(solution)/shard_map/pallas_call | solution.py:70
  58.1 2.4 %shard_map.109 = bf16[16,128,128]{2,1,0:T(8,128)(2,1)} custom-call(bf16[16,128,128]{2,1,0:T(8,128)(2,1)S(1)} %get-tuple-element.27.refs_8_.refs_0_, bf16[8,256,128]{2,1,0:T(8,128)(2,1)S(1)} %get-tuple-element.31.refs_1_, bf16[8,256,128]{2,1,0:T(8,128)(2,1)S(1)} %get-tuple-element.32.refs_2_, f32[16,128,128]{2,1,0:T(8,128)S(1)} %get-tuple-element.33.refs_11_.refs_3_, ...), custom_call_target="tpu_custom_call" | custom-call | tf_op jit(solution)/shard_map/pallas_call | solution.py:70
  (19 shorter events, 0.1 us)
Async XLA Ops:
  0.0 24.1 %copy-start = (bf16[16,128,128]{2,1,0:T(8,128)(2,1)S(1)}, bf16[16,128,128]{2,1,0:T(8,128)(2,1)}, u32[]{:S(2)}) copy-start(bf16[16,128,128]{2,1,0:T(8,128)(2,1)} %refs_3_.1) | copy-start | bytes 1572868
  2.1 6.0 %collective-permute-start.1 = (bf16[16,16,128]{2,1,0:T(8,128)(2,1)S(1)}, bf16[16,16,128]{2,1,0:T(8,128)(2,1)S(1)}, u32[]{:S(2)}, u32[]{:S(2)}) collective-permute-start(bf16[16,16,128]{2,1,0:T(8,128)(2,1)S(1)} %get-tuple-element.24), channel_id=1, source_target_pairs={{0,16},{1,0},{2,18},{3,2},{4,20},{5,4},{6,22},{7,6},{8,24},{9,8},{... | collective-permute-start | bytes 196616 | tf_op jit(solution)/shard_map/ppermute | solution.py:377
  6.2 1.9 %collective-permute-start.2 = (bf16[16,16,128]{2,1,0:T(8,128)(2,1)S(1)}, bf16[16,16,128]{2,1,0:T(8,128)(2,1)S(1)}, u32[]{:S(2)}, u32[]{:S(2)}) collective-permute-start(bf16[16,16,128]{2,1,0:T(8,128)(2,1)S(1)} %get-tuple-element.24), channel_id=1, source_target_pairs={{1,16},{3,18},{5,20},{7,22},{9,24},{11,26},{13,28},{15,30},{16,1},... | collective-permute-start | bytes 196616 | tf_op jit(solution)/shard_map/ppermute | solution.py:377
  8.1 15.9 %copy-start.2 = (bf16[128,640]{1,0:T(8,128)(2,1)S(1)}, bf16[128,640]{1,0:T(8,128)(2,1)}, u32[]{:S(2)}) copy-start(bf16[128,640]{1,0:T(8,128)(2,1)} %w_ref.4) | copy-start | bytes 491524
  8.2 6.3 %collective-permute-start.3 = (bf16[2,16,16,128]{3,2,1,0:T(8,128)(2,1)S(1)}, bf16[2,16,16,128]{3,2,1,0:T(8,128)(2,1)S(1)}, u32[]{:S(2)}, u32[]{:S(2)}) collective-permute-start(bf16[2,16,16,128]{3,2,1,0:T(8,128)(2,1)S(1)} %maximum_select_fusion.refs_2_), channel_id=1, source_target_pairs={{0,8},{1,9},{2,10},{3,11},{4,12},{5,13},{6,14},{7,15},{8,0},{9,1},... | collective-permute-start | bytes 393224 | tf_op jit(solution)/shard_map/ppermute | solution.py:377
  10.6 5.9 %collective-permute-start.6 = (bf16[2,16,16,128]{3,2,1,0:T(8,128)(2,1)S(1)}, bf16[2,16,16,128]{3,2,1,0:T(8,128)(2,1)S(1)}, u32[]{:S(2)}, u32[]{:S(2)}) collective-permute-start(bf16[2,16,16,128]{3,2,1,0:T(8,128)(2,1)S(1)} %maximum_select_fusion.refs_2_), channel_id=1, source_target_pairs={{0,4},{1,5},{2,6},{3,7},{4,0},{5,1},{6,2},{7,3},{8,12},{9,13},{10,... | collective-permute-start | bytes 393224 | tf_op jit(solution)/shard_map/ppermute | solution.py:377
  14.5 5.0 %collective-permute-start.4 = (bf16[2,16,16,128]{3,2,1,0:T(8,128)(2,1)S(1)}, bf16[2,16,16,128]{3,2,1,0:T(8,128)(2,1)S(1)}, u32[]{:S(2)}, u32[]{:S(2)}) collective-permute-start(bf16[2,16,16,128]{3,2,1,0:T(8,128)(2,1)S(1)} %collective-permute-done.3.refs_4_), channel_id=1, source_target_pairs={{0,4},{1,5},{2,6},{3,7},{4,0},{5,1},{6,2},{7,3},{8,12},{9,13},{10,... | collective-permute-start | bytes 393224 | tf_op jit(solution)/shard_map/ppermute | solution.py:377
  16.0 10.9 %collective-permute-start.8 = (bf16[2,16,16,128]{3,2,1,0:T(8,128)(2,1)S(1)}, bf16[2,16,16,128]{3,2,1,0:T(8,128)(2,1)S(1)}, u32[]{:S(2)}, u32[]{:S(2)}) collective-permute-start(bf16[2,16,16,128]{3,2,1,0:T(8,128)(2,1)S(1)} %maximum_select_fusion.refs_2_), channel_id=1, source_target_pairs={{0,2},{1,3},{2,0},{3,1},{4,6},{5,7},{6,4},{7,5},{8,10},{9,11},{10,... | collective-permute-start | bytes 393224 | tf_op jit(solution)/shard_map/ppermute | solution.py:377
  16.0 10.9 %collective-permute-start.9 = (bf16[2,16,16,128]{3,2,1,0:T(8,128)(2,1)S(1)}, bf16[2,16,16,128]{3,2,1,0:T(8,128)(2,1)S(1)}, u32[]{:S(2)}, u32[]{:S(2)}) collective-permute-start(bf16[2,16,16,128]{3,2,1,0:T(8,128)(2,1)S(1)} %collective-permute-done.3.refs_4_), channel_id=1, source_target_pairs={{0,2},{1,3},{2,0},{3,1},{4,6},{5,7},{6,4},{7,5},{8,10},{9,11},{10,... | collective-permute-start | bytes 393224 | tf_op jit(solution)/shard_map/ppermute | solution.py:377
  16.5 11.7 %collective-permute-start.7 = (bf16[2,16,16,128]{3,2,1,0:T(8,128)(2,1)S(1)}, bf16[2,16,16,128]{3,2,1,0:T(8,128)(2,1)S(1)}, u32[]{:S(2)}, u32[]{:S(2)}) collective-permute-start(bf16[2,16,16,128]{3,2,1,0:T(8,128)(2,1)S(1)} %collective-permute-done.6.refs_2_), channel_id=1, source_target_pairs={{0,2},{1,3},{2,0},{3,1},{4,6},{5,7},{6,4},{7,5},{8,10},{9,11},{10,... | collective-permute-start | bytes 393224 | tf_op jit(solution)/shard_map/ppermute | solution.py:377
  19.4 9.8 %collective-permute-start.5 = (bf16[2,16,16,128]{3,2,1,0:T(8,128)(2,1)S(1)}, bf16[2,16,16,128]{3,2,1,0:T(8,128)(2,1)S(1)}, u32[]{:S(2)}, u32[]{:S(2)}) collective-permute-start(bf16[2,16,16,128]{3,2,1,0:T(8,128)(2,1)S(1)} %collective-permute-done.4.refs_2_), channel_id=1, source_target_pairs={{0,2},{1,3},{2,0},{3,1},{4,6},{5,7},{6,4},{7,5},{8,10},{9,11},{10,... | collective-permute-start | bytes 393224 | tf_op jit(solution)/shard_map/ppermute | solution.py:377
  19.4 7.4 %collective-permute-start = (bf16[16,16,128]{2,1,0:T(8,128)(2,1)S(1)}, bf16[16,16,128]{2,1,0:T(8,128)(2,1)S(1)}, u32[]{:S(2)}, u32[]{:S(2)}) collective-permute-start(bf16[16,16,128]{2,1,0:T(8,128)(2,1)S(1)} %get-tuple-element.23.refs_0_), channel_id=1, source_target_pairs={{0,1},{1,0},{2,3},{3,2},{4,5},{5,4},{6,7},{7,6},{8,9},{9,8},{10,11... | collective-permute-start | bytes 196616 | tf_op jit(solution)/shard_map/ppermute | solution.py:377
  28.8 0.8 %copy-start.4 = (bf16[128,128]{1,0:T(8,128)(2,1)S(1)}, bf16[128,128]{1,0:T(8,128)(2,1)}, u32[]{:S(2)}) copy-start(bf16[128,128]{1,0:T(8,128)(2,1)} %refs_6_.2) | copy-start | bytes 98308
  29.2 0.7 %copy-start.5 = (bf16[128,4]{0,1:T(4,128)(2,1)S(1)}, bf16[128,4]{0,1:T(4,128)(2,1)}, u32[]{:S(2)}) copy-start(bf16[128,4]{0,1:T(4,128)(2,1)} %param.18) | copy-start | bytes 3076
  29.9 24.4 %copy-start.1 = (bf16[128,512]{1,0:T(8,128)(2,1)S(1)}, bf16[128,512]{1,0:T(8,128)(2,1)}, u32[]{:S(2)}) copy-start(bf16[128,512]{1,0:T(8,128)(2,1)} %refs_4_.3) | copy-start | bytes 393220
  32.0 21.7 %collective-permute-start.20 = (bf16[8,128,128]{2,1,0:T(8,128)(2,1)S(1)}, bf16[8,128,128]{2,1,0:T(8,128)(2,1)S(1)}, u32[]{:S(2)}, u32[]{:S(2)}) collective-permute-start(bf16[8,128,128]{2,1,0:T(8,128)(2,1)S(1)} %get-tuple-element.36.refs_12_), channel_id=1, source_target_pairs={{0,1},{1,0},{2,3},{3,2},{4,5},{5,4},{6,7},{7,6},{8,9},{9,8},{10,11... | collective-permute-start | bytes 786440 | tf_op jit(solution)/shard_map/ppermute | solution.py:377
  33.8 21.7 %collective-permute-start.10 = (bf16[8,128,128]{2,1,0:T(8,128)(2,1)S(1)}, bf16[8,128,128]{2,1,0:T(8,128)(2,1)S(1)}, u32[]{:S(2)}, u32[]{:S(2)}) collective-permute-start(bf16[8,128,128]{2,1,0:T(8,128)(2,1)S(1)} %get-tuple-element.28.refs_4_), channel_id=1, source_target_pairs={{0,1},{1,0},{2,3},{3,2},{4,5},{5,4},{6,7},{7,6},{8,9},{9,8},{10,11... | collective-permute-start | bytes 786440 | tf_op jit(solution)/shard_map/ppermute | solution.py:377
  34.1 12.1 %collective-permute-start.11 = (bf16[4,16,128]{2,1,0:T(8,128)(2,1)S(1)}, bf16[4,16,128]{2,1,0:T(8,128)(2,1)S(1)}, u32[]{:S(2)}, u32[]{:S(2)}) collective-permute-start(bf16[4,16,128]{2,1,0:T(8,128)(2,1)S(1)} %get-tuple-element.35), channel_id=1, source_target_pairs={{0,16},{1,0},{2,18},{3,2},{4,20},{5,4},{6,22},{7,6},{8,24},{9,8},{... | collective-permute-start | bytes 49160 | tf_op jit(solution)/shard_map/ppermute | solution.py:377
  37.7 8.5 %collective-permute-start.12 = (bf16[4,16,128]{2,1,0:T(8,128)(2,1)S(1)}, bf16[4,16,128]{2,1,0:T(8,128)(2,1)S(1)}, u32[]{:S(2)}, u32[]{:S(2)}) collective-permute-start(bf16[4,16,128]{2,1,0:T(8,128)(2,1)S(1)} %get-tuple-element.35), channel_id=1, source_target_pairs={{1,16},{3,18},{5,20},{7,22},{9,24},{11,26},{13,28},{15,30},{16,1},... | collective-permute-start | bytes 49160 | tf_op jit(solution)/shard_map/ppermute | solution.py:377
  46.2 4.2 %collective-permute-start.13 = (bf16[2,4,16,128]{3,2,1,0:T(8,128)(2,1)S(1)}, bf16[2,4,16,128]{3,2,1,0:T(8,128)(2,1)S(1)}, u32[]{:S(2)}, u32[]{:S(2)}) collective-permute-start(bf16[2,4,16,128]{3,2,1,0:T(8,128)(2,1)S(1)} %maximum_select_fusion.1.refs_0_), channel_id=1, source_target_pairs={{0,8},{1,9},{2,10},{3,11},{4,12},{5,13},{6,14},{7,15},{8,0},{9,1},... | collective-permute-start | bytes 98312 | tf_op jit(solution)/shard_map/ppermute | solution.py:377
  47.5 4.2 %collective-permute-start.14 = (bf16[2,4,16,128]{3,2,1,0:T(8,128)(2,1)S(1)}, bf16[2,4,16,128]{3,2,1,0:T(8,128)(2,1)S(1)}, u32[]{:S(2)}, u32[]{:S(2)}) collective-permute-start(bf16[2,4,16,128]{3,2,1,0:T(8,128)(2,1)S(1)} %maximum_select_fusion.1.refs_0_), channel_id=1, source_target_pairs={{0,4},{1,5},{2,6},{3,7},{4,0},{5,1},{6,2},{7,3},{8,12},{9,13},{10,... | collective-permute-start | bytes 98312 | tf_op jit(solution)/shard_map/ppermute | solution.py:377
  48.9 4.8 %collective-permute-start.15 = (bf16[2,4,16,128]{3,2,1,0:T(8,128)(2,1)S(1)}, bf16[2,4,16,128]{3,2,1,0:T(8,128)(2,1)S(1)}, u32[]{:S(2)}, u32[]{:S(2)}) collective-permute-start(bf16[2,4,16,128]{3,2,1,0:T(8,128)(2,1)S(1)} %maximum_select_fusion.1.refs_0_), channel_id=1, source_target_pairs={{0,12},{1,13},{2,14},{3,15},{4,8},{5,9},{6,10},{7,11},{8,4},{9,5},... | collective-permute-start | bytes 98312 | tf_op jit(solution)/shard_map/ppermute | solution.py:377
  50.4 5.8 %collective-permute-start.16 = (bf16[2,4,16,128]{3,2,1,0:T(8,128)(2,1)S(1)}, bf16[2,4,16,128]{3,2,1,0:T(8,128)(2,1)S(1)}, u32[]{:S(2)}, u32[]{:S(2)}) collective-permute-start(bf16[2,4,16,128]{3,2,1,0:T(8,128)(2,1)S(1)} %maximum_select_fusion.1.refs_0_), channel_id=1, source_target_pairs={{0,2},{1,3},{2,0},{3,1},{4,6},{5,7},{6,4},{7,5},{8,10},{9,11},{10,... | collective-permute-start | bytes 98312 | tf_op jit(solution)/shard_map/ppermute | solution.py:377
  51.7 4.5 %collective-permute-start.17 = (bf16[2,4,16,128]{3,2,1,0:T(8,128)(2,1)S(1)}, bf16[2,4,16,128]{3,2,1,0:T(8,128)(2,1)S(1)}, u32[]{:S(2)}, u32[]{:S(2)}) collective-permute-start(bf16[2,4,16,128]{3,2,1,0:T(8,128)(2,1)S(1)} %collective-permute-done.13.refs_1_), channel_id=1, source_target_pairs={{0,2},{1,3},{2,0},{3,1},{4,6},{5,7},{6,4},{7,5},{8,10},{9,11},{10,... | collective-permute-start | bytes 98312 | tf_op jit(solution)/shard_map/ppermute | solution.py:377
  53.8 2.4 %collective-permute-start.18 = (bf16[2,4,16,128]{3,2,1,0:T(8,128)(2,1)S(1)}, bf16[2,4,16,128]{3,2,1,0:T(8,128)(2,1)S(1)}, u32[]{:S(2)}, u32[]{:S(2)}) collective-permute-start(bf16[2,4,16,128]{3,2,1,0:T(8,128)(2,1)S(1)} %collective-permute-done.14.refs_2_), channel_id=1, source_target_pairs={{0,2},{1,3},{2,0},{3,1},{4,6},{5,7},{6,4},{7,5},{8,10},{9,11},{10,... | collective-permute-start | bytes 98312 | tf_op jit(solution)/shard_map/ppermute | solution.py:377
  53.8 2.4 %collective-permute-start.19 = (bf16[2,4,16,128]{3,2,1,0:T(8,128)(2,1)S(1)}, bf16[2,4,16,128]{3,2,1,0:T(8,128)(2,1)S(1)}, u32[]{:S(2)}, u32[]{:S(2)}) collective-permute-start(bf16[2,4,16,128]{3,2,1,0:T(8,128)(2,1)S(1)} %collective-permute-done.15.refs_3_), channel_id=1, source_target_pairs={{0,2},{1,3},{2,0},{3,1},{4,6},{5,7},{6,4},{7,5},{8,10},{9,11},{10,... | collective-permute-start | bytes 98312 | tf_op jit(solution)/shard_map/ppermute | solution.py:377
  55.6 0.8 %copy-start.3 = (bf16[128,128]{1,0:T(8,128)(2,1)S(1)}, bf16[128,128]{1,0:T(8,128)(2,1)}, u32[]{:S(2)}) copy-start(bf16[128,128]{1,0:T(8,128)(2,1)} %refs_6_.3) | copy-start | bytes 98308
